TPU v7x, 128 devices: a whole 4x4x4 slice. The times are simulated.
128 devices in a mesh: row: 16 (over z, x_hi, core), col: 8 (over x_lo, y).
Axes of the slice: x: 4 (x_hi: 2, x_lo: 2; x = x_hi * 2 + x_lo), y: 4, z: 4, core: 2. Of those that a mesh axis runs over, the one named last changes fastest.
Arguments:
- stored: bfloat16 [1024, 51200], P(('row', 'col')), may hold values from -24 to 24
- integrals: bfloat16 [51200, 25600], P('row', 'col'), may hold values from -0.02734375 to 0.02734375
- layout: int32 [1024], replicated, may hold values from 0 to 1023, each once
- partner: int32 [1024], replicated, may hold values from 0 to 1023, as said below
Outputs:
- residual_out: bfloat16 [1024, 25600], P('row', 'col')
Inputs may be any that keep to these rules, and one draw needn't show every extreme that they name: partner is an involution without fixed points: partner[p] != p and partner[partner[p]] = p. `layout`: each slab pair stands in exactly one stored row.
All inputs are finite; a program needn't handle non-finite values.
Results may differ from a plain program's by a relative error of at most 0.001.
Values may be sent and summed in bfloat16 or wider, within the bound.
A program may use at most 128 MiB of HBM per device.

v0:
```python
import jax
import jax.numpy as jnp
from jax import lax
from jax.sharding import PartitionSpec as P


def per_device(stored, integrals, layout, partner):
    local_rows = stored.shape[0]
    n_row = lax.axis_size("row")
    n_col = lax.axis_size("col")
    total = local_rows * n_row * n_col
    regrouped = lax.all_to_all(stored, "row", split_axis=1, concat_axis=0, tiled=True)
    partial_sums = jnp.dot(
        lax.all_gather(regrouped, "col", axis=0, tiled=True),
        integrals,
        preferred_element_type=jnp.float32,
    )
    place = jnp.arange(total, dtype=jnp.int32)
    group_size = n_row * local_rows
    source_col = place // group_size
    remain = place % group_size
    source_row = remain // local_rows
    offset = remain % local_rows
    stored_index = (source_row * n_col + source_col) * local_rows + offset
    where_global = jnp.zeros((total,), jnp.int32).at[layout[stored_index]].set(place)
    difference = partial_sums[where_global] - partial_sums[where_global[partner]]
    return lax.psum_scatter(difference, "row", scatter_dimension=0, tiled=True).astype(jnp.bfloat16)


def solution(mesh):
    return jax.shard_map(
        per_device,
        mesh=mesh,
        in_specs=(P(("row", "col"), None), P("row", "col"), P(), P()),
        out_specs=P("row", "col"),
        check_vma=False,
    )
```

profile of v0, /device:TPU:0, one launch (start us, length us, event | category | flops | bytes accessed | tf_op | source)
XLA Modules:
  0.0 313.6 jit_solution(5771795690259070240)
XLA Ops:
  6.5 0.0 copy-start
  6.5 0.0 all-gather.2.cloned.1.call-start
  6.5 23.7 %all_to_all.19 = bf16[8,16,3200]{2,0,1:T(8,128)(2,1)} all-to-all(bf16[8,16,3200]{2,0,1:T(8,128)(2,1)} %bitcast.13), channel_id=1, replica_groups=mesh['row'=16,'col'=8] {'row'}, dimensions={1} | all-to-all | bytes 1638400 | tf_op jit(solution)/shard_map/all_to_all | solution.py:12
  30.3 0.0 all-gather.2.cloned.1.call-update
  30.3 0.0 reduce-scatter.2.cloned.1.call-start
  30.4 0.0 copy-done
  30.4 4.5 %gather_fusion = s32[1024]{0:T(1024)S(1)} fusion(s32[1024]{0:T(1024)S(1)} %copy-done, s32[1024]{0:T(1024)S(1)} %broadcast_clamp_fusion.1), kind=kCustom, calls=%fused_computation | custom fusion | bytes 12288 | tf_op jit(solution)/shard_map/gather | solution.py:25
  35.0 4.3 %scatter_custom_fusion = s32[1024]{0:T(1024)S(1)} fusion(s32[1024]{0:T(1024)S(1)} %bitcast.18, s32[1024]{0:T(1024)S(1)} %iota.7, s32[]{:T(128)} %constant.45.clone.1), kind=kCustom, calls=%fused_computation.27 | custom fusion | bytes 4100 | tf_op jit(solution)/shard_map/scatter | solution.py:25
  39.3 0.7 fusion.4
  40.0 4.5 %gather_fusion.2 = s32[1024]{0:T(1024)S(1)} fusion(s32[1024]{0:T(1024)S(1)} %scatter_custom_fusion, s32[1024]{0:T(1024)S(1)} %fusion.4), kind=kCustom, calls=%fused_computation.2 | custom fusion | bytes 12288 | tf_op jit(solution)/shard_map/gather | solution.py:26
  44.5 57.4 %all-gather.2.cloned.1.call-done = bf16[1024,3200]{1,0:T(8,128)(2,1)} async-done(((bf16[128,3200]{1,0:T(8,128)(2,1)}), bf16[1024,3200]{1,0:T(8,128)(2,1)}) %all-gather.2.cloned.1.call-update) | async-done | bytes 6553616 | tf_op jit(solution)/shard_map/all_gather | solution.py:14
  102.0 30.6 %fusion.7 = f32[1024,3200]{1,0:T(8,128)} fusion(bf16[1024,3200]{1,0:T(8,128)(2,1)} %all-gather.2.cloned.1.call-done, bf16[3200,3200]{1,0:T(8,128)(2,1)} %param.5), kind=kOutput, calls=%fused_computation.29 | convolution fusion | flops 20971520000 | bytes 40140800 | tf_op jit(solution)/shard_map/dot_general | solution.py:13
  132.5 17.1 %gather_fusion.3 = f32[1024,3200]{1,0:T(8,128)} fusion(f32[1024,3200]{1,0:T(8,128)} %fusion.7, s32[1024]{0:T(1024)S(1)} %broadcast_clamp_fusion), kind=kCustom, calls=%fused_computation.3 | custom fusion | bytes 26218496 | tf_op jit(solution)/shard_map/gather | solution.py:26
  149.7 17.1 %gather_fusion.1 = f32[1024,3200]{1,0:T(8,128)} fusion(f32[1024,3200]{1,0:T(8,128)} %fusion.7, s32[1024]{0:T(1024)S(1)} %fusion.3), kind=kCustom, calls=%fused_computation.1 | custom fusion | bytes 26218496 | tf_op jit(solution)/shard_map/gather | solution.py:26
  166.7 0.0 copy-start.1
  166.7 14.4 %sub.15 = f32[1024,3200]{1,0:T(8,128)} subtract(f32[1024,3200]{1,0:T(8,128)} %gather_fusion.1, f32[1024,3200]{1,0:T(8,128)} %gather_fusion.3) | non-fusion elementwise | flops 3276800 | bytes 39321600 | tf_op jit(solution)/shard_map/sub | solution.py:26
  181.1 0.0 reduce-scatter.2.cloned.1.call-update
  181.1 123.7 %reduce-scatter.2.cloned.1.call-done = f32[64,3200]{1,0:T(8,128)} async-done(((f32[1024,3200]{1,0:T(8,128)}), f32[64,3200]{1,0:T(8,128)}) %reduce-scatter.2.cloned.1.call-update) | async-done | bytes 819216 | tf_op jit(solution)/shard_map/reduce_scatter | solution.py:27
  304.8 1.9 convert_element_type.3
  306.8 0.0 copy-done.1
  (7 shorter events, 0.1 us)
Async XLA Ops:
  6.5 23.9 %copy-start = (s32[1024]{0:T(1024)S(1)}, s32[1024]{0:T(1024)}, u32[]{:S(2)}) copy-start(s32[1024]{0:T(1024)} %param.6) | copy-start | bytes 12292
  6.5 95.4 %all-gather.2.cloned.1.call-start = ((), (), s32[]{:S(2)}) async-start(), calls=%async_computation.2 | async-start | bytes 7372800 | tf_op jit(solution)/shard_map/all_gather | solution.py:14
  30.3 274.5 %reduce-scatter.2.cloned.1.call-start = ((), (), s32[]{:S(2)}) async-start(), calls=%async_computation.3 | async-start | bytes 13926400 | tf_op jit(solution)/shard_map/reduce_scatter | solution.py:27
  166.7 140.1 %copy-start.1 = (s32[1024]{0:T(1024)S(1)}, s32[1024]{0:T(1024)}, u32[]{:S(2)}) copy-start(s32[1024]{0:T(1024)} %param.6) | copy-start | bytes 12292
Sparse Core Ops, SparseCore 0:
  30.4 71.5 all-gather.1
  181.2 123.5 reduce-scatter.1
where the time goes:
time: 314 us
  waiting for transfers between devices  181 us (58%)
  local copies, waits for them, and re-layouts  47.5 us (15%)
  matrix products  30.6 us (10%)
  blocking collectives  23.7 us (8%)
  other arithmetic  17.1 us (5%)
  between operations  13.5 us (4%)
    reduce_scatter x1, waiting for transfers between devices, per_device(): lax.psum_scatter(difference, 'row', scatter_dimension=0, tiled=True)  124 us
    all_gather x1, waiting for transfers between devices, per_device(): lax.all_gather(regrouped, 'col', axis=0, tiled=True)  57.4 us
    dot_general x1, matrix products, per_device(): jnp.dot(lax.all_gather(regrouped, 'col', axis=0, tiled=True), integrals,...  30.6 us
    all_to_all x1, blocking collectives, per_device(): lax.all_to_all(stored, 'row', split_axis=1, concat_axis=0, tiled=True)  23.7 us
    gather x1, local copies, waits for them, and re-layouts, per_device(): partial_sums[where_global[partner]]  17.1 us
    gather x1, local copies, waits for them, and re-layouts, per_device(): partial_sums[where_global] - partial_sums[where_global[partner]]  17.1 us
    sub x1, other arithmetic, per_device(): partial_sums[where_global] - partial_sums[where_global[partner]]  14.4 us
  transfers between devices with their start and end apart: 2, of which 2 were waited for; matrix products, arithmetic and copies ran while one was open for 5% of the time, Pallas kernels for 0%

commit v1 on v0

v1 whole, which is shorter than its diff:
```python
import jax
import jax.numpy as jnp
from jax import lax
from jax.sharding import Mesh, PartitionSpec as P

ROW_AXES = ("z", "xh", "core")
COL_AXES = ("xl", "y")
N_CHUNKS = 5


def per_device(stored, integrals, layout, partner):
    local_rows = stored.shape[0]
    n_z = lax.axis_size("z")
    n_xh = lax.axis_size("xh")
    n_core = lax.axis_size("core")
    n_row = n_z * n_xh * n_core
    n_col = lax.axis_size("xl") * lax.axis_size("y")
    total = local_rows * n_row * n_col
    block = total // n_row

    regrouped = lax.all_to_all(stored, ROW_AXES, split_axis=1, concat_axis=0, tiled=True)
    gathered = lax.all_gather(regrouped, COL_AXES, axis=0, tiled=True)

    s = jnp.arange(total, dtype=jnp.int32)
    s_row = s // (local_rows * n_col)
    s_col = (s // local_rows) % n_col
    s_off = s % local_rows
    pos_of_stored = s_col * (n_row * local_rows) + s_row * local_rows + s_off
    inv = jnp.zeros((total,), jnp.int32).at[layout].set(s)

    i = jnp.arange(total, dtype=jnp.int32)
    t = i % block
    g = i // block
    xh = g % n_xh
    z = (g // n_xh) % n_z
    core = g // (n_xh * n_z)
    p_of_i = ((z * n_xh + xh) * n_core + core) * block + t
    pt = partner[p_of_i]
    pt_t = pt % block
    pt_g = pt // block
    pt_core = pt_g % n_core
    pt_xh = (pt_g // n_core) % n_xh
    pt_z = pt_g // (n_core * n_xh)
    partner_i = ((pt_core * n_z + pt_z) * n_xh + pt_xh) * block + pt_t

    amps = gathered[pos_of_stored[inv[p_of_i]]]

    n_cols = integrals.shape[1]
    width = n_cols // N_CHUNKS
    outs = []
    for j in range(N_CHUNKS):
        cols = integrals[:, j * width:(j + 1) * width]
        ladder = jnp.dot(amps, cols, preferred_element_type=jnp.float32)
        difference = ladder - ladder[partner_i]
        part = lax.psum_scatter(difference, "core", scatter_dimension=0, tiled=True)
        part = lax.psum_scatter(part, ("z", "xh"), scatter_dimension=0, tiled=True)
        outs.append(part.astype(jnp.bfloat16))
    return jnp.concatenate(outs, axis=1)


def solution(mesh):
    n_row, n_col = mesh.devices.shape
    fine = Mesh(mesh.devices.reshape(4, n_row // 8, 2, 2, n_col // 2), ROW_AXES + COL_AXES)
    return jax.shard_map(
        per_device,
        mesh=fine,
        in_specs=(P(ROW_AXES + COL_AXES, None), P(ROW_AXES, COL_AXES), P(), P()),
        out_specs=P(ROW_AXES, COL_AXES),
        check_vma=False,
    )
```

time: 314 us -> 609 us (1.94)
  waiting for transfers between devices: 181 us -> 443 us
  matrix products: 30.6 us -> 43.7 us
  local copies, waits for them, and re-layouts: 47.5 us -> 60.1 us
  other arithmetic: 17.1 us -> 24.1 us
    reduce_scatter x1 -> x10, waiting for transfers between devices: 124 us -> 388 us  [the longest x5 379 us: per_device(): part = lax.psum_scatter(part, ('z', 'xh'), scatter_dimension=0, tiled=True)]
    dot_general x1 -> x5, matrix products: 30.6 us -> 43.7 us  [per_device(): ladder = jnp.dot(amps, cols, preferred_element_type=jnp.float32)]
    gather x4 -> x9, local copies, waits for them, and re-layouts: 43.2 us -> 55.8 us  [the longest x5 25.9 us: per_device(): difference = ladder - ladder[partner_i]]
    sub x1 -> x5, other arithmetic: 14.4 us -> 18 us  [per_device(): difference = ladder - ladder[partner_i]]
  transfers between devices with their start and end apart: 2 -> 11, of which waited for: 2 -> 7; matrix products, arithmetic and copies ran while one was open for 5% -> 15% of each run, Pallas kernels for 0% -> 0%
where the time goes in v1:
time: 609 us
  waiting for transfers between devices  443 us (73%)
  local copies, waits for them, and re-layouts  60.1 us (10%)
  matrix products  43.7 us (7%)
  other arithmetic  24.1 us (4%)
  blocking collectives  23.7 us (4%)
  between operations  13.4 us (2%)
    reduce_scatter x5, waiting for transfers between devices, per_device(): part = lax.psum_scatter(part, ('z', 'xh'), scatter_dimension=0, tiled=True)  379 us
    all_gather x1, waiting for transfers between devices, per_device(): gathered = lax.all_gather(regrouped, COL_AXES, axis=0, tiled=True)  52.8 us
    dot_general x5, matrix products, per_device(): ladder = jnp.dot(amps, cols, preferred_element_type=jnp.float32)  43.7 us
    gather x5, local copies, waits for them, and re-layouts, per_device(): difference = ladder - ladder[partner_i]  25.9 us
    gather x3, local copies, waits for them, and re-layouts, per_device(): amps = gathered[pos_of_stored[inv[p_of_i]]]  25.3 us
    all_to_all x1, blocking collectives, per_device(): lax.all_to_all(stored, ROW_AXES, split_axis=1, concat_axis=0, tiled=True)  23.7 us
    sub x5, other arithmetic, per_device(): difference = ladder - ladder[partner_i]  18 us
  transfers between devices with their start and end apart: 11, of which 7 were waited for; matrix products, arithmetic and copies ran while one was open for 15% of the time, Pallas kernels for 0%

profile of v1, /device:TPU:0, one launch (start us, length us, event | category | flops | bytes accessed | tf_op | source)
XLA Modules:
  0.0 608.9 jit_solution(10416544063559315658)
XLA Ops:
  6.5 23.7 %all_to_all.19 = bf16[8,16,3200]{2,0,1:T(8,128)(2,1)} all-to-all(bf16[8,16,3200]{2,0,1:T(8,128)(2,1)} %bitcast.17), channel_id=1, replica_groups=mesh['z'=4,'xh'=2,'core'=2,'xl'=2,'y'=4] {'z','xh','core'}, dimensions={1} | all-to-all | bytes 1638400 | tf_op jit(solution)/shard_map/all_to_all | solution.py:21
  31.0 4.3 scatter_custom_fusion
  35.4 4.5 gather_fusion
  39.9 4.5 gather_fusion.3
  44.5 4.5 gather_fusion.1
  49.2 52.8 %all-gather.2.cloned.1.call-done = bf16[1024,3200]{1,0:T(8,128)(2,1)} async-done(((bf16[128,3200]{1,0:T(8,128)(2,1)}), bf16[1024,3200]{1,0:T(8,128)(2,1)}) %all-gather.2.cloned.1.call-update) | async-done | bytes 6553616 | tf_op jit(solution)/shard_map/all_gather | solution.py:22
  102.0 16.3 %gather_fusion.2 = bf16[1024,3200]{1,0:T(8,128)(2,1)} fusion(bf16[1024,3200]{1,0:T(8,128)(2,1)} %all-gather.2.cloned.1.call-done, s32[1024]{0:T(1024)S(1)} %broadcast_clamp_fusion.3), kind=kCustom, calls=%fused_computation.2 | custom fusion | bytes 13111296 | tf_op jit(solution)/shard_map/gather | solution.py:46
  118.2 8.7 %fusion.8 = f32[1024,640]{1,0:T(8,128)S(1)} fusion(bf16[1024,3200]{1,0:T(8,128)(2,1)} %gather_fusion.2, bf16[3200,3200]{1,0:T(8,128)(2,1)} %param.5), kind=kOutput, calls=%fused_computation.18 | convolution fusion | flops 4194304000 | bytes 13271040 | tf_op jit(solution)/shard_map/dot_general | solution.py:53
  127.0 5.2 gather_fusion.4
  132.2 3.6 sub.63
  135.9 8.8 %fusion.6 = f32[1024,640]{1,0:T(8,128)S(1)} fusion(bf16[1024,3200]{1,0:T(8,128)(2,1)} %gather_fusion.2, bf16[3200,3200]{1,0:T(8,128)(2,1)} %param.5), kind=kOutput, calls=%fused_computation.16 | convolution fusion | flops 4194304000 | bytes 13271040 | tf_op jit(solution)/shard_map/dot_general | solution.py:53
  144.7 5.2 gather_fusion.5
  149.9 3.5 sub.64
  153.7 8.8 %fusion.4 = f32[1024,640]{1,0:T(8,128)S(1)} fusion(bf16[1024,3200]{1,0:T(8,128)(2,1)} %gather_fusion.2, bf16[3200,3200]{1,0:T(8,128)(2,1)} %param.5), kind=kOutput, calls=%fused_computation.14 | convolution fusion | flops 4194304000 | bytes 13271040 | tf_op jit(solution)/shard_map/dot_general | solution.py:53
  162.4 5.2 gather_fusion.6
  167.6 3.7 sub.65
  171.3 8.8 %fusion.2 = f32[1024,640]{1,0:T(8,128)S(1)} fusion(bf16[1024,3200]{1,0:T(8,128)(2,1)} %gather_fusion.2, bf16[3200,3200]{1,0:T(8,128)(2,1)} %param.5), kind=kOutput, calls=%fused_computation.12 | convolution fusion | flops 4194304000 | bytes 13271040 | tf_op jit(solution)/shard_map/dot_general | solution.py:53
  180.1 5.2 gather_fusion.7
  185.3 3.6 sub.66
  188.9 8.8 %fusion = f32[1024,640]{1,0:T(8,128)S(1)} fusion(bf16[1024,3200]{1,0:T(8,128)(2,1)} %gather_fusion.2, bf16[3200,3200]{1,0:T(8,128)(2,1)} %param.5), kind=kOutput, calls=%fused_computation.10 | convolution fusion | flops 4194304000 | bytes 13271040 | tf_op jit(solution)/shard_map/dot_general | solution.py:53
  197.7 5.1 gather_fusion.8
  202.8 3.6 sub.67
  209.3 9.0 %reduce-scatter.27.cloned.1.call-done = f32[512,640]{1,0:T(8,128)} async-done(((f32[1024,640]{1,0:T(8,128)}), f32[512,640]{1,0:T(8,128)}) %reduce-scatter.27.cloned.1.call-update) | async-done | bytes 1310736 | tf_op jit(solution)/shard_map/reduce_scatter | solution.py:55
  218.3 78.5 %reduce-scatter.13.cloned.1.call-done = f32[64,640]{1,0:T(8,128)} async-done(((f32[512,640]{1,0:T(8,128)}), f32[64,640]{1,0:T(8,128)}) %reduce-scatter.13.cloned.1.call-update) | async-done | bytes 163856 | tf_op jit(solution)/shard_map/reduce_scatter | solution.py:56
  297.7 75.1 %reduce-scatter.17.cloned.1.call-done = f32[64,640]{1,0:T(8,128)} async-done(((f32[512,640]{1,0:T(8,128)}), f32[64,640]{1,0:T(8,128)}) %reduce-scatter.17.cloned.1.call-update) | async-done | bytes 163856 | tf_op jit(solution)/shard_map/reduce_scatter | solution.py:56
  372.8 0.9 convert_dynamic-update-slice_fusion.3
  373.8 75.1 %reduce-scatter.21.cloned.1.call-done = f32[64,640]{1,0:T(8,128)} async-done(((f32[512,640]{1,0:T(8,128)}), f32[64,640]{1,0:T(8,128)}) %reduce-scatter.21.cloned.1.call-update) | async-done | bytes 163856 | tf_op jit(solution)/shard_map/reduce_scatter | solution.py:56
  448.9 0.9 convert_dynamic-update-slice_fusion.2
  449.8 75.0 %reduce-scatter.25.cloned.1.call-done = f32[64,640]{1,0:T(8,128)} async-done(((f32[512,640]{1,0:T(8,128)}), f32[64,640]{1,0:T(8,128)}) %reduce-scatter.25.cloned.1.call-update) | async-done | bytes 163856 | tf_op jit(solution)/shard_map/reduce_scatter | solution.py:56
  524.8 0.9 convert_dynamic-update-slice_fusion.1
  525.7 75.1 %reduce-scatter.29.cloned.1.call-done = f32[64,640]{1,0:T(8,128)} async-done(((f32[512,640]{1,0:T(8,128)}), f32[64,640]{1,0:T(8,128)}) %reduce-scatter.29.cloned.1.call-update) | async-done | bytes 163856 | tf_op jit(solution)/shard_map/reduce_scatter | solution.py:56
  600.8 1.6 convert_dynamic-update-slice_fusion
  (43 shorter events, 5.1 us)
Async XLA Ops:
  6.5 33.4 %copy-start = (s32[1024]{0:T(1024)S(1)}, s32[1024]{0:T(1024)}, u32[]{:S(2)}) copy-start(s32[1024]{0:T(1024)} %param.7) | copy-start | bytes 12292
  6.5 95.4 %all-gather.2.cloned.1.call-start = ((), (), s32[]{:S(2)}) async-start(), calls=%async_computation.11 | async-start | bytes 7372800 | tf_op jit(solution)/shard_map/all_gather | solution.py:22
  30.3 176.2 %reduce-scatter.11.cloned.1.call-start = ((), (), s32[]{:S(2)}) async-start(), calls=%async_computation.12 | async-start | bytes 3932160 | tf_op jit(solution)/shard_map/reduce_scatter | solution.py:55
  135.9 71.4 %reduce-scatter.15.cloned.1.call-start = ((), (), s32[]{:S(2)}) async-start(), calls=%async_computation.14 | async-start | bytes 3932160 | tf_op jit(solution)/shard_map/reduce_scatter | solution.py:55
  153.4 54.6 %reduce-scatter.19.cloned.1.call-start = ((), (), s32[]{:S(2)}) async-start(), calls=%async_computation.16 | async-start | bytes 3932160 | tf_op jit(solution)/shard_map/reduce_scatter | solution.py:55
  171.3 37.4 %reduce-scatter.23.cloned.1.call-start = ((), (), s32[]{:S(2)}) async-start(), calls=%async_computation.18 | async-start | bytes 3932160 | tf_op jit(solution)/shard_map/reduce_scatter | solution.py:55
  188.9 29.4 %reduce-scatter.27.cloned.1.call-start = ((), (), s32[]{:S(2)}) async-start(), calls=%async_computation.20 | async-start | bytes 3932160 | tf_op jit(solution)/shard_map/reduce_scatter | solution.py:55
  206.4 90.4 %reduce-scatter.13.cloned.1.call-start = ((), (), s32[]{:S(2)}) async-start(), calls=%async_computation.13 | async-start | bytes 1474560 | tf_op jit(solution)/shard_map/reduce_scatter | solution.py:56
  207.2 165.7 %reduce-scatter.17.cloned.1.call-start = ((), (), s32[]{:S(2)}) async-start(), calls=%async_computation.15 | async-start | bytes 1474560 | tf_op jit(solution)/shard_map/reduce_scatter | solution.py:56
  207.9 394.5 %copy-start.1 = (s32[1024]{0:T(1024)S(1)}, s32[1024]{0:T(1024)}, u32[]{:S(2)}) copy-start(s32[1024]{0:T(1024)} %param.7) | copy-start | bytes 12292
  207.9 240.9 %reduce-scatter.21.cloned.1.call-start = ((), (), s32[]{:S(2)}) async-start(), calls=%async_computation.17 | async-start | bytes 1474560 | tf_op jit(solution)/shard_map/reduce_scatter | solution.py:56
  208.7 316.1 %reduce-scatter.25.cloned.1.call-start = ((), (), s32[]{:S(2)}) async-start(), calls=%async_computation.19 | async-start | bytes 1474560 | tf_op jit(solution)/shard_map/reduce_scatter | solution.py:56
  209.3 391.6 %reduce-scatter.29.cloned.1.call-start = ((), (), s32[]{:S(2)}) async-start(), calls=%async_computation.21 | async-start | bytes 1474560 | tf_op jit(solution)/shard_map/reduce_scatter | solution.py:56
  525.7 75.1 %copy-start.2 = (bf16[64,3200]{1,0:T(8,128)(2,1)}, bf16[64,3200]{1,0:T(8,128)(2,1)S(1)}, u32[]{:S(2)}) copy-start(bf16[64,3200]{1,0:T(8,128)(2,1)S(1)} %convert_dynamic-update-slice_fusion.1) | copy-start | bytes 1228804
Sparse Core Ops, SparseCore 0:
  30.4 71.5 all-gather.1
  136.0 11.5 reduce-scatter.10
  153.6 11.5 reduce-scatter.14
  171.4 11.5 reduce-scatter.18
  189.0 11.6 reduce-scatter.22
  206.5 11.6 reduce-scatter.26
  222.4 74.4 reduce-scatter.12
  300.9 71.8 reduce-scatter.16
  376.9 71.9 reduce-scatter.20
  452.8 71.9 reduce-scatter.24
  528.9 71.8 reduce-scatter.28

commit v2 on v1

--- a/solution.py
+++ b/solution.py
@@ -5,7 +5,7 @@
 
 ROW_AXES = ("z", "xh", "core")
 COL_AXES = ("xl", "y")
-N_CHUNKS = 5
+N_CHUNKS = 4
 
 
 def per_device(stored, integrals, layout, partner):
@@ -28,32 +28,17 @@
     pos_of_stored = s_col * (n_row * local_rows) + s_row * local_rows + s_off
     inv = jnp.zeros((total,), jnp.int32).at[layout].set(s)
 
-    i = jnp.arange(total, dtype=jnp.int32)
-    t = i % block
-    g = i // block
-    xh = g % n_xh
-    z = (g // n_xh) % n_z
-    core = g // (n_xh * n_z)
-    p_of_i = ((z * n_xh + xh) * n_core + core) * block + t
-    pt = partner[p_of_i]
-    pt_t = pt % block
-    pt_g = pt // block
-    pt_core = pt_g % n_core
-    pt_xh = (pt_g // n_core) % n_xh
-    pt_z = pt_g // (n_core * n_xh)
-    partner_i = ((pt_core * n_z + pt_z) * n_xh + pt_xh) * block + pt_t
-
-    amps = gathered[pos_of_stored[inv[p_of_i]]]
+    amps = gathered[pos_of_stored[inv]]
 
     n_cols = integrals.shape[1]
-    width = n_cols // N_CHUNKS
+    tiles = n_cols // 128
+    bounds = [128 * (tiles * j // N_CHUNKS) for j in range(N_CHUNKS)] + [n_cols]
     outs = []
     for j in range(N_CHUNKS):
-        cols = integrals[:, j * width:(j + 1) * width]
+        cols = integrals[:, bounds[j]:bounds[j + 1]]
         ladder = jnp.dot(amps, cols, preferred_element_type=jnp.float32)
-        difference = ladder - ladder[partner_i]
-        part = lax.psum_scatter(difference, "core", scatter_dimension=0, tiled=True)
-        part = lax.psum_scatter(part, ("z", "xh"), scatter_dimension=0, tiled=True)
+        difference = ladder - ladder[partner]
+        part = lax.psum_scatter(difference, ROW_AXES, scatter_dimension=0, tiled=True)
         outs.append(part.astype(jnp.bfloat16))
     return jnp.concatenate(outs, axis=1)
 

time: 609 us -> 457 us (0.75)
  waiting for transfers between devices: 443 us -> 307 us
  local copies, waits for them, and re-layouts: 60.1 us -> 49.1 us
    reduce_scatter x10 -> x4, waiting for transfers between devices: 388 us -> 245 us  [per_device(): lax.psum_scatter(difference, ROW_AXES, scatter_dimension=0, tiled=True)]
    gather x9 -> x6, local copies, waits for them, and re-layouts: 55.8 us -> 44.8 us  [the longest x4 24 us: per_device(): difference = ladder - ladder[partner]]
    all_gather x1, waiting for transfers between devices: 52.8 us -> 62 us  [per_device(): gathered = lax.all_gather(regrouped, COL_AXES, axis=0, tiled=True)]
    dot_general x5 -> x4, matrix products: 43.7 us -> 39.5 us  [per_device(): ladder = jnp.dot(amps, cols, preferred_element_type=jnp.float32)]
    sub x5 -> x4, other arithmetic: 18 us -> 17.5 us  [per_device(): difference = ladder - ladder[partner]]
  transfers between devices with their start and end apart: 11 -> 5, of which waited for: 7 -> 5; matrix products, arithmetic and copies ran while one was open for 15% -> 16% of each run, Pallas kernels for 0% -> 0%
where the time goes in v2:
time: 457 us; the launch traced here: 456 us
  waiting for transfers between devices  307 us (67%)
  local copies, waits for them, and re-layouts  49.1 us (11%)
  matrix products  39.5 us (9%)
  blocking collectives  23.7 us (5%)
  other arithmetic  22.8 us (5%)
  between operations  13.2 us (3%)
    reduce_scatter x4, waiting for transfers between devices, per_device(): lax.psum_scatter(difference, ROW_AXES, scatter_dimension=0, tiled=True)  245 us
    all_gather x1, waiting for transfers between devices, per_device(): gathered = lax.all_gather(regrouped, COL_AXES, axis=0, tiled=True)  62 us
    dot_general x4, matrix products, per_device(): ladder = jnp.dot(amps, cols, preferred_element_type=jnp.float32)  39.5 us
    gather x4, local copies, waits for them, and re-layouts, per_device(): difference = ladder - ladder[partner]  24 us
    all_to_all x1, blocking collectives, per_device(): lax.all_to_all(stored, ROW_AXES, split_axis=1, concat_axis=0, tiled=True)  23.7 us
    gather x2, local copies, waits for them, and re-layouts, per_device(): amps = gathered[pos_of_stored[inv]]  20.8 us
    sub x4, other arithmetic, per_device(): difference = ladder - ladder[partner]  17.5 us
  transfers between devices with their start and end apart: 5, of which 5 were waited for; matrix products, arithmetic and copies ran while one was open for 16% of the time, Pallas kernels for 0%

profile of v2, /device:TPU:0, one launch (start us, length us, event | category | flops | bytes accessed | tf_op | source)
XLA Modules:
  0.0 456.2 jit_solution(9454027328959855415)
XLA Ops:
  6.5 23.7 %all_to_all.19 = bf16[8,16,3200]{2,0,1:T(8,128)(2,1)} all-to-all(bf16[8,16,3200]{2,0,1:T(8,128)(2,1)} %bitcast.11), channel_id=1, replica_groups=mesh['z'=4,'xh'=2,'core'=2,'xl'=2,'y'=4] {'z','xh','core'}, dimensions={1} | all-to-all | bytes 1638400 | tf_op jit(solution)/shard_map/all_to_all | solution.py:21
  30.3 0.0 all-gather.2.cloned.1.call-update
  30.3 0.0 reduce-scatter.5.cloned.1.call-start
  30.3 0.7 compare_select_fusion.3
  31.0 4.3 scatter_custom_fusion
  35.4 4.5 gather_fusion
  39.9 62.0 %all-gather.2.cloned.1.call-done = bf16[1024,3200]{1,0:T(8,128)(2,1)} async-done(((bf16[128,3200]{1,0:T(8,128)(2,1)}), bf16[1024,3200]{1,0:T(8,128)(2,1)}) %all-gather.2.cloned.1.call-update) | async-done | bytes 6553616 | tf_op jit(solution)/shard_map/all_gather | solution.py:22
  102.0 16.3 %gather_fusion.1 = bf16[1024,3200]{1,0:T(8,128)(2,1)} fusion(bf16[1024,3200]{1,0:T(8,128)(2,1)} %all-gather.2.cloned.1.call-done, s32[1024]{0:T(1024)S(1)} %broadcast_clamp_fusion), kind=kCustom, calls=%fused_computation.1 | custom fusion | bytes 13111296 | tf_op jit(solution)/shard_map/gather | solution.py:31
  118.3 9.0 %fusion.6 = f32[1024,768]{1,0:T(8,128)S(1)} fusion(bf16[1024,3200]{1,0:T(8,128)(2,1)} %gather_fusion.1, bf16[3200,3200]{1,0:T(8,128)(2,1)} %param.5), kind=kOutput, calls=%fused_computation.13 | convolution fusion | flops 5033164800 | bytes 14614528 | tf_op jit(solution)/shard_map/dot_general | solution.py:39
  127.3 5.3 %gather_fusion.2 = f32[1024,768]{1,0:T(8,128)} fusion(f32[1024,768]{1,0:T(8,128)S(1)} %fusion.6, s32[1024]{0:T(1024)S(1)} %fusion.20), kind=kCustom, calls=%fused_computation.2 | custom fusion | bytes 6295552 | tf_op jit(solution)/shard_map/gather | solution.py:40
  132.5 3.9 sub.24
  136.5 0.0 reduce-scatter.7.cloned.1.call-start
  136.5 9.0 %fusion.4 = f32[1024,768]{1,0:T(8,128)S(1)} fusion(bf16[1024,3200]{1,0:T(8,128)(2,1)} %gather_fusion.1, bf16[3200,3200]{1,0:T(8,128)(2,1)} %param.5), kind=kOutput, calls=%fused_computation.11 | convolution fusion | flops 5033164800 | bytes 14614528 | tf_op jit(solution)/shard_map/dot_general | solution.py:39
  145.6 5.3 %gather_fusion.3 = f32[1024,768]{1,0:T(8,128)} fusion(f32[1024,768]{1,0:T(8,128)S(1)} %fusion.4, s32[1024]{0:T(1024)S(1)} %fusion.20), kind=kCustom, calls=%fused_computation.3 | custom fusion | bytes 6295552 | tf_op jit(solution)/shard_map/gather | solution.py:40
  150.9 4.0 sub.25
  155.0 0.2 reduce-scatter.9.cloned.1.call-start
  155.2 9.2 %fusion.2 = f32[1024,768]{1,0:T(8,128)S(1)} fusion(bf16[1024,3200]{1,0:T(8,128)(2,1)} %gather_fusion.1, bf16[3200,3200]{1,0:T(8,128)(2,1)} %param.5), kind=kOutput, calls=%fused_computation.9 | convolution fusion | flops 5033164800 | bytes 14614528 | tf_op jit(solution)/shard_map/dot_general | solution.py:39
  164.4 5.3 %gather_fusion.4 = f32[1024,768]{1,0:T(8,128)} fusion(f32[1024,768]{1,0:T(8,128)S(1)} %fusion.2, s32[1024]{0:T(1024)S(1)} %fusion.20), kind=kCustom, calls=%fused_computation.4 | custom fusion | bytes 6295552 | tf_op jit(solution)/shard_map/gather | solution.py:40
  169.8 4.0 sub.26
  173.8 0.0 reduce-scatter.11.cloned.1.call-start
  173.8 12.2 %fusion = f32[1024,896]{1,0:T(8,128)} fusion(bf16[1024,3200]{1,0:T(8,128)(2,1)} %gather_fusion.1, bf16[3200,3200]{1,0:T(8,128)(2,1)} %param.5), kind=kOutput, calls=%fused_computation.7 | convolution fusion | flops 5872025600 | bytes 15958016 | tf_op jit(solution)/shard_map/dot_general | solution.py:39
  186.1 8.1 %gather_fusion.5 = f32[1024,896]{1,0:T(8,128)} fusion(f32[1024,896]{1,0:T(8,128)} %fusion, s32[1024]{0:T(1024)S(1)} %fusion.20), kind=kCustom, calls=%fused_computation.5 | custom fusion | bytes 7344128 | tf_op jit(solution)/shard_map/gather | solution.py:40
  194.2 5.5 %sub.27 = f32[1024,896]{1,0:T(8,128)} subtract(f32[1024,896]{1,0:T(8,128)} %fusion, f32[1024,896]{1,0:T(8,128)} %gather_fusion.5) | non-fusion elementwise | flops 917504 | bytes 11010048 | tf_op jit(solution)/shard_map/sub | solution.py:40
  199.8 11.2 %reduce-scatter.5.cloned.1.call-done = f32[64,768]{1,0:T(8,128)} async-done(((f32[1024,768]{1,0:T(8,128)}), f32[64,768]{1,0:T(8,128)}) %reduce-scatter.5.cloned.1.call-update) | async-done | bytes 196624 | tf_op jit(solution)/shard_map/reduce_scatter | solution.py:41
  210.9 0.9 convert_element_type.12
  211.9 77.4 %reduce-scatter.7.cloned.1.call-done = f32[64,768]{1,0:T(8,128)} async-done(((f32[1024,768]{1,0:T(8,128)}), f32[64,768]{1,0:T(8,128)}) %reduce-scatter.7.cloned.1.call-update) | async-done | bytes 196624 | tf_op jit(solution)/shard_map/reduce_scatter | solution.py:41
  289.3 0.9 convert_element_type.13
  290.2 77.3 %reduce-scatter.9.cloned.1.call-done = f32[64,768]{1,0:T(8,128)} async-done(((f32[1024,768]{1,0:T(8,128)}), f32[64,768]{1,0:T(8,128)}) %reduce-scatter.9.cloned.1.call-update) | async-done | bytes 196624 | tf_op jit(solution)/shard_map/reduce_scatter | solution.py:41
  367.5 0.9 convert_element_type.14
  368.5 79.4 %reduce-scatter.11.cloned.1.call-done = f32[64,896]{1,0:T(8,128)} async-done(((f32[1024,896]{1,0:T(8,128)}), f32[64,896]{1,0:T(8,128)}) %reduce-scatter.11.cloned.1.call-update) | async-done | bytes 229392 | tf_op jit(solution)/shard_map/reduce_scatter | solution.py:41
  447.9 1.0 convert_element_type.15
  448.9 0.8 pad_maximum_fusion
  (12 shorter events, 0.1 us)
Async XLA Ops:
  6.5 33.4 %copy-start = (s32[1024]{0:T(1024)S(1)}, s32[1024]{0:T(1024)}, u32[]{:S(2)}) copy-start(s32[1024]{0:T(1024)} %param.7) | copy-start | bytes 12292
  6.5 95.4 %all-gather.2.cloned.1.call-start = ((), (), s32[]{:S(2)}) async-start(), calls=%async_computation.5 | async-start | bytes 7372800 | tf_op jit(solution)/shard_map/all_gather | solution.py:22
  30.3 180.6 %reduce-scatter.5.cloned.1.call-start = ((), (), s32[]{:S(2)}) async-start(), calls=%async_computation.6 | async-start | bytes 3342336 | tf_op jit(solution)/shard_map/reduce_scatter | solution.py:41
  136.5 152.8 %reduce-scatter.7.cloned.1.call-start = ((), (), s32[]{:S(2)}) async-start(), calls=%async_computation.7 | async-start | bytes 3342336 | tf_op jit(solution)/shard_map/reduce_scatter | solution.py:41
  155.0 212.6 %reduce-scatter.9.cloned.1.call-start = ((), (), s32[]{:S(2)}) async-start(), calls=%async_computation.8 | async-start | bytes 3342336 | tf_op jit(solution)/shard_map/reduce_scatter | solution.py:41
  173.8 274.1 %reduce-scatter.11.cloned.1.call-start = ((), (), s32[]{:S(2)}) async-start(), calls=%async_computation.9 | async-start | bytes 3899392 | tf_op jit(solution)/shard_map/reduce_scatter | solution.py:41
Sparse Core Ops, SparseCore 0:
  30.4 71.5 all-gather.1
  136.6 74.2 reduce-scatter.4
  215.0 74.2 reduce-scatter.6
  293.2 74.2 reduce-scatter.8
  371.5 76.3 reduce-scatter.10

commit v3 on v2

v3 whole, which is shorter than its diff:
```python
import jax
import jax.numpy as jnp
from jax import lax
from jax.sharding import Mesh, PartitionSpec as P

ROW_AXES = ("z", "xh", "core")
COL_AXES = ("xl", "y")


def per_device(stored, integrals, layout, partner):
    local_rows, k_total = stored.shape
    n_row = lax.axis_size(ROW_AXES)
    n_col = lax.axis_size(COL_AXES)
    total = local_rows * n_row * n_col
    k_local = integrals.shape[0]

    pieces = stored.reshape(local_rows, n_row, k_local).transpose(1, 0, 2)
    outgoing = jnp.broadcast_to(pieces[:, None], (n_row, n_col, local_rows, k_local)).reshape(total, k_local)
    by_stored = lax.all_to_all(outgoing, ROW_AXES + COL_AXES, split_axis=0, concat_axis=0, tiled=True)

    inv = jnp.zeros((total,), jnp.int32).at[layout].set(jnp.arange(total, dtype=jnp.int32))
    amps = by_stored[inv]

    ladder = jnp.dot(amps, integrals, preferred_element_type=jnp.float32)
    difference = ladder - ladder[partner]
    blocks = difference.reshape(n_row, total // n_row, difference.shape[1])
    received = lax.all_to_all(blocks, ROW_AXES, split_axis=0, concat_axis=0, tiled=True)
    return jnp.sum(received, axis=0).astype(jnp.bfloat16)


def solution(mesh):
    n_row, n_col = mesh.devices.shape
    fine = Mesh(mesh.devices.reshape(4, n_row // 8, 2, 2, n_col // 2), ROW_AXES + COL_AXES)
    return jax.shard_map(
        per_device,
        mesh=fine,
        in_specs=(P(ROW_AXES + COL_AXES, None), P(ROW_AXES, COL_AXES), P(), P()),
        out_specs=P(ROW_AXES, COL_AXES),
        check_vma=False,
    )
```

time: 457 us -> 329 us (0.72)
  waiting for transfers between devices: 307 us -> 74.8 us
  blocking collectives: 23.7 us -> 154 us
  between operations: 13.2 us -> 0.07 us
  starting transfers between devices: 0.35 us -> 11.6 us
  matrix products: 39.5 us -> 30.5 us
  other arithmetic: 22.8 us -> 15.4 us
  local copies, waits for them, and re-layouts: 49.1 us -> 42.1 us
    reduce_scatter x4 -> x0, waiting for transfers between devices: 245 us -> none  [per_device(): lax.psum_scatter(difference, ROW_AXES, scatter_dimension=0, tiled=True)]
    all_to_all x1, blocking collectives: 23.7 us -> 154 us  [per_device(): lax.all_to_all(blocks, ROW_AXES, split_axis=0, concat_axis=0, tiled=True)]
    all_to_all x0 -> x1, waiting for transfers between devices: none -> 74.8 us  [per_device(): lax.all_to_all(outgoing, ROW_AXES + COL_AXES, split_axis=0, concat_axis=0...]
    all_gather x1 -> x0, waiting for transfers between devices: 62 us -> none  [per_device(): gathered = lax.all_gather(regrouped, COL_AXES, axis=0, tiled=True)]
    all_to_all x0 -> x1, starting transfers between devices: none -> 11.6 us  [per_device(): lax.all_to_all(outgoing, ROW_AXES + COL_AXES, split_axis=0, concat_axis=0...]
    dot_general x4 -> x1, matrix products: 39.5 us -> 30.5 us  [per_device(): ladder = jnp.dot(amps, integrals, preferred_element_type=jnp.float32)]
    sub x4 -> x1, other arithmetic: 17.5 us -> 9.22 us  [per_device(): difference = ladder - ladder[partner]]
    gather x4 -> x1, local copies, waits for them, and re-layouts: 24 us -> 17.1 us  [per_device(): difference = ladder - ladder[partner]]
  transfers between devices with their start and end apart: 5 -> 1, of which waited for: 5 -> 1; matrix products, arithmetic and copies ran while one was open for 16% -> 1% of each run, Pallas kernels for 0% -> 0%
where the time goes in v3:
time: 329 us; the launch traced here: 328 us
  blocking collectives  154 us (47%)
  waiting for transfers between devices  74.8 us (23%)
  local copies, waits for them, and re-layouts  42.1 us (13%)
  matrix products  30.5 us (9%)
  other arithmetic  15.4 us (5%)
  starting transfers between devices  11.6 us (4%)
    all_to_all x1, blocking collectives, per_device(): lax.all_to_all(blocks, ROW_AXES, split_axis=0, concat_axis=0, tiled=True)  154 us
    all_to_all x1, waiting for transfers between devices, per_device(): lax.all_to_all(outgoing, ROW_AXES + COL_AXES, split_axis=0, concat_axis=0...  74.8 us
    dot_general x1, matrix products, per_device(): ladder = jnp.dot(amps, integrals, preferred_element_type=jnp.float32)  30.5 us
    gather x1, local copies, waits for them, and re-layouts, per_device(): difference = ladder - ladder[partner]  17.1 us
    gather x1, local copies, waits for them, and re-layouts, per_device(): amps = by_stored[inv]  16.3 us
    all_to_all x1, starting transfers between devices, per_device(): lax.all_to_all(outgoing, ROW_AXES + COL_AXES, split_axis=0, concat_axis=0...  11.6 us
    sub x1, other arithmetic, per_device(): difference = ladder - ladder[partner]  9.22 us
  transfers between devices with their start and end apart: 1, of which 1 were waited for; matrix products, arithmetic and copies ran while one was open for 1% of the time, Pallas kernels for 0%

profile of v3, /device:TPU:0, one launch (start us, length us, event | category | flops | bytes accessed | tf_op | source)
XLA Modules:
  0.0 328.3 jit_solution(6145515449185926482)
XLA Ops:
  0.0 0.0 copy-start
  0.0 0.0 copy-start.1
  0.0 4.3 %broadcast_in_dim.15 = bf16[16,8,8,3200]{3,2,1,0:T(8,128)(2,1)} broadcast(bf16[16,8,3200]{2,1,0:T(8,128)(2,1)} %bitcast.11), dimensions={0,2,3} | broadcast | bytes 7372800 | tf_op jit(solution)/shard_map/broadcast_in_dim | solution.py:18
  4.3 11.6 %all-to-all-start = ((bf16[128,8,3200]{2,1,0:T(8,128)(2,1)}), bf16[128,8,3200]{2,1,0:T(8,128)(2,1)}, u32[]{:S(2)}, u32[]{:S(2)}) async-start(bf16[128,8,3200]{2,1,0:T(8,128)(2,1)} %bitcast.10), calls=%async_computation | async-start | bytes 13107200 | tf_op jit(solution)/shard_map/all_to_all | solution.py:19
  15.9 0.0 copy-done
  16.0 4.3 %scatter_custom_fusion = s32[1024]{0:T(1024)S(1)} fusion(s32[1024]{0:T(1024)S(1)} %compare_select_fusion.2, s32[1024]{0:T(1024)S(1)} %iota.3, s32[]{:T(128)} %constant.0.clone.1), kind=kCustom, calls=%fused_computation.8 | custom fusion | bytes 4100 | tf_op jit(solution)/shard_map/scatter | solution.py:21
  20.3 0.0 copy-done.1
  20.3 74.8 %all-to-all-done = bf16[128,8,3200]{2,1,0:T(8,128)(2,1)} async-done(((bf16[128,8,3200]{2,1,0:T(8,128)(2,1)}), bf16[128,8,3200]{2,1,0:T(8,128)(2,1)}, u32[]{:S(2)}, u32[]{:S(2)}) %all-to-all-start) | async-done | bytes 6553632 | tf_op jit(solution)/shard_map/all_to_all | solution.py:19
  95.1 16.3 %gather_fusion = bf16[1024,3200]{1,0:T(8,128)(2,1)} fusion(bf16[1024,3200]{1,0:T(8,128)(2,1)} %bitcast.3, s32[1024]{0:T(1024)S(1)} %fusion), kind=kCustom, calls=%fused_computation | custom fusion | bytes 13111296 | tf_op jit(solution)/shard_map/gather | solution.py:22
  111.4 30.5 %fusion.4 = f32[1024,3200]{1,0:T(8,128)} fusion(bf16[1024,3200]{1,0:T(8,128)(2,1)} %gather_fusion, bf16[3200,3200]{1,0:T(8,128)(2,1)} %param.5), kind=kOutput, calls=%fused_computation.10 | convolution fusion | flops 20971520000 | bytes 40140800 | tf_op jit(solution)/shard_map/dot_general | solution.py:24
  141.9 17.1 %gather_fusion.1 = f32[1024,3200]{1,0:T(8,128)} fusion(f32[1024,3200]{1,0:T(8,128)} %fusion.4, s32[1024]{0:T(1024)S(1)} %fusion.1), kind=kCustom, calls=%fused_computation.1 | custom fusion | bytes 26218496 | tf_op jit(solution)/shard_map/gather | solution.py:25
  159.1 9.2 %sub.3 = f32[1024,3200]{1,0:T(8,128)S(1)} subtract(f32[1024,3200]{1,0:T(8,128)} %fusion.4, f32[1024,3200]{1,0:T(8,128)} %gather_fusion.1) | non-fusion elementwise | flops 3276800 | bytes 39321600 | tf_op jit(solution)/shard_map/sub | solution.py:25
  168.3 153.8 %all_to_all.17 = f32[16,64,3200]{2,1,0:T(8,128)} all-to-all(f32[16,64,3200]{2,1,0:T(8,128)S(1)} %bitcast.9), channel_id=1, replica_groups=mesh['z'=4,'xh'=2,'core'=2,'xl'=2,'y'=4] {'z','xh','core'}, dimensions={0} | all-to-all | bytes 26214400 | tf_op jit(solution)/shard_map/all_to_all | solution.py:27
  322.1 6.2 %reduce_sum.9 = bf16[64,3200]{1,0:T(8,128)(2,1)} reduce(f32[16,64,3200]{2,1,0:T(8,128)} %all_to_all.17, f32[]{:T(128)} %constant.2.clone.1), dimensions={0}, to_apply=%region_1.0 | reduce | flops 3072000 | bytes 13516804 | tf_op jit(solution)/shard_map/reduce_sum | solution.py:28
  (4 shorter events, 0.0 us)
Async XLA Ops:
  0.0 15.9 %copy-start = (s32[1024]{0:T(1024)S(1)}, s32[1024]{0:T(1024)}, u32[]{:S(2)}) copy-start(s32[1024]{0:T(1024)} %param.6) | copy-start | bytes 12292
  0.0 20.3 %copy-start.1 = (s32[1024]{0:T(1024)S(1)}, s32[1024]{0:T(1024)}, u32[]{:S(2)}) copy-start(s32[1024]{0:T(1024)} %param.7) | copy-start | bytes 12292
  4.3 90.8 %all-to-all-start = ((bf16[128,8,3200]{2,1,0:T(8,128)(2,1)}), bf16[128,8,3200]{2,1,0:T(8,128)(2,1)}, u32[]{:S(2)}, u32[]{:S(2)}) async-start(bf16[128,8,3200]{2,1,0:T(8,128)(2,1)} %bitcast.10), calls=%async_computation | async-start | bytes 13107200 | tf_op jit(solution)/shard_map/all_to_all | solution.py:19

commit v4 on v2

--- a/solution.py
+++ b/solution.py
@@ -5,7 +5,6 @@
 
 ROW_AXES = ("z", "xh", "core")
 COL_AXES = ("xl", "y")
-N_CHUNKS = 4
 
 
 def per_device(stored, integrals, layout, partner):
@@ -14,7 +13,7 @@
     n_xh = lax.axis_size("xh")
     n_core = lax.axis_size("core")
     n_row = n_z * n_xh * n_core
-    n_col = lax.axis_size("xl") * lax.axis_size("y")
+    n_col = lax.axis_size(COL_AXES)
     total = local_rows * n_row * n_col
     block = total // n_row
 
@@ -28,19 +27,25 @@
     pos_of_stored = s_col * (n_row * local_rows) + s_row * local_rows + s_off
     inv = jnp.zeros((total,), jnp.int32).at[layout].set(s)
 
-    amps = gathered[pos_of_stored[inv]]
+    i = jnp.arange(total, dtype=jnp.int32)
+    g = i // block
+    xh = g % n_xh
+    core = (g // n_xh) % n_core
+    z = g // (n_xh * n_core)
+    p_of_i = ((z * n_xh + xh) * n_core + core) * block + (i % block)
+    q = partner[p_of_i]
+    q_g = q // block
+    q_core = q_g % n_core
+    q_xh = (q_g // n_core) % n_xh
+    q_z = q_g // (n_core * n_xh)
+    partner_i = ((q_z * n_core + q_core) * n_xh + q_xh) * block + (q % block)
 
-    n_cols = integrals.shape[1]
-    tiles = n_cols // 128
-    bounds = [128 * (tiles * j // N_CHUNKS) for j in range(N_CHUNKS)] + [n_cols]
-    outs = []
-    for j in range(N_CHUNKS):
-        cols = integrals[:, bounds[j]:bounds[j + 1]]
-        ladder = jnp.dot(amps, cols, preferred_element_type=jnp.float32)
-        difference = ladder - ladder[partner]
-        part = lax.psum_scatter(difference, ROW_AXES, scatter_dimension=0, tiled=True)
-        outs.append(part.astype(jnp.bfloat16))
-    return jnp.concatenate(outs, axis=1)
+    amps = gathered[pos_of_stored[inv[p_of_i]]]
+    ladder = jnp.dot(amps, integrals, preferred_element_type=jnp.float32)
+    difference = ladder - ladder[partner_i]
+    part = lax.psum_scatter(difference, ("z", "core"), scatter_dimension=0, tiled=True)
+    part = lax.psum_scatter(part, "xh", scatter_dimension=0, tiled=True)
+    return part.astype(jnp.bfloat16)
 
 
 def solution(mesh):

time: 457 us -> 297 us (0.65)
  waiting for transfers between devices: 307 us -> 159 us
  matrix products: 39.5 us -> 30.5 us
  other arithmetic: 22.8 us -> 17.2 us
    reduce_scatter x4 -> x2, waiting for transfers between devices: 245 us -> 107 us  [the longest x1 74 us: per_device(): lax.psum_scatter(difference, ('z', 'core'), scatter_dimension=0, tiled=True)]
    all_gather x1, waiting for transfers between devices: 62 us -> 52.8 us  [per_device(): gathered = lax.all_gather(regrouped, COL_AXES, axis=0, tiled=True)]
    dot_general x4 -> x1, matrix products: 39.5 us -> 30.5 us  [per_device(): ladder = jnp.dot(amps, integrals, preferred_element_type=jnp.float32)]
    sub x4 -> x1, other arithmetic: 17.5 us -> 14.4 us  [per_device(): difference = ladder - ladder[partner_i]]
    gather x6 -> x5, local copies, waits for them, and re-layouts: 44.8 us -> 47 us  [the longest x3 25.3 us: per_device(): amps = gathered[pos_of_stored[inv[p_of_i]]]]
  transfers between devices with their start and end apart: 5 -> 3, of which waited for: 5 -> 3; matrix products, arithmetic and copies ran while one was open for 16% -> 6% of each run, Pallas kernels for 0% -> 0%
where the time goes in v4:
time: 297 us; the launch traced here: 295 us
  waiting for transfers between devices  159 us (54%)
  local copies, waits for them, and re-layouts  51.3 us (17%)
  matrix products  30.5 us (10%)
  blocking collectives  23.7 us (8%)
  other arithmetic  17.2 us (6%)
  between operations  13.2 us (4%)
    reduce_scatter x1, waiting for transfers between devices, per_device(): lax.psum_scatter(difference, ('z', 'core'), scatter_dimension=0, tiled=True)  74 us
    all_gather x1, waiting for transfers between devices, per_device(): gathered = lax.all_gather(regrouped, COL_AXES, axis=0, tiled=True)  52.8 us
    reduce_scatter x1, waiting for transfers between devices, per_device(): part = lax.psum_scatter(part, 'xh', scatter_dimension=0, tiled=True)  32.7 us
    dot_general x1, matrix products, per_device(): ladder = jnp.dot(amps, integrals, preferred_element_type=jnp.float32)  30.5 us
    gather x3, local copies, waits for them, and re-layouts, per_device(): amps = gathered[pos_of_stored[inv[p_of_i]]]  25.3 us
    all_to_all x1, blocking collectives, per_device(): lax.all_to_all(stored, ROW_AXES, split_axis=1, concat_axis=0, tiled=True)  23.7 us
    gather x1, local copies, waits for them, and re-layouts, per_device(): difference = ladder - ladder[partner_i]  17.1 us
    sub x1, other arithmetic, per_device(): difference = ladder - ladder[partner_i]  14.4 us
  transfers between devices with their start and end apart: 3, of which 3 were waited for; matrix products, arithmetic and copies ran while one was open for 6% of the time, Pallas kernels for 0%

profile of v4, /device:TPU:0, one launch (start us, length us, event | category | flops | bytes accessed | tf_op | source)
XLA Modules:
  0.0 295.5 jit_solution(10515165706835330987)
XLA Ops:
  6.5 0.0 copy-start
  6.5 0.0 all-gather.2.cloned.1.call-start
  6.5 23.7 %all_to_all.19 = bf16[8,16,3200]{2,0,1:T(8,128)(2,1)} all-to-all(bf16[8,16,3200]{2,0,1:T(8,128)(2,1)} %bitcast.15), channel_id=1, replica_groups=mesh['z'=4,'xh'=2,'core'=2,'xl'=2,'y'=4] {'z','xh','core'}, dimensions={1} | all-to-all | bytes 1638400 | tf_op jit(solution)/shard_map/all_to_all | solution.py:20
  30.3 0.0 all-gather.2.cloned.1.call-update
  30.3 0.0 reduce-scatter.3.cloned.1.call-start
  30.4 0.0 copy-done
  30.4 4.5 %gather_fusion.3 = s32[1024]{0:T(1024)S(1)} fusion(s32[1024]{0:T(1024)S(1)} %copy-done, s32[1024]{0:T(1024)S(1)} %broadcast_clamp_fusion.1), kind=kCustom, calls=%fused_computation.3 | custom fusion | bytes 12288 | tf_op jit(solution)/shard_map/gather | solution.py:36
  34.9 0.7 compare_select_fusion.8
  35.6 4.3 %scatter_custom_fusion = s32[1024]{0:T(1024)S(1)} fusion(s32[1024]{0:T(1024)S(1)} %compare_select_fusion.8, s32[1024]{0:T(1024)S(1)} %iota.13, s32[]{:T(128)} %constant.129.clone.1), kind=kCustom, calls=%fused_computation.79 | custom fusion | bytes 4100 | tf_op jit(solution)/shard_map/scatter | solution.py:28
  39.9 4.5 %gather_fusion = s32[1024]{0:T(1024)S(1)} fusion(s32[1024]{0:T(1024)S(1)} %scatter_custom_fusion, s32[1024]{0:T(1024)S(1)} %broadcast_clamp_fusion.1), kind=kCustom, calls=%fused_computation | custom fusion | bytes 12288 | tf_op jit(solution)/shard_map/gather | solution.py:43
  44.5 4.5 %gather_fusion.1 = s32[1024]{0:T(1024)S(1)} fusion(s32[1024]{0:T(1024)S(1)} %get-tuple-element.5, s32[1024]{0:T(1024)S(1)} %get-tuple-element.6), kind=kCustom, calls=%fused_computation.1 | custom fusion | bytes 12288 | tf_op jit(solution)/shard_map/gather | solution.py:43
  49.0 0.1 compare_select_fusion
  49.2 52.8 %all-gather.2.cloned.1.call-done = bf16[1024,3200]{1,0:T(8,128)(2,1)} async-done(((bf16[128,3200]{1,0:T(8,128)(2,1)}), bf16[1024,3200]{1,0:T(8,128)(2,1)}) %all-gather.2.cloned.1.call-update) | async-done | bytes 6553616 | tf_op jit(solution)/shard_map/all_gather | solution.py:21
  102.0 16.3 %gather_fusion.2 = bf16[1024,3200]{1,0:T(8,128)(2,1)} fusion(bf16[1024,3200]{1,0:T(8,128)(2,1)} %all-gather.2.cloned.1.call-done, s32[1024]{0:T(1024)S(1)} %broadcast_clamp_fusion.3), kind=kCustom, calls=%fused_computation.2 | custom fusion | bytes 13111296 | tf_op jit(solution)/shard_map/gather | solution.py:43
  118.3 30.5 %fusion.24 = f32[1024,3200]{1,0:T(8,128)} fusion(bf16[1024,3200]{1,0:T(8,128)(2,1)} %gather_fusion.2, bf16[3200,3200]{1,0:T(8,128)(2,1)} %param.5), kind=kOutput, calls=%fused_computation.81 | convolution fusion | flops 20971520000 | bytes 40140800 | tf_op jit(solution)/shard_map/dot_general | solution.py:44
  148.8 17.1 %gather_fusion.4 = f32[1024,3200]{1,0:T(8,128)} fusion(f32[1024,3200]{1,0:T(8,128)} %fusion.24, s32[1024]{0:T(1024)S(1)} %broadcast_clamp_fusion), kind=kCustom, calls=%fused_computation.4 | custom fusion | bytes 26218496 | tf_op jit(solution)/shard_map/gather | solution.py:45
  165.9 0.0 copy-start.1
  165.9 14.4 %sub.51 = f32[1024,3200]{1,0:T(8,128)} subtract(f32[1024,3200]{1,0:T(8,128)} %fusion.24, f32[1024,3200]{1,0:T(8,128)} %gather_fusion.4) | non-fusion elementwise | flops 3276800 | bytes 39321600 | tf_op jit(solution)/shard_map/sub | solution.py:45
  180.3 0.0 reduce-scatter.3.cloned.1.call-update
  180.3 0.0 reduce-scatter.5.cloned.1.call-start
  180.4 74.0 %reduce-scatter.3.cloned.1.call-done = f32[128,3200]{1,0:T(8,128)} async-done(((f32[1024,3200]{1,0:T(8,128)}), f32[128,3200]{1,0:T(8,128)}) %reduce-scatter.3.cloned.1.call-update) | async-done | bytes 1638416 | tf_op jit(solution)/shard_map/reduce_scatter | solution.py:46
  254.3 0.0 reduce-scatter.5.cloned.1.call-update
  254.4 32.7 %reduce-scatter.5.cloned.1.call-done = f32[64,3200]{1,0:T(8,128)} async-done(((f32[128,3200]{1,0:T(8,128)}), f32[64,3200]{1,0:T(8,128)}) %reduce-scatter.5.cloned.1.call-update) | async-done | bytes 819216 | tf_op jit(solution)/shard_map/reduce_scatter | solution.py:47
  287.0 1.9 convert_element_type.3
  289.0 0.0 copy-done.1
  (8 shorter events, 0.1 us)
Async XLA Ops:
  6.5 23.9 %copy-start = (s32[1024]{0:T(1024)S(1)}, s32[1024]{0:T(1024)}, u32[]{:S(2)}) copy-start(s32[1024]{0:T(1024)} %param.7) | copy-start | bytes 12292
  6.5 95.4 %all-gather.2.cloned.1.call-start = ((), (), s32[]{:S(2)}) async-start(), calls=%async_computation.3 | async-start | bytes 7372800 | tf_op jit(solution)/shard_map/all_gather | solution.py:21
  30.3 224.1 %reduce-scatter.3.cloned.1.call-start = ((), (), s32[]{:S(2)}) async-start(), calls=%async_computation.4 | async-start | bytes 14745600 | tf_op jit(solution)/shard_map/reduce_scatter | solution.py:46
  165.9 123.1 %copy-start.1 = (s32[1024]{0:T(1024)S(1)}, s32[1024]{0:T(1024)}, u32[]{:S(2)}) copy-start(s32[1024]{0:T(1024)} %param.7) | copy-start | bytes 12292
  180.3 106.7 %reduce-scatter.5.cloned.1.call-start = ((), (), s32[]{:S(2)}) async-start(), calls=%async_computation.5 | async-start | bytes 2457600 | tf_op jit(solution)/shard_map/reduce_scatter | solution.py:47
Sparse Core Ops, SparseCore 0:
  30.4 71.5 all-gather.1
  180.4 73.8 reduce-scatter.2
  256.7 30.2 reduce-scatter.4

commit v5 on v4

--- a/solution.py
+++ b/solution.py
@@ -1,10 +1,45 @@
 import jax
 import jax.numpy as jnp
 from jax import lax
+from jax.experimental import pallas as pl
+from jax.experimental.pallas import tpu as pltpu
 from jax.sharding import Mesh, PartitionSpec as P
 
 ROW_AXES = ("z", "xh", "core")
 COL_AXES = ("xl", "y")
+
+
+def _antisym_kernel(idx_ref, own_ref, all_ref, out_ref, buf, sem):
+    rows = out_ref.shape[0]
+    base = pl.program_id(0) * rows
+
+    def start(r, carry):
+        src = idx_ref[base + r]
+        pltpu.make_async_copy(all_ref.at[pl.ds(src, 1)], buf.at[pl.ds(r, 1)], sem.at[0]).start()
+        return carry
+
+    lax.fori_loop(0, rows, start, 0)
+    pltpu.make_async_copy(all_ref.at[pl.ds(0, rows)], buf, sem.at[0]).wait()
+    out_ref[...] = own_ref[...] - buf[...]
+
+
+def antisymmetrize(ladder, partner_rows, rows=128):
+    total, width = ladder.shape
+    return pl.pallas_call(
+        _antisym_kernel,
+        grid_spec=pltpu.PrefetchScalarGridSpec(
+            num_scalar_prefetch=1,
+            grid=(total // rows,),
+            in_specs=[
+                pl.BlockSpec((rows, width), lambda b, idx: (b, 0)),
+                pl.BlockSpec(memory_space=pl.ANY),
+            ],
+            out_specs=pl.BlockSpec((rows, width), lambda b, idx: (b, 0)),
+            scratch_shapes=[pltpu.VMEM((rows, width), ladder.dtype), pltpu.SemaphoreType.DMA((1,))],
+        ),
+        out_shape=jax.ShapeDtypeStruct(ladder.shape, ladder.dtype),
+        cost_estimate=pl.CostEstimate(flops=total * width, transcendentals=0, bytes_accessed=3 * total * width * 4),
+    )(partner_rows, ladder, ladder)
 
 
 def per_device(stored, integrals, layout, partner):
@@ -42,7 +77,7 @@
 
     amps = gathered[pos_of_stored[inv[p_of_i]]]
     ladder = jnp.dot(amps, integrals, preferred_element_type=jnp.float32)
-    difference = ladder - ladder[partner_i]
+    difference = antisymmetrize(ladder, partner_i)
     part = lax.psum_scatter(difference, ("z", "core"), scatter_dimension=0, tiled=True)
     part = lax.psum_scatter(part, "xh", scatter_dimension=0, tiled=True)
     return part.astype(jnp.bfloat16)

time: 297 us -> 289 us (0.973)
  Pallas kernels: 0 us -> 24 us
  local copies, waits for them, and re-layouts: 51.3 us -> 34.2 us
  other arithmetic: 17.2 us -> 2.64 us
    pallas_call x0 -> x1, Pallas kernels: none -> 24 us  [antisymmetrize(): pl.pallas_call(_antisym_kernel, grid_spec=pltpu.PrefetchScalarGridSpec(nu...]
    gather x1 -> x0, local copies, waits for them, and re-layouts: 17.1 us -> none  [per_device(): difference = ladder - ladder[partner_i]]
    sub x1 -> x0, other arithmetic: 14.4 us -> none  [per_device(): difference = ladder - ladder[partner_i]]
where the time goes in v5:
time: 289 us; the launch traced here: 288 us
  waiting for transfers between devices  160 us (55%)
  local copies, waits for them, and re-layouts  34.2 us (12%)
  matrix products  30.5 us (11%)
  Pallas kernels  24 us (8%)
  blocking collectives  23.7 us (8%)
  between operations  13.2 us (5%)
    reduce_scatter x1, waiting for transfers between devices, per_device(): lax.psum_scatter(difference, ('z', 'core'), scatter_dimension=0, tiled=True)  74 us
    all_gather x1, waiting for transfers between devices, per_device(): gathered = lax.all_gather(regrouped, COL_AXES, axis=0, tiled=True)  52.9 us
    reduce_scatter x1, waiting for transfers between devices, per_device(): part = lax.psum_scatter(part, 'xh', scatter_dimension=0, tiled=True)  32.6 us
    dot_general x1, matrix products, per_device(): ladder = jnp.dot(amps, integrals, preferred_element_type=jnp.float32)  30.5 us
    gather x3, local copies, waits for them, and re-layouts, per_device(): amps = gathered[pos_of_stored[inv[p_of_i]]]  25.3 us
    pallas_call x1, Pallas kernels, antisymmetrize(): pl.pallas_call(_antisym_kernel, grid_spec=pltpu.PrefetchScalarGridSpec(nu...  24 us
    all_to_all x1, blocking collectives, per_device(): lax.all_to_all(stored, ROW_AXES, split_axis=1, concat_axis=0, tiled=True)  23.7 us
  transfers between devices with their start and end apart: 3, of which 3 were waited for; matrix products, arithmetic and copies ran while one was open for 6% of the time, Pallas kernels for 0%

profile of v5, /device:TPU:0, one launch (start us, length us, event | category | flops | bytes accessed | tf_op | source)
XLA Modules:
  0.0 287.9 jit_solution(3061572115310903159)
XLA Ops:
  6.5 0.0 copy-start
  6.5 0.0 copy-start.1
  6.5 0.0 all-gather.2.cloned.1.call-start
  6.5 23.7 %all_to_all.19 = bf16[8,16,3200]{2,0,1:T(8,128)(2,1)} all-to-all(bf16[8,16,3200]{2,0,1:T(8,128)(2,1)} %bitcast.13), channel_id=1, replica_groups=mesh['z'=4,'xh'=2,'core'=2,'xl'=2,'y'=4] {'z','xh','core'}, dimensions={1} | all-to-all | bytes 1638400 | tf_op jit(solution)/shard_map/all_to_all | solution.py:55
  30.3 0.0 all-gather.2.cloned.1.call-update
  30.3 0.0 reduce-scatter.3.cloned.1.call-start
  30.4 0.0 copy-done
  30.4 4.5 %gather_fusion = s32[1024]{0:T(1024)S(1)} fusion(s32[1024]{0:T(1024)S(1)} %copy-done, s32[1024]{0:T(1024)S(1)} %broadcast_clamp_fusion.2), kind=kCustom, calls=%fused_computation | custom fusion | bytes 12288 | tf_op jit(solution)/shard_map/gather | solution.py:71
  34.9 0.0 copy-done.1
  35.0 4.3 %scatter_custom_fusion = s32[1024]{0:T(1024)S(1)} fusion(s32[1024]{0:T(1024)S(1)} %compare_select_fusion.5, s32[1024]{0:T(1024)S(1)} %iota.16, s32[]{:T(128)} %constant.129.clone.1), kind=kCustom, calls=%fused_computation.84 | custom fusion | bytes 4100 | tf_op jit(solution)/shard_map/scatter | solution.py:63
  39.3 4.5 %gather_fusion.1 = s32[1024]{0:T(1024)S(1)} fusion(s32[1024]{0:T(1024)S(1)} %scatter_custom_fusion, s32[1024]{0:T(1024)S(1)} %broadcast_clamp_fusion.2), kind=kCustom, calls=%fused_computation.1 | custom fusion | bytes 12288 | tf_op jit(solution)/shard_map/gather | solution.py:78
  43.9 4.5 %gather_fusion.2 = s32[1024]{0:T(1024)S(1)} fusion(s32[1024]{0:T(1024)S(1)} %get-tuple-element.5, s32[1024]{0:T(1024)S(1)} %get-tuple-element.6), kind=kCustom, calls=%fused_computation.2 | custom fusion | bytes 12288 | tf_op jit(solution)/shard_map/gather | solution.py:78
  48.4 0.6 fusion.13.idx_ref
  49.0 52.9 %all-gather.2.cloned.1.call-done = bf16[1024,3200]{1,0:T(8,128)(2,1)} async-done(((bf16[128,3200]{1,0:T(8,128)(2,1)}), bf16[1024,3200]{1,0:T(8,128)(2,1)}) %all-gather.2.cloned.1.call-update) | async-done | bytes 6553616 | tf_op jit(solution)/shard_map/all_gather | solution.py:56
  102.0 16.3 %gather_fusion.3 = bf16[1024,3200]{1,0:T(8,128)(2,1)} fusion(bf16[1024,3200]{1,0:T(8,128)(2,1)} %all-gather.2.cloned.1.call-done, s32[1024]{0:T(1024)S(1)} %broadcast_clamp_fusion), kind=kCustom, calls=%fused_computation.3 | custom fusion | bytes 13111296 | tf_op jit(solution)/shard_map/gather | solution.py:78
  118.3 30.5 %fusion.29.own_ref.all_ref = f32[1024,3200]{1,0:T(8,128)} fusion(bf16[1024,3200]{1,0:T(8,128)(2,1)} %gather_fusion.3, bf16[3200,3200]{1,0:T(8,128)(2,1)} %param.5), kind=kOutput, calls=%fused_computation.86 | convolution fusion | flops 20971520000 | bytes 40140800 | tf_op jit(solution)/shard_map/dot_general | solution.py:79
  148.8 24.0 %shard_map.46 = f32[1024,3200]{1,0:T(8,128)} custom-call(s32[1024]{0:T(1024)} %fusion.13.idx_ref, f32[1024,3200]{1,0:T(8,128)} %fusion.29.own_ref.all_ref, f32[1024,3200]{1,0:T(8,128)} %fusion.29.own_ref.all_ref), custom_call_target="tpu_custom_call" | custom-call | flops 3276800 | bytes 39321600 | tf_op jit(solution)/shard_map/pallas_call | solution.py:28
  172.8 0.0 reduce-scatter.3.cloned.1.call-update
  172.8 0.0 reduce-scatter.5.cloned.1.call-start
  172.8 74.0 %reduce-scatter.3.cloned.1.call-done = f32[128,3200]{1,0:T(8,128)} async-done(((f32[1024,3200]{1,0:T(8,128)}), f32[128,3200]{1,0:T(8,128)}) %reduce-scatter.3.cloned.1.call-update) | async-done | bytes 1638416 | tf_op jit(solution)/shard_map/reduce_scatter | solution.py:81
  246.8 0.0 reduce-scatter.5.cloned.1.call-update
  246.8 32.6 %reduce-scatter.5.cloned.1.call-done = f32[64,3200]{1,0:T(8,128)} async-done(((f32[128,3200]{1,0:T(8,128)}), f32[64,3200]{1,0:T(8,128)}) %reduce-scatter.5.cloned.1.call-update) | async-done | bytes 819216 | tf_op jit(solution)/shard_map/reduce_scatter | solution.py:82
  279.5 1.9 convert_element_type.3
  (8 shorter events, 0.1 us)
Async XLA Ops:
  6.5 23.9 %copy-start = (s32[1024]{0:T(1024)S(1)}, s32[1024]{0:T(1024)}, u32[]{:S(2)}) copy-start(s32[1024]{0:T(1024)} %param.7) | copy-start | bytes 12292
  6.5 28.4 %copy-start.1 = (s32[1024]{0:T(1024)S(1)}, s32[1024]{0:T(1024)}, u32[]{:S(2)}) copy-start(s32[1024]{0:T(1024)} %param.6) | copy-start | bytes 12292
  6.5 95.4 %all-gather.2.cloned.1.call-start = ((), (), s32[]{:S(2)}) async-start(), calls=%async_computation.3 | async-start | bytes 7372800 | tf_op jit(solution)/shard_map/all_gather | solution.py:56
  30.3 216.5 %reduce-scatter.3.cloned.1.call-start = ((), (), s32[]{:S(2)}) async-start(), calls=%async_computation.4 | async-start | bytes 14745600 | tf_op jit(solution)/shard_map/reduce_scatter | solution.py:81
  172.8 106.7 %reduce-scatter.5.cloned.1.call-start = ((), (), s32[]{:S(2)}) async-start(), calls=%async_computation.5 | async-start | bytes 2457600 | tf_op jit(solution)/shard_map/reduce_scatter | solution.py:82
Sparse Core Ops, SparseCore 0:
  30.4 71.5 all-gather.1
  172.9 73.8 reduce-scatter.2
  249.2 30.2 reduce-scatter.4

commit v6 on v4

--- a/solution.py
+++ b/solution.py
@@ -1,10 +1,62 @@
 import jax
 import jax.numpy as jnp
 from jax import lax
+from jax.experimental import pallas as pl
+from jax.experimental.pallas import tpu as pltpu
 from jax.sharding import Mesh, PartitionSpec as P
 
 ROW_AXES = ("z", "xh", "core")
 COL_AXES = ("xl", "y")
+
+
+def _antisym_kernel(own_idx, partner_idx, all_ref, out_ref, own_buf, partner_buf, sem):
+    rows = out_ref.shape[0]
+    step = pl.program_id(0)
+    steps = pl.num_programs(0)
+
+    def issue(at, slot):
+        base = at * rows
+
+        def body(r, carry):
+            pltpu.make_async_copy(all_ref.at[pl.ds(own_idx[base + r], 1)], own_buf.at[slot, pl.ds(r, 1)], sem.at[0, slot]).start()
+            pltpu.make_async_copy(all_ref.at[pl.ds(partner_idx[base + r], 1)], partner_buf.at[slot, pl.ds(r, 1)], sem.at[1, slot]).start()
+            return carry
+
+        lax.fori_loop(0, rows, body, 0)
+
+    @pl.when(step == 0)
+    def _():
+        issue(0, 0)
+
+    @pl.when(step + 1 < steps)
+    def _():
+        issue(step + 1, (step + 1) % 2)
+
+    slot = step % 2
+    pltpu.make_async_copy(all_ref.at[pl.ds(0, rows)], own_buf.at[slot], sem.at[0, slot]).wait()
+    pltpu.make_async_copy(all_ref.at[pl.ds(0, rows)], partner_buf.at[slot], sem.at[1, slot]).wait()
+    out_ref[...] = own_buf[slot] - partner_buf[slot]
+
+
+def antisymmetrize(ladder, own_rows, partner_rows, rows=64):
+    total, width = ladder.shape
+    return pl.pallas_call(
+        _antisym_kernel,
+        grid_spec=pltpu.PrefetchScalarGridSpec(
+            num_scalar_prefetch=2,
+            grid=(total // rows,),
+            in_specs=[pl.BlockSpec(memory_space=pl.ANY)],
+            out_specs=pl.BlockSpec((rows, width), lambda b, own, other: (b, 0)),
+            scratch_shapes=[
+                pltpu.VMEM((2, rows, width), ladder.dtype),
+                pltpu.VMEM((2, rows, width), ladder.dtype),
+                pltpu.SemaphoreType.DMA((2, 2)),
+            ],
+        ),
+        out_shape=jax.ShapeDtypeStruct(ladder.shape, ladder.dtype),
+        compiler_params=pltpu.CompilerParams(dimension_semantics=("arbitrary",)),
+        cost_estimate=pl.CostEstimate(flops=total * width, transcendentals=0, bytes_accessed=3 * total * width * 4),
+    )(own_rows, partner_rows, ladder)
 
 
 def per_device(stored, integrals, layout, partner):
@@ -34,15 +86,9 @@
     z = g // (n_xh * n_core)
     p_of_i = ((z * n_xh + xh) * n_core + core) * block + (i % block)
     q = partner[p_of_i]
-    q_g = q // block
-    q_core = q_g % n_core
-    q_xh = (q_g // n_core) % n_xh
-    q_z = q_g // (n_core * n_xh)
-    partner_i = ((q_z * n_core + q_core) * n_xh + q_xh) * block + (q % block)
 
-    amps = gathered[pos_of_stored[inv[p_of_i]]]
-    ladder = jnp.dot(amps, integrals, preferred_element_type=jnp.float32)
-    difference = ladder - ladder[partner_i]
+    ladder = jnp.dot(gathered, integrals, preferred_element_type=jnp.float32)
+    difference = antisymmetrize(ladder, pos_of_stored[inv[p_of_i]], pos_of_stored[inv[q]])
     part = lax.psum_scatter(difference, ("z", "core"), scatter_dimension=0, tiled=True)
     part = lax.psum_scatter(part, "xh", scatter_dimension=0, tiled=True)
     return part.astype(jnp.bfloat16)

time: 297 us -> 268 us (0.902)
  Pallas kernels: 0 us -> 18.9 us
  waiting for transfers between devices: 159 us -> 142 us
  local copies, waits for them, and re-layouts: 51.3 us -> 35.5 us
  other arithmetic: 17.2 us -> 2.71 us
    pallas_call x0 -> x1, Pallas kernels: none -> 18.9 us  [antisymmetrize(): pl.pallas_call(_antisym_kernel, grid_spec=pltpu.PrefetchScalarGridSpec(nu...]
    all_gather x1, waiting for transfers between devices: 52.8 us -> 35.2 us  [per_device(): gathered = lax.all_gather(regrouped, COL_AXES, axis=0, tiled=True)]
    gather x4, local copies, waits for them, and re-layouts: 42.5 us -> 26.7 us  [the longest x1 8.84 us: per_device(): pos_of_stored[inv[p_of_i]]]
    sub x1 -> x0, other arithmetic: 14.4 us -> none  [per_device(): difference = ladder - ladder[partner_i]]
  transfers between devices with their start and end apart: 3 -> 3, of which waited for: 3 -> 3; matrix products, arithmetic and copies ran while one was open for 6% -> 14% of each run, Pallas kernels for 0% -> 0%
where the time goes in v6:
time: 268 us; the launch traced here: 267 us
  waiting for transfers between devices  142 us (53%)
  local copies, waits for them, and re-layouts  35.5 us (13%)
  matrix products  30.5 us (11%)
  blocking collectives  23.7 us (9%)
  Pallas kernels  18.9 us (7%)
  between operations  13.2 us (5%)
  other arithmetic  2.71 us (1%)
    reduce_scatter x1, waiting for transfers between devices, per_device(): lax.psum_scatter(difference, ('z', 'core'), scatter_dimension=0, tiled=True)  74 us
    all_gather x1, waiting for transfers between devices, per_device(): gathered = lax.all_gather(regrouped, COL_AXES, axis=0, tiled=True)  35.2 us
    reduce_scatter x1, waiting for transfers between devices, per_device(): part = lax.psum_scatter(part, 'xh', scatter_dimension=0, tiled=True)  32.7 us
    dot_general x1, matrix products, per_device(): ladder = jnp.dot(gathered, integrals, preferred_element_type=jnp.float32)  30.5 us
    all_to_all x1, blocking collectives, per_device(): lax.all_to_all(stored, ROW_AXES, split_axis=1, concat_axis=0, tiled=True)  23.7 us
    pallas_call x1, Pallas kernels, antisymmetrize(): pl.pallas_call(_antisym_kernel, grid_spec=pltpu.PrefetchScalarGridSpec(nu...  18.9 us
    gather x1, local copies, waits for them, and re-layouts, per_device(): pos_of_stored[inv[p_of_i]]  8.84 us
    gather x1, local copies, waits for them, and re-layouts, per_device(): pos_of_stored[inv[q]]  8.8 us
  transfers between devices with their start and end apart: 3, of which 3 were waited for; matrix products, arithmetic and copies ran while one was open for 14% of the time, Pallas kernels for 0%

profile of v6, /device:TPU:0, one launch (start us, length us, event | category | flops | bytes accessed | tf_op | source)
XLA Modules:
  0.0 266.6 jit_solution(18025709439750470751)
XLA Ops:
  6.5 0.0 copy-start
  6.5 0.0 all-gather.2.cloned.1.call-start
  6.5 23.7 %all_to_all.19 = bf16[8,16,3200]{2,0,1:T(8,128)(2,1)} all-to-all(bf16[8,16,3200]{2,0,1:T(8,128)(2,1)} %bitcast.15), channel_id=1, replica_groups=mesh['z'=4,'xh'=2,'core'=2,'xl'=2,'y'=4] {'z','xh','core'}, dimensions={1} | all-to-all | bytes 1638400 | tf_op jit(solution)/shard_map/all_to_all | solution.py:72
  30.3 0.0 all-gather.2.cloned.1.call-update
  30.3 0.0 reduce-scatter.3.cloned.1.call-start
  30.4 0.0 copy-done
  30.4 4.5 %gather_fusion.2 = s32[1024]{0:T(1024)S(1)} fusion(s32[1024]{0:T(1024)S(1)} %copy-done, s32[1024]{0:T(1024)S(1)} %broadcast_clamp_fusion.2), kind=kCustom, calls=%fused_computation.2 | custom fusion | bytes 12288 | tf_op jit(solution)/shard_map/gather | solution.py:88
  34.9 0.7 compare_select_fusion.6
  35.6 4.3 %scatter_custom_fusion = s32[1024]{0:T(1024)S(1)} fusion(s32[1024]{0:T(1024)S(1)} %compare_select_fusion.6, s32[1024]{0:T(1024)S(1)} %iota.15, s32[]{:T(128)} %constant.93.clone.1), kind=kCustom, calls=%fused_computation.59 | custom fusion | bytes 4100 | tf_op jit(solution)/shard_map/scatter | solution.py:80
  39.9 4.5 %gather_fusion = s32[1024]{0:T(1024)S(1)} fusion(s32[1024]{0:T(1024)S(1)} %scatter_custom_fusion, s32[1024]{0:T(1024)S(1)} %broadcast_clamp_fusion.2), kind=kCustom, calls=%fused_computation | custom fusion | bytes 12288 | tf_op jit(solution)/shard_map/gather | solution.py:91
  44.5 4.5 %gather_fusion.3 = s32[1024]{0:T(1024)S(1)} fusion(s32[1024]{0:T(1024)S(1)} %scatter_custom_fusion, s32[1024]{0:T(1024)S(1)} %broadcast_clamp_fusion), kind=kCustom, calls=%fused_computation.3 | custom fusion | bytes 12288 | tf_op jit(solution)/shard_map/gather | solution.py:91
  49.1 8.8 %gather_fusion.1 = s32[1024]{0:T(1024)} fusion(s32[1024]{0:T(1024)S(1)} %get-tuple-element.5, s32[1024]{0:T(1024)S(1)} %get-tuple-element.6), kind=kCustom, calls=%fused_computation.1 | custom fusion | bytes 12288 | tf_op jit(solution)/shard_map/gather | solution.py:91
  57.9 8.8 %gather_fusion.4 = s32[1024]{0:T(1024)} fusion(s32[1024]{0:T(1024)S(1)} %get-tuple-element.5, s32[1024]{0:T(1024)S(1)} %broadcast_clamp_fusion.1), kind=kCustom, calls=%fused_computation.4 | custom fusion | bytes 12288 | tf_op jit(solution)/shard_map/gather | solution.py:91
  66.7 35.2 %all-gather.2.cloned.1.call-done = bf16[1024,3200]{1,0:T(8,128)(2,1)} async-done(((bf16[128,3200]{1,0:T(8,128)(2,1)}), bf16[1024,3200]{1,0:T(8,128)(2,1)}) %all-gather.2.cloned.1.call-update) | async-done | bytes 6553616 | tf_op jit(solution)/shard_map/all_gather | solution.py:73
  102.0 30.5 %fusion.20.all_ref = f32[1024,3200]{1,0:T(8,128)} fusion(bf16[1024,3200]{1,0:T(8,128)(2,1)} %all-gather.2.cloned.1.call-done, bf16[3200,3200]{1,0:T(8,128)(2,1)} %param.5), kind=kOutput, calls=%fused_computation.61 | convolution fusion | flops 20971520000 | bytes 40140800 | tf_op jit(solution)/shard_map/dot_general | solution.py:90
  132.5 18.9 %shard_map.46 = f32[1024,3200]{1,0:T(8,128)} custom-call(s32[1024]{0:T(1024)} %gather_fusion.1, s32[1024]{0:T(1024)} %gather_fusion.4, f32[1024,3200]{1,0:T(8,128)} %fusion.20.all_ref), custom_call_target="tpu_custom_call" | custom-call | flops 3276800 | bytes 39321600 | tf_op jit(solution)/shard_map/pallas_call | solution.py:43
  151.4 0.0 reduce-scatter.3.cloned.1.call-update
  151.4 0.0 reduce-scatter.5.cloned.1.call-start
  151.5 74.0 %reduce-scatter.3.cloned.1.call-done = f32[128,3200]{1,0:T(8,128)} async-done(((f32[1024,3200]{1,0:T(8,128)}), f32[128,3200]{1,0:T(8,128)}) %reduce-scatter.3.cloned.1.call-update) | async-done | bytes 1638416 | tf_op jit(solution)/shard_map/reduce_scatter | solution.py:92
  225.5 0.0 reduce-scatter.5.cloned.1.call-update
  225.5 32.7 %reduce-scatter.5.cloned.1.call-done = f32[64,3200]{1,0:T(8,128)} async-done(((f32[128,3200]{1,0:T(8,128)}), f32[64,3200]{1,0:T(8,128)}) %reduce-scatter.5.cloned.1.call-update) | async-done | bytes 819216 | tf_op jit(solution)/shard_map/reduce_scatter | solution.py:93
  258.1 1.9 convert_element_type.3
  (9 shorter events, 0.1 us)
Async XLA Ops:
  6.5 23.9 %copy-start = (s32[1024]{0:T(1024)S(1)}, s32[1024]{0:T(1024)}, u32[]{:S(2)}) copy-start(s32[1024]{0:T(1024)} %param.7) | copy-start | bytes 12292
  6.5 95.4 %all-gather.2.cloned.1.call-start = ((), (), s32[]{:S(2)}) async-start(), calls=%async_computation.3 | async-start | bytes 7372800 | tf_op jit(solution)/shard_map/all_gather | solution.py:73
  30.3 195.2 %reduce-scatter.3.cloned.1.call-start = ((), (), s32[]{:S(2)}) async-start(), calls=%async_computation.4 | async-start | bytes 14745600 | tf_op jit(solution)/shard_map/reduce_scatter | solution.py:92
  151.4 106.7 %reduce-scatter.5.cloned.1.call-start = ((), (), s32[]{:S(2)}) async-start(), calls=%async_computation.5 | async-start | bytes 2457600 | tf_op jit(solution)/shard_map/reduce_scatter | solution.py:93
Sparse Core Ops, SparseCore 0:
  30.4 71.5 all-gather.1
  151.5 73.8 reduce-scatter.2
  227.8 30.2 reduce-scatter.4

commit v7 on v6

--- a/solution.py
+++ b/solution.py
@@ -59,6 +59,58 @@
     )(own_rows, partner_rows, ladder)
 
 
+def _exchange_kernel(src_ref, out_ref, send_sem, recv_sem, local_sem):
+    n_z, n_xh, n_core = (lax.axis_size(a) for a in ROW_AXES)
+    n = n_z * n_xh * n_core
+    z, xh, core, xl, y = (lax.axis_index(a) for a in ROW_AXES + COL_AXES)
+    me = (z * n_xh + xh) * n_core + core
+
+    def peer(k):
+        t = lax.rem(me + k, n)
+        return t, (t // (n_xh * n_core), lax.rem(t // n_core, n_xh), lax.rem(t, n_core), xl, y)
+
+    barrier = pltpu.get_barrier_semaphore()
+    for k in range(1, n):
+        pl.semaphore_signal(barrier, inc=1, device_id=peer(k)[1], device_id_type=pl.DeviceIdType.MESH)
+    pl.semaphore_wait(barrier, n - 1)
+
+    local = pltpu.make_async_copy(src_ref.at[me], out_ref.at[me], local_sem.at[0])
+    local.start()
+    sends = []
+    for k in range(1, n):
+        t, where = peer(k)
+        copy = pltpu.make_async_remote_copy(
+            src_ref=src_ref.at[t],
+            dst_ref=out_ref.at[me],
+            send_sem=send_sem.at[k - 1],
+            recv_sem=recv_sem.at[0],
+            device_id=where,
+            device_id_type=pl.DeviceIdType.MESH,
+        )
+        copy.start()
+        sends.append(copy)
+    for copy in sends:
+        copy.wait_send()
+    pltpu.make_async_copy(src_ref.at[pl.ds(0, n - 1)], out_ref.at[pl.ds(0, n - 1)], recv_sem.at[0]).wait()
+    local.wait()
+
+
+def exchange_over_row(pieces):
+    n = pieces.shape[0]
+    return pl.pallas_call(
+        _exchange_kernel,
+        out_shape=jax.ShapeDtypeStruct(pieces.shape, pieces.dtype),
+        in_specs=[pl.BlockSpec(memory_space=pl.ANY)],
+        out_specs=pl.BlockSpec(memory_space=pl.ANY),
+        scratch_shapes=[
+            pltpu.SemaphoreType.DMA((n - 1,)),
+            pltpu.SemaphoreType.DMA((1,)),
+            pltpu.SemaphoreType.DMA((1,)),
+        ],
+        compiler_params=pltpu.CompilerParams(collective_id=0, has_side_effects=True),
+    )(pieces)
+
+
 def per_device(stored, integrals, layout, partner):
     local_rows = stored.shape[0]
     n_z = lax.axis_size("z")
@@ -69,7 +121,8 @@
     total = local_rows * n_row * n_col
     block = total // n_row
 
-    regrouped = lax.all_to_all(stored, ROW_AXES, split_axis=1, concat_axis=0, tiled=True)
+    pieces = stored.reshape(local_rows, n_row, stored.shape[1] // n_row).transpose(1, 0, 2)
+    regrouped = exchange_over_row(pieces).reshape(n_row * local_rows, pieces.shape[2])
     gathered = lax.all_gather(regrouped, COL_AXES, axis=0, tiled=True)
 
     s = jnp.arange(total, dtype=jnp.int32)

time: 268 us -> 266 us (level)
  blocking collectives: 23.7 us -> 0 us
  Pallas kernels: 18.9 us -> 36.3 us
  waiting for transfers between devices: 142 us -> 146 us
    all_to_all x1 -> x0, blocking collectives: 23.7 us -> none  [per_device(): lax.all_to_all(stored, ROW_AXES, split_axis=1, concat_axis=0, tiled=True)]
    pallas_call x0 -> x1, Pallas kernels: none -> 17.4 us  [exchange_over_row(): pl.pallas_call(_exchange_kernel, out_shape=jax.ShapeDtypeStruct(pieces.sh...]
    all_gather x1, waiting for transfers between devices: 35.2 us -> 39.5 us  [per_device(): gathered = lax.all_gather(regrouped, COL_AXES, axis=0, tiled=True)]
where the time goes in v7:
time: 266 us; the launch traced here: 264 us
  waiting for transfers between devices  146 us (55%)
  Pallas kernels  36.3 us (14%)
  local copies, waits for them, and re-layouts  35.5 us (13%)
  matrix products  30.5 us (11%)
  between operations  13.2 us (5%)
  other arithmetic  2.71 us (1%)
    reduce_scatter x1, waiting for transfers between devices, per_device(): lax.psum_scatter(difference, ('z', 'core'), scatter_dimension=0, tiled=True)  74 us
    all_gather x1, waiting for transfers between devices, per_device(): gathered = lax.all_gather(regrouped, COL_AXES, axis=0, tiled=True)  39.5 us
    reduce_scatter x1, waiting for transfers between devices, per_device(): part = lax.psum_scatter(part, 'xh', scatter_dimension=0, tiled=True)  32.6 us
    dot_general x1, matrix products, per_device(): ladder = jnp.dot(gathered, integrals, preferred_element_type=jnp.float32)  30.5 us
    pallas_call x1, Pallas kernels, antisymmetrize(): pl.pallas_call(_antisym_kernel, grid_spec=pltpu.PrefetchScalarGridSpec(nu...  18.9 us
    pallas_call x1, Pallas kernels, exchange_over_row(): pl.pallas_call(_exchange_kernel, out_shape=jax.ShapeDtypeStruct(pieces.sh...  17.4 us
    gather x1, local copies, waits for them, and re-layouts, per_device(): pos_of_stored[inv[p_of_i]]  8.84 us
    gather x1, local copies, waits for them, and re-layouts, per_device(): pos_of_stored[inv[q]]  8.8 us
  transfers between devices with their start and end apart: 3, of which 3 were waited for; matrix products, arithmetic and copies ran while one was open for 14% of the time, Pallas kernels for 0%

profile of v7, /device:TPU:0, one launch (start us, length us, event | category | flops | bytes accessed | tf_op | source)
XLA Modules:
  0.0 264.5 jit_solution(14729665902582979525)
XLA Ops:
  6.5 0.0 copy-start
  6.5 0.0 all-gather.2.cloned.1.call-start
  6.5 17.4 %shard_map.46 = bf16[16,8,3200]{2,1,0:T(8,128)(2,1)} custom-call(bf16[16,8,3200]{2,1,0:T(8,128)(2,1)} %bitcast.15), custom_call_target="tpu_custom_call" | custom-call | tf_op jit(solution)/shard_map/pallas_call | solution.py:100
  24.0 0.0 all-gather.2.cloned.1.call-update
  24.0 0.0 reduce-scatter.3.cloned.1.call-start
  24.1 0.0 copy-done
  24.1 4.5 %gather_fusion.2 = s32[1024]{0:T(1024)S(1)} fusion(s32[1024]{0:T(1024)S(1)} %copy-done, s32[1024]{0:T(1024)S(1)} %broadcast_clamp_fusion.2), kind=kCustom, calls=%fused_computation.2 | custom fusion | bytes 12288 | tf_op jit(solution)/shard_map/gather | solution.py:141
  28.6 0.7 compare_select_fusion.6
  29.3 4.3 %scatter_custom_fusion = s32[1024]{0:T(1024)S(1)} fusion(s32[1024]{0:T(1024)S(1)} %compare_select_fusion.6, s32[1024]{0:T(1024)S(1)} %iota.15, s32[]{:T(128)} %constant.93.clone.1), kind=kCustom, calls=%fused_computation.59 | custom fusion | bytes 4100 | tf_op jit(solution)/shard_map/scatter | solution.py:133
  33.6 4.5 %gather_fusion = s32[1024]{0:T(1024)S(1)} fusion(s32[1024]{0:T(1024)S(1)} %scatter_custom_fusion, s32[1024]{0:T(1024)S(1)} %broadcast_clamp_fusion.2), kind=kCustom, calls=%fused_computation | custom fusion | bytes 12288 | tf_op jit(solution)/shard_map/gather | solution.py:144
  38.2 4.5 %gather_fusion.3 = s32[1024]{0:T(1024)S(1)} fusion(s32[1024]{0:T(1024)S(1)} %scatter_custom_fusion, s32[1024]{0:T(1024)S(1)} %broadcast_clamp_fusion), kind=kCustom, calls=%fused_computation.3 | custom fusion | bytes 12288 | tf_op jit(solution)/shard_map/gather | solution.py:144
  42.8 8.8 %gather_fusion.1 = s32[1024]{0:T(1024)} fusion(s32[1024]{0:T(1024)S(1)} %get-tuple-element.5, s32[1024]{0:T(1024)S(1)} %get-tuple-element.6), kind=kCustom, calls=%fused_computation.1 | custom fusion | bytes 12288 | tf_op jit(solution)/shard_map/gather | solution.py:144
  51.6 8.8 %gather_fusion.4 = s32[1024]{0:T(1024)} fusion(s32[1024]{0:T(1024)S(1)} %get-tuple-element.5, s32[1024]{0:T(1024)S(1)} %broadcast_clamp_fusion.1), kind=kCustom, calls=%fused_computation.4 | custom fusion | bytes 12288 | tf_op jit(solution)/shard_map/gather | solution.py:144
  60.4 39.5 %all-gather.2.cloned.1.call-done = bf16[1024,3200]{1,0:T(8,128)(2,1)} async-done(((bf16[128,3200]{1,0:T(8,128)(2,1)}), bf16[1024,3200]{1,0:T(8,128)(2,1)}) %all-gather.2.cloned.1.call-update) | async-done | bytes 6553616 | tf_op jit(solution)/shard_map/all_gather | solution.py:126
  99.9 30.5 %fusion.20.all_ref = f32[1024,3200]{1,0:T(8,128)} fusion(bf16[1024,3200]{1,0:T(8,128)(2,1)} %all-gather.2.cloned.1.call-done, bf16[3200,3200]{1,0:T(8,128)(2,1)} %param.5), kind=kOutput, calls=%fused_computation.61 | convolution fusion | flops 20971520000 | bytes 40140800 | tf_op jit(solution)/shard_map/dot_general | solution.py:143
  130.4 18.9 %shard_map.47 = f32[1024,3200]{1,0:T(8,128)} custom-call(s32[1024]{0:T(1024)} %gather_fusion.1, s32[1024]{0:T(1024)} %gather_fusion.4, f32[1024,3200]{1,0:T(8,128)} %fusion.20.all_ref), custom_call_target="tpu_custom_call" | custom-call | flops 3276800 | bytes 39321600 | tf_op jit(solution)/shard_map/pallas_call | solution.py:43
  149.3 0.0 reduce-scatter.3.cloned.1.call-update
  149.3 0.0 reduce-scatter.5.cloned.1.call-start
  149.4 74.0 %reduce-scatter.3.cloned.1.call-done = f32[128,3200]{1,0:T(8,128)} async-done(((f32[1024,3200]{1,0:T(8,128)}), f32[128,3200]{1,0:T(8,128)}) %reduce-scatter.3.cloned.1.call-update) | async-done | bytes 1638416 | tf_op jit(solution)/shard_map/reduce_scatter | solution.py:145
  223.4 0.0 reduce-scatter.5.cloned.1.call-update
  223.4 32.6 %reduce-scatter.5.cloned.1.call-done = f32[64,3200]{1,0:T(8,128)} async-done(((f32[128,3200]{1,0:T(8,128)}), f32[64,3200]{1,0:T(8,128)}) %reduce-scatter.5.cloned.1.call-update) | async-done | bytes 819216 | tf_op jit(solution)/shard_map/reduce_scatter | solution.py:146
  256.0 1.9 convert_element_type.3
  (9 shorter events, 0.1 us)
Async XLA Ops:
  6.5 17.5 %copy-start = (s32[1024]{0:T(1024)S(1)}, s32[1024]{0:T(1024)}, u32[]{:S(2)}) copy-start(s32[1024]{0:T(1024)} %param.7) | copy-start | bytes 12292
  6.5 93.4 %all-gather.2.cloned.1.call-start = ((), (), s32[]{:S(2)}) async-start(), calls=%async_computation.2 | async-start | bytes 7372800 | tf_op jit(solution)/shard_map/all_gather | solution.py:126
  24.0 199.4 %reduce-scatter.3.cloned.1.call-start = ((), (), s32[]{:S(2)}) async-start(), calls=%async_computation.3 | async-start | bytes 14745600 | tf_op jit(solution)/shard_map/reduce_scatter | solution.py:145
  149.3 106.7 %reduce-scatter.5.cloned.1.call-start = ((), (), s32[]{:S(2)}) async-start(), calls=%async_computation.4 | async-start | bytes 2457600 | tf_op jit(solution)/shard_map/reduce_scatter | solution.py:146
Sparse Core Ops, SparseCore 0:
  24.1 75.7 all-gather.1
  149.5 73.8 reduce-scatter.2
  225.8 30.2 reduce-scatter.4

commit v8 on v7

--- a/solution.py
+++ b/solution.py
@@ -111,6 +111,51 @@
     )(pieces)
 
 
+def _pair_sum_kernel(part_ref, out_ref, own_buf, recv_buf, send_sem, recv_sem, local_sem):
+    n_xh = lax.axis_size("xh")
+    z, xh, core, xl, y = (lax.axis_index(a) for a in ROW_AXES + COL_AXES)
+    other = lax.rem(xh + 1, n_xh)
+    where = (z, other, core, xl, y)
+
+    barrier = pltpu.get_barrier_semaphore()
+    pl.semaphore_signal(barrier, inc=1, device_id=where, device_id_type=pl.DeviceIdType.MESH)
+    pl.semaphore_wait(barrier, 1)
+
+    local = pltpu.make_async_copy(part_ref.at[xh], own_buf, local_sem.at[0])
+    local.start()
+    copy = pltpu.make_async_remote_copy(
+        src_ref=part_ref.at[other],
+        dst_ref=recv_buf,
+        send_sem=send_sem.at[0],
+        recv_sem=recv_sem.at[0],
+        device_id=where,
+        device_id_type=pl.DeviceIdType.MESH,
+    )
+    copy.start()
+    local.wait()
+    copy.wait_send()
+    copy.wait_recv()
+    out_ref[...] = (own_buf[...] + recv_buf[...]).astype(out_ref.dtype)
+
+
+def sum_over_pair(part):
+    _, rows, width = part.shape
+    return pl.pallas_call(
+        _pair_sum_kernel,
+        out_shape=jax.ShapeDtypeStruct((rows, width), jnp.bfloat16),
+        in_specs=[pl.BlockSpec(memory_space=pl.ANY)],
+        out_specs=pl.BlockSpec(memory_space=pltpu.VMEM),
+        scratch_shapes=[
+            pltpu.VMEM((rows, width), part.dtype),
+            pltpu.VMEM((rows, width), part.dtype),
+            pltpu.SemaphoreType.DMA((1,)),
+            pltpu.SemaphoreType.DMA((1,)),
+            pltpu.SemaphoreType.DMA((1,)),
+        ],
+        compiler_params=pltpu.CompilerParams(collective_id=1, has_side_effects=True),
+    )(part)
+
+
 def per_device(stored, integrals, layout, partner):
     local_rows = stored.shape[0]
     n_z = lax.axis_size("z")
@@ -143,8 +188,7 @@
     ladder = jnp.dot(gathered, integrals, preferred_element_type=jnp.float32)
     difference = antisymmetrize(ladder, pos_of_stored[inv[p_of_i]], pos_of_stored[inv[q]])
     part = lax.psum_scatter(difference, ("z", "core"), scatter_dimension=0, tiled=True)
-    part = lax.psum_scatter(part, "xh", scatter_dimension=0, tiled=True)
-    return part.astype(jnp.bfloat16)
+    return sum_over_pair(part.reshape(n_xh, block, part.shape[1]))
 
 
 def solution(mesh):

time: 266 us -> 254 us (0.955)
  waiting for transfers between devices: 146 us -> 114 us
  Pallas kernels: 36.3 us -> 58.1 us
    reduce_scatter x1 -> x0, waiting for transfers between devices: 32.6 us -> none  [per_device(): part = lax.psum_scatter(part, 'xh', scatter_dimension=0, tiled=True)]
    pallas_call x0 -> x1, Pallas kernels: none -> 21.8 us  [sum_over_pair(): pl.pallas_call(_pair_sum_kernel, out_shape=jax.ShapeDtypeStruct((rows, wi...]
  transfers between devices with their start and end apart: 3 -> 2, of which waited for: 3 -> 2; matrix products, arithmetic and copies ran while one was open for 14% -> 14% of each run, Pallas kernels for 0% -> 0%
where the time goes in v8:
time: 254 us
  waiting for transfers between devices  114 us (45%)
  Pallas kernels  58.1 us (23%)
  local copies, waits for them, and re-layouts  37.3 us (15%)
  matrix products  30.5 us (12%)
  between operations  13.5 us (5%)
    reduce_scatter x1, waiting for transfers between devices, per_device(): lax.psum_scatter(difference, ('z', 'core'), scatter_dimension=0, tiled=True)  74 us
    all_gather x1, waiting for transfers between devices, per_device(): gathered = lax.all_gather(regrouped, COL_AXES, axis=0, tiled=True)  39.5 us
    dot_general x1, matrix products, per_device(): ladder = jnp.dot(gathered, integrals, preferred_element_type=jnp.float32)  30.5 us
    pallas_call x1, Pallas kernels, sum_over_pair(): pl.pallas_call(_pair_sum_kernel, out_shape=jax.ShapeDtypeStruct((rows, wi...  21.8 us
    pallas_call x1, Pallas kernels, antisymmetrize(): pl.pallas_call(_antisym_kernel, grid_spec=pltpu.PrefetchScalarGridSpec(nu...  18.9 us
    pallas_call x1, Pallas kernels, exchange_over_row(): pl.pallas_call(_exchange_kernel, out_shape=jax.ShapeDtypeStruct(pieces.sh...  17.4 us
    gather x1, local copies, waits for them, and re-layouts, per_device(): pos_of_stored[inv[p_of_i]]  8.84 us
    gather x1, local copies, waits for them, and re-layouts, per_device(): pos_of_stored[inv[q]]  8.8 us
  transfers between devices with their start and end apart: 2, of which 2 were waited for; matrix products, arithmetic and copies ran while one was open for 14% of the time, Pallas kernels for 0%

profile of v8, /device:TPU:0, one launch (start us, length us, event | category | flops | bytes accessed | tf_op | source)
XLA Modules:
  0.0 253.8 jit_solution(9949452054212357420)
XLA Ops:
  6.5 0.0 copy-start
  6.5 0.0 all-gather.2.cloned.1.call-start
  6.5 17.4 %shard_map.46 = bf16[16,8,3200]{2,1,0:T(8,128)(2,1)} custom-call(bf16[16,8,3200]{2,1,0:T(8,128)(2,1)} %bitcast.17), custom_call_target="tpu_custom_call" | custom-call | tf_op jit(solution)/shard_map/pallas_call | solution.py:100
  24.0 0.0 all-gather.2.cloned.1.call-update
  24.0 0.0 reduce-scatter.2.cloned.1.call-start
  24.1 0.0 copy-done
  24.1 4.5 %gather_fusion.2 = s32[1024]{0:T(1024)S(1)} fusion(s32[1024]{0:T(1024)S(1)} %copy-done, s32[1024]{0:T(1024)S(1)} %broadcast_clamp_fusion.2), kind=kCustom, calls=%fused_computation.2 | custom fusion | bytes 12288 | tf_op jit(solution)/shard_map/gather | solution.py:186
  28.6 0.7 compare_select_fusion.6
  29.3 4.3 %scatter_custom_fusion = s32[1024]{0:T(1024)S(1)} fusion(s32[1024]{0:T(1024)S(1)} %compare_select_fusion.6, s32[1024]{0:T(1024)S(1)} %iota.15, s32[]{:T(128)} %constant.93.clone.1), kind=kCustom, calls=%fused_computation.59 | custom fusion | bytes 4100 | tf_op jit(solution)/shard_map/scatter | solution.py:178
  33.6 4.5 %gather_fusion = s32[1024]{0:T(1024)S(1)} fusion(s32[1024]{0:T(1024)S(1)} %scatter_custom_fusion, s32[1024]{0:T(1024)S(1)} %broadcast_clamp_fusion.2), kind=kCustom, calls=%fused_computation | custom fusion | bytes 12288 | tf_op jit(solution)/shard_map/gather | solution.py:189
  38.2 4.5 %gather_fusion.3 = s32[1024]{0:T(1024)S(1)} fusion(s32[1024]{0:T(1024)S(1)} %scatter_custom_fusion, s32[1024]{0:T(1024)S(1)} %broadcast_clamp_fusion), kind=kCustom, calls=%fused_computation.3 | custom fusion | bytes 12288 | tf_op jit(solution)/shard_map/gather | solution.py:189
  42.8 8.8 %gather_fusion.1 = s32[1024]{0:T(1024)} fusion(s32[1024]{0:T(1024)S(1)} %get-tuple-element.5, s32[1024]{0:T(1024)S(1)} %get-tuple-element.6), kind=kCustom, calls=%fused_computation.1 | custom fusion | bytes 12288 | tf_op jit(solution)/shard_map/gather | solution.py:189
  51.6 8.8 %gather_fusion.4 = s32[1024]{0:T(1024)} fusion(s32[1024]{0:T(1024)S(1)} %get-tuple-element.5, s32[1024]{0:T(1024)S(1)} %broadcast_clamp_fusion.1), kind=kCustom, calls=%fused_computation.4 | custom fusion | bytes 12288 | tf_op jit(solution)/shard_map/gather | solution.py:189
  60.4 39.5 %all-gather.2.cloned.1.call-done = bf16[1024,3200]{1,0:T(8,128)(2,1)} async-done(((bf16[128,3200]{1,0:T(8,128)(2,1)}), bf16[1024,3200]{1,0:T(8,128)(2,1)}) %all-gather.2.cloned.1.call-update) | async-done | bytes 6553616 | tf_op jit(solution)/shard_map/all_gather | solution.py:171
  99.9 30.5 %fusion.20.all_ref = f32[1024,3200]{1,0:T(8,128)} fusion(bf16[1024,3200]{1,0:T(8,128)(2,1)} %all-gather.2.cloned.1.call-done, bf16[3200,3200]{1,0:T(8,128)(2,1)} %param.5), kind=kOutput, calls=%fused_computation.61 | convolution fusion | flops 20971520000 | bytes 40140800 | tf_op jit(solution)/shard_map/dot_general | solution.py:188
  130.4 18.9 %shard_map.47 = f32[1024,3200]{1,0:T(8,128)} custom-call(s32[1024]{0:T(1024)} %gather_fusion.1, s32[1024]{0:T(1024)} %gather_fusion.4, f32[1024,3200]{1,0:T(8,128)} %fusion.20.all_ref), custom_call_target="tpu_custom_call" | custom-call | flops 3276800 | bytes 39321600 | tf_op jit(solution)/shard_map/pallas_call | solution.py:43
  149.3 0.0 reduce-scatter.2.cloned.1.call-update
  149.3 74.0 %reduce-scatter.2.cloned.1.call-done = f32[128,3200]{1,0:T(8,128)} async-done(((f32[1024,3200]{1,0:T(8,128)}), f32[128,3200]{1,0:T(8,128)}) %reduce-scatter.2.cloned.1.call-update) | async-done | bytes 1638416 | tf_op jit(solution)/shard_map/reduce_scatter | solution.py:190
  223.4 21.8 %shard_map.48 = bf16[64,3200]{1,0:T(8,128)(2,1)} custom-call(f32[2,64,3200]{2,1,0:T(8,128)} %bitcast.16), custom_call_target="tpu_custom_call" | custom-call | tf_op jit(solution)/shard_map/pallas_call | solution.py:143
  245.2 1.8 copy.6
  (9 shorter events, 0.1 us)
Async XLA Ops:
  6.5 17.5 %copy-start = (s32[1024]{0:T(1024)S(1)}, s32[1024]{0:T(1024)}, u32[]{:S(2)}) copy-start(s32[1024]{0:T(1024)} %param.7) | copy-start | bytes 12292
  6.5 93.4 %all-gather.2.cloned.1.call-start = ((), (), s32[]{:S(2)}) async-start(), calls=%async_computation.1 | async-start | bytes 7372800 | tf_op jit(solution)/shard_map/all_gather | solution.py:171
  24.0 199.4 %reduce-scatter.2.cloned.1.call-start = ((), (), s32[]{:S(2)}) async-start(), calls=%async_computation.2 | async-start | bytes 14745600 | tf_op jit(solution)/shard_map/reduce_scatter | solution.py:190
Sparse Core Ops, SparseCore 0:
  24.1 75.7 all-gather.1
  149.5 73.8 reduce-scatter.1

commit v9 on v8

--- a/solution.py
+++ b/solution.py
@@ -116,6 +116,8 @@
     z, xh, core, xl, y = (lax.axis_index(a) for a in ROW_AXES + COL_AXES)
     other = lax.rem(xh + 1, n_xh)
     where = (z, other, core, xl, y)
+    pieces = send_sem.shape[0]
+    rows = own_buf.shape[0] // pieces
 
     barrier = pltpu.get_barrier_semaphore()
     pl.semaphore_signal(barrier, inc=1, device_id=where, device_id_type=pl.DeviceIdType.MESH)
@@ -123,22 +125,26 @@
 
     local = pltpu.make_async_copy(part_ref.at[xh], own_buf, local_sem.at[0])
     local.start()
-    copy = pltpu.make_async_remote_copy(
-        src_ref=part_ref.at[other],
-        dst_ref=recv_buf,
-        send_sem=send_sem.at[0],
-        recv_sem=recv_sem.at[0],
-        device_id=where,
-        device_id_type=pl.DeviceIdType.MESH,
-    )
-    copy.start()
+    sends = []
+    for k in range(pieces):
+        copy = pltpu.make_async_remote_copy(
+            src_ref=part_ref.at[other, pl.ds(k * rows, rows)],
+            dst_ref=recv_buf.at[pl.ds(k * rows, rows)],
+            send_sem=send_sem.at[k],
+            recv_sem=recv_sem.at[0],
+            device_id=where,
+            device_id_type=pl.DeviceIdType.MESH,
+        )
+        copy.start()
+        sends.append(copy)
     local.wait()
-    copy.wait_send()
-    copy.wait_recv()
+    for copy in sends:
+        copy.wait_send()
+    pltpu.make_async_copy(part_ref.at[xh], recv_buf, recv_sem.at[0]).wait()
     out_ref[...] = (own_buf[...] + recv_buf[...]).astype(out_ref.dtype)
 
 
-def sum_over_pair(part):
+def sum_over_pair(part, pieces=4):
     _, rows, width = part.shape
     return pl.pallas_call(
         _pair_sum_kernel,
@@ -148,7 +154,7 @@
         scratch_shapes=[
             pltpu.VMEM((rows, width), part.dtype),
             pltpu.VMEM((rows, width), part.dtype),
-            pltpu.SemaphoreType.DMA((1,)),
+            pltpu.SemaphoreType.DMA((pieces,)),
             pltpu.SemaphoreType.DMA((1,)),
             pltpu.SemaphoreType.DMA((1,)),
         ],

time: 254 us -> 254 us (level)
  no operation moved by 1% of the time
where the time goes in v9:
time: 254 us
  waiting for transfers between devices  114 us (45%)
  Pallas kernels  58.2 us (23%)
  local copies, waits for them, and re-layouts  37.3 us (15%)
  matrix products  30.5 us (12%)
  between operations  13.5 us (5%)
    reduce_scatter x1, waiting for transfers between devices, per_device(): lax.psum_scatter(difference, ('z', 'core'), scatter_dimension=0, tiled=True)  74 us
    all_gather x1, waiting for transfers between devices, per_device(): gathered = lax.all_gather(regrouped, COL_AXES, axis=0, tiled=True)  39.5 us
    dot_general x1, matrix products, per_device(): ladder = jnp.dot(gathered, integrals, preferred_element_type=jnp.float32)  30.5 us
    pallas_call x1, Pallas kernels, sum_over_pair(): pl.pallas_call(_pair_sum_kernel, out_shape=jax.ShapeDtypeStruct((rows, wi...  21.9 us
    pallas_call x1, Pallas kernels, antisymmetrize(): pl.pallas_call(_antisym_kernel, grid_spec=pltpu.PrefetchScalarGridSpec(nu...  18.9 us
    pallas_call x1, Pallas kernels, exchange_over_row(): pl.pallas_call(_exchange_kernel, out_shape=jax.ShapeDtypeStruct(pieces.sh...  17.4 us
    gather x1, local copies, waits for them, and re-layouts, per_device(): pos_of_stored[inv[p_of_i]]  8.84 us
    gather x1, local copies, waits for them, and re-layouts, per_device(): pos_of_stored[inv[q]]  8.8 us
  transfers between devices with their start and end apart: 2, of which 2 were waited for; matrix products, arithmetic and copies ran while one was open for 14% of the time, Pallas kernels for 0%

profile of v9, /device:TPU:0, one launch (start us, length us, event | category | flops | bytes accessed | tf_op | source)
XLA Modules:
  0.0 253.9 jit_solution(13842493942551854721)
XLA Ops:
  6.5 0.0 copy-start
  6.5 0.0 all-gather.2.cloned.1.call-start
  6.5 17.4 %shard_map.46 = bf16[16,8,3200]{2,1,0:T(8,128)(2,1)} custom-call(bf16[16,8,3200]{2,1,0:T(8,128)(2,1)} %bitcast.17), custom_call_target="tpu_custom_call" | custom-call | tf_op jit(solution)/shard_map/pallas_call | solution.py:100
  24.0 0.0 all-gather.2.cloned.1.call-update
  24.0 0.0 reduce-scatter.2.cloned.1.call-start
  24.1 0.0 copy-done
  24.1 4.5 %gather_fusion.2 = s32[1024]{0:T(1024)S(1)} fusion(s32[1024]{0:T(1024)S(1)} %copy-done, s32[1024]{0:T(1024)S(1)} %broadcast_clamp_fusion.2), kind=kCustom, calls=%fused_computation.2 | custom fusion | bytes 12288 | tf_op jit(solution)/shard_map/gather | solution.py:192
  28.6 0.7 compare_select_fusion.6
  29.3 4.3 %scatter_custom_fusion = s32[1024]{0:T(1024)S(1)} fusion(s32[1024]{0:T(1024)S(1)} %compare_select_fusion.6, s32[1024]{0:T(1024)S(1)} %iota.15, s32[]{:T(128)} %constant.93.clone.1), kind=kCustom, calls=%fused_computation.59 | custom fusion | bytes 4100 | tf_op jit(solution)/shard_map/scatter | solution.py:184
  33.6 4.5 %gather_fusion = s32[1024]{0:T(1024)S(1)} fusion(s32[1024]{0:T(1024)S(1)} %scatter_custom_fusion, s32[1024]{0:T(1024)S(1)} %broadcast_clamp_fusion.2), kind=kCustom, calls=%fused_computation | custom fusion | bytes 12288 | tf_op jit(solution)/shard_map/gather | solution.py:195
  38.2 4.5 %gather_fusion.3 = s32[1024]{0:T(1024)S(1)} fusion(s32[1024]{0:T(1024)S(1)} %scatter_custom_fusion, s32[1024]{0:T(1024)S(1)} %broadcast_clamp_fusion), kind=kCustom, calls=%fused_computation.3 | custom fusion | bytes 12288 | tf_op jit(solution)/shard_map/gather | solution.py:195
  42.8 8.8 %gather_fusion.1 = s32[1024]{0:T(1024)} fusion(s32[1024]{0:T(1024)S(1)} %get-tuple-element.5, s32[1024]{0:T(1024)S(1)} %get-tuple-element.6), kind=kCustom, calls=%fused_computation.1 | custom fusion | bytes 12288 | tf_op jit(solution)/shard_map/gather | solution.py:195
  51.6 8.8 %gather_fusion.4 = s32[1024]{0:T(1024)} fusion(s32[1024]{0:T(1024)S(1)} %get-tuple-element.5, s32[1024]{0:T(1024)S(1)} %broadcast_clamp_fusion.1), kind=kCustom, calls=%fused_computation.4 | custom fusion | bytes 12288 | tf_op jit(solution)/shard_map/gather | solution.py:195
  60.4 39.5 %all-gather.2.cloned.1.call-done = bf16[1024,3200]{1,0:T(8,128)(2,1)} async-done(((bf16[128,3200]{1,0:T(8,128)(2,1)}), bf16[1024,3200]{1,0:T(8,128)(2,1)}) %all-gather.2.cloned.1.call-update) | async-done | bytes 6553616 | tf_op jit(solution)/shard_map/all_gather | solution.py:177
  99.9 30.5 %fusion.20.all_ref = f32[1024,3200]{1,0:T(8,128)} fusion(bf16[1024,3200]{1,0:T(8,128)(2,1)} %all-gather.2.cloned.1.call-done, bf16[3200,3200]{1,0:T(8,128)(2,1)} %param.5), kind=kOutput, calls=%fused_computation.61 | convolution fusion | flops 20971520000 | bytes 40140800 | tf_op jit(solution)/shard_map/dot_general | solution.py:194
  130.4 18.9 %shard_map.47 = f32[1024,3200]{1,0:T(8,128)} custom-call(s32[1024]{0:T(1024)} %gather_fusion.1, s32[1024]{0:T(1024)} %gather_fusion.4, f32[1024,3200]{1,0:T(8,128)} %fusion.20.all_ref), custom_call_target="tpu_custom_call" | custom-call | flops 3276800 | bytes 39321600 | tf_op jit(solution)/shard_map/pallas_call | solution.py:43
  149.3 0.0 reduce-scatter.2.cloned.1.call-update
  149.3 74.0 %reduce-scatter.2.cloned.1.call-done = f32[128,3200]{1,0:T(8,128)} async-done(((f32[1024,3200]{1,0:T(8,128)}), f32[128,3200]{1,0:T(8,128)}) %reduce-scatter.2.cloned.1.call-update) | async-done | bytes 1638416 | tf_op jit(solution)/shard_map/reduce_scatter | solution.py:196
  223.4 21.9 %shard_map.48 = bf16[64,3200]{1,0:T(8,128)(2,1)} custom-call(f32[2,64,3200]{2,1,0:T(8,128)} %bitcast.16), custom_call_target="tpu_custom_call" | custom-call | tf_op jit(solution)/shard_map/pallas_call | solution.py:149
  245.2 1.8 copy.6
  (9 shorter events, 0.1 us)
Async XLA Ops:
  6.5 17.5 %copy-start = (s32[1024]{0:T(1024)S(1)}, s32[1024]{0:T(1024)}, u32[]{:S(2)}) copy-start(s32[1024]{0:T(1024)} %param.7) | copy-start | bytes 12292
  6.5 93.4 %all-gather.2.cloned.1.call-start = ((), (), s32[]{:S(2)}) async-start(), calls=%async_computation.1 | async-start | bytes 7372800 | tf_op jit(solution)/shard_map/all_gather | solution.py:177
  24.0 199.4 %reduce-scatter.2.cloned.1.call-start = ((), (), s32[]{:S(2)}) async-start(), calls=%async_computation.2 | async-start | bytes 14745600 | tf_op jit(solution)/shard_map/reduce_scatter | solution.py:196
Sparse Core Ops, SparseCore 0:
  24.1 75.7 all-gather.1
  149.5 73.8 reduce-scatter.1

commit v10 on v9

--- a/solution.py
+++ b/solution.py
@@ -38,7 +38,7 @@
     out_ref[...] = own_buf[slot] - partner_buf[slot]
 
 
-def antisymmetrize(ladder, own_rows, partner_rows, rows=64):
+def antisymmetrize(ladder, own_rows, partner_rows, rows=128):
     total, width = ladder.shape
     return pl.pallas_call(
         _antisym_kernel,

time: 254 us -> 254 us (level)
  no operation moved by 1% of the time
where the time goes in v10:
time: 254 us
  waiting for transfers between devices  114 us (45%)
  Pallas kernels  58 us (23%)
  local copies, waits for them, and re-layouts  37.3 us (15%)
  matrix products  30.5 us (12%)
  between operations  13.5 us (5%)
    reduce_scatter x1, waiting for transfers between devices, per_device(): lax.psum_scatter(difference, ('z', 'core'), scatter_dimension=0, tiled=True)  74 us
    all_gather x1, waiting for transfers between devices, per_device(): gathered = lax.all_gather(regrouped, COL_AXES, axis=0, tiled=True)  39.5 us
    dot_general x1, matrix products, per_device(): ladder = jnp.dot(gathered, integrals, preferred_element_type=jnp.float32)  30.5 us
    pallas_call x1, Pallas kernels, sum_over_pair(): pl.pallas_call(_pair_sum_kernel, out_shape=jax.ShapeDtypeStruct((rows, wi...  21.9 us
    pallas_call x1, Pallas kernels, antisymmetrize(): pl.pallas_call(_antisym_kernel, grid_spec=pltpu.PrefetchScalarGridSpec(nu...  18.7 us
    pallas_call x1, Pallas kernels, exchange_over_row(): pl.pallas_call(_exchange_kernel, out_shape=jax.ShapeDtypeStruct(pieces.sh...  17.4 us
    gather x1, local copies, waits for them, and re-layouts, per_device(): pos_of_stored[inv[p_of_i]]  8.84 us
    gather x1, local copies, waits for them, and re-layouts, per_device(): pos_of_stored[inv[q]]  8.8 us
  transfers between devices with their start and end apart: 2, of which 2 were waited for; matrix products, arithmetic and copies ran while one was open for 14% of the time, Pallas kernels for 0%

profile of v10, /device:TPU:0, one launch (start us, length us, event | category | flops | bytes accessed | tf_op | source)
XLA Modules:
  0.0 253.7 jit_solution(247447060530445114)
XLA Ops:
  6.5 0.0 copy-start
  6.5 0.0 all-gather.2.cloned.1.call-start
  6.5 17.4 %shard_map.46 = bf16[16,8,3200]{2,1,0:T(8,128)(2,1)} custom-call(bf16[16,8,3200]{2,1,0:T(8,128)(2,1)} %bitcast.17), custom_call_target="tpu_custom_call" | custom-call | tf_op jit(solution)/shard_map/pallas_call | solution.py:100
  24.0 0.0 all-gather.2.cloned.1.call-update
  24.0 0.0 reduce-scatter.2.cloned.1.call-start
  24.1 0.0 copy-done
  24.1 4.5 %gather_fusion.2 = s32[1024]{0:T(1024)S(1)} fusion(s32[1024]{0:T(1024)S(1)} %copy-done, s32[1024]{0:T(1024)S(1)} %broadcast_clamp_fusion.2), kind=kCustom, calls=%fused_computation.2 | custom fusion | bytes 12288 | tf_op jit(solution)/shard_map/gather | solution.py:192
  28.6 0.7 compare_select_fusion.6
  29.3 4.3 %scatter_custom_fusion = s32[1024]{0:T(1024)S(1)} fusion(s32[1024]{0:T(1024)S(1)} %compare_select_fusion.6, s32[1024]{0:T(1024)S(1)} %iota.15, s32[]{:T(128)} %constant.93.clone.1), kind=kCustom, calls=%fused_computation.59 | custom fusion | bytes 4100 | tf_op jit(solution)/shard_map/scatter | solution.py:184
  33.6 4.5 %gather_fusion = s32[1024]{0:T(1024)S(1)} fusion(s32[1024]{0:T(1024)S(1)} %scatter_custom_fusion, s32[1024]{0:T(1024)S(1)} %broadcast_clamp_fusion.2), kind=kCustom, calls=%fused_computation | custom fusion | bytes 12288 | tf_op jit(solution)/shard_map/gather | solution.py:195
  38.2 4.5 %gather_fusion.3 = s32[1024]{0:T(1024)S(1)} fusion(s32[1024]{0:T(1024)S(1)} %scatter_custom_fusion, s32[1024]{0:T(1024)S(1)} %broadcast_clamp_fusion), kind=kCustom, calls=%fused_computation.3 | custom fusion | bytes 12288 | tf_op jit(solution)/shard_map/gather | solution.py:195
  42.8 8.8 %gather_fusion.1 = s32[1024]{0:T(1024)} fusion(s32[1024]{0:T(1024)S(1)} %get-tuple-element.5, s32[1024]{0:T(1024)S(1)} %get-tuple-element.6), kind=kCustom, calls=%fused_computation.1 | custom fusion | bytes 12288 | tf_op jit(solution)/shard_map/gather | solution.py:195
  51.6 8.8 %gather_fusion.4 = s32[1024]{0:T(1024)} fusion(s32[1024]{0:T(1024)S(1)} %get-tuple-element.5, s32[1024]{0:T(1024)S(1)} %broadcast_clamp_fusion.1), kind=kCustom, calls=%fused_computation.4 | custom fusion | bytes 12288 | tf_op jit(solution)/shard_map/gather | solution.py:195
  60.4 39.5 %all-gather.2.cloned.1.call-done = bf16[1024,3200]{1,0:T(8,128)(2,1)} async-done(((bf16[128,3200]{1,0:T(8,128)(2,1)}), bf16[1024,3200]{1,0:T(8,128)(2,1)}) %all-gather.2.cloned.1.call-update) | async-done | bytes 6553616 | tf_op jit(solution)/shard_map/all_gather | solution.py:177
  99.9 30.5 %fusion.20.all_ref = f32[1024,3200]{1,0:T(8,128)} fusion(bf16[1024,3200]{1,0:T(8,128)(2,1)} %all-gather.2.cloned.1.call-done, bf16[3200,3200]{1,0:T(8,128)(2,1)} %param.5), kind=kOutput, calls=%fused_computation.61 | convolution fusion | flops 20971520000 | bytes 40140800 | tf_op jit(solution)/shard_map/dot_general | solution.py:194
  130.4 18.7 %shard_map.47 = f32[1024,3200]{1,0:T(8,128)} custom-call(s32[1024]{0:T(1024)} %gather_fusion.1, s32[1024]{0:T(1024)} %gather_fusion.4, f32[1024,3200]{1,0:T(8,128)} %fusion.20.all_ref), custom_call_target="tpu_custom_call" | custom-call | flops 3276800 | bytes 39321600 | tf_op jit(solution)/shard_map/pallas_call | solution.py:43
  149.1 0.0 reduce-scatter.2.cloned.1.call-update
  149.2 74.0 %reduce-scatter.2.cloned.1.call-done = f32[128,3200]{1,0:T(8,128)} async-done(((f32[1024,3200]{1,0:T(8,128)}), f32[128,3200]{1,0:T(8,128)}) %reduce-scatter.2.cloned.1.call-update) | async-done | bytes 1638416 | tf_op jit(solution)/shard_map/reduce_scatter | solution.py:196
  223.2 21.9 %shard_map.48 = bf16[64,3200]{1,0:T(8,128)(2,1)} custom-call(f32[2,64,3200]{2,1,0:T(8,128)} %bitcast.16), custom_call_target="tpu_custom_call" | custom-call | tf_op jit(solution)/shard_map/pallas_call | solution.py:149
  245.1 1.8 copy.6
  (9 shorter events, 0.1 us)
Async XLA Ops:
  6.5 17.5 %copy-start = (s32[1024]{0:T(1024)S(1)}, s32[1024]{0:T(1024)}, u32[]{:S(2)}) copy-start(s32[1024]{0:T(1024)} %param.7) | copy-start | bytes 12292
  6.5 93.4 %all-gather.2.cloned.1.call-start = ((), (), s32[]{:S(2)}) async-start(), calls=%async_computation.1 | async-start | bytes 7372800 | tf_op jit(solution)/shard_map/all_gather | solution.py:177
  24.0 199.2 %reduce-scatter.2.cloned.1.call-start = ((), (), s32[]{:S(2)}) async-start(), calls=%async_computation.2 | async-start | bytes 14745600 | tf_op jit(solution)/shard_map/reduce_scatter | solution.py:196
Sparse Core Ops, SparseCore 0:
  24.1 75.7 all-gather.1
  149.3 73.8 reduce-scatter.1

commit v11 on v10

--- a/solution.py
+++ b/solution.py
@@ -59,56 +59,79 @@
     )(own_rows, partner_rows, ladder)
 
 
-def _exchange_kernel(src_ref, out_ref, send_sem, recv_sem, local_sem):
-    n_z, n_xh, n_core = (lax.axis_size(a) for a in ROW_AXES)
-    n = n_z * n_xh * n_core
+def _spread_kernel(src_ref, out_ref, send_sem, recv_sem, local_sem):
+    n_z, n_xh, n_core, n_xl, n_y = (lax.axis_size(a) for a in ROW_AXES + COL_AXES)
+    n_col = n_xl * n_y
+    n = n_z * n_xh * n_core * n_col
     z, xh, core, xl, y = (lax.axis_index(a) for a in ROW_AXES + COL_AXES)
-    me = (z * n_xh + xh) * n_core + core
+    me = ((z * n_xh + xh) * n_core + core) * n_col + xl * n_y + y
 
     def peer(k):
         t = lax.rem(me + k, n)
-        return t, (t // (n_xh * n_core), lax.rem(t // n_core, n_xh), lax.rem(t, n_core), xl, y)
+        r, c = t // n_col, lax.rem(t, n_col)
+        return r, (r // (n_xh * n_core), lax.rem(r // n_core, n_xh), lax.rem(r, n_core), c // n_y, lax.rem(c, n_y))
 
     barrier = pltpu.get_barrier_semaphore()
-    for k in range(1, n):
+
+    def signal(k, carry):
         pl.semaphore_signal(barrier, inc=1, device_id=peer(k)[1], device_id_type=pl.DeviceIdType.MESH)
+        return carry
+
+    lax.fori_loop(1, n, signal, 0)
     pl.semaphore_wait(barrier, n - 1)
 
-    local = pltpu.make_async_copy(src_ref.at[me], out_ref.at[me], local_sem.at[0])
+    local = pltpu.make_async_copy(src_ref.at[me // n_col], out_ref.at[me], local_sem.at[0])
     local.start()
-    sends = []
-    for k in range(1, n):
-        t, where = peer(k)
-        copy = pltpu.make_async_remote_copy(
-            src_ref=src_ref.at[t],
+
+    def send(k):
+        r, where = peer(k)
+        return pltpu.make_async_remote_copy(
+            src_ref=src_ref.at[r],
             dst_ref=out_ref.at[me],
             send_sem=send_sem.at[k - 1],
             recv_sem=recv_sem.at[0],
             device_id=where,
             device_id_type=pl.DeviceIdType.MESH,
         )
-        copy.start()
-        sends.append(copy)
-    for copy in sends:
-        copy.wait_send()
-    pltpu.make_async_copy(src_ref.at[pl.ds(0, n - 1)], out_ref.at[pl.ds(0, n - 1)], recv_sem.at[0]).wait()
+
+    def start(k, carry):
+        send(k).start()
+        return carry
+
+    def finish(k, carry):
+        send(k).wait_send()
+        return carry
+
+    lax.fori_loop(1, n, start, 0)
+    lax.fori_loop(1, n, finish, 0)
+    pltpu.make_async_copy(out_ref.at[pl.ds(0, n - 1)], out_ref.at[pl.ds(0, n - 1)], recv_sem.at[0]).wait()
     local.wait()
 
 
-def exchange_over_row(pieces):
-    n = pieces.shape[0]
+def spread(pieces, devices):
+    _, rows, width = pieces.shape
     return pl.pallas_call(
-        _exchange_kernel,
-        out_shape=jax.ShapeDtypeStruct(pieces.shape, pieces.dtype),
+        _spread_kernel,
+        out_shape=jax.ShapeDtypeStruct((devices, rows, width), pieces.dtype),
         in_specs=[pl.BlockSpec(memory_space=pl.ANY)],
         out_specs=pl.BlockSpec(memory_space=pl.ANY),
         scratch_shapes=[
-            pltpu.SemaphoreType.DMA((n - 1,)),
+            pltpu.SemaphoreType.DMA((devices - 1,)),
             pltpu.SemaphoreType.DMA((1,)),
             pltpu.SemaphoreType.DMA((1,)),
         ],
         compiler_params=pltpu.CompilerParams(collective_id=0, has_side_effects=True),
     )(pieces)
+
+
+def _lookup(table, index):
+    hits = index[:, None] == jnp.arange(table.shape[0], dtype=jnp.int32)[None, :]
+    return jnp.sum(jnp.where(hits, table[None, :], 0), axis=1)
+
+
+def _inverse(perm):
+    hits = perm[None, :] == jnp.arange(perm.shape[0], dtype=jnp.int32)[:, None]
+    return jnp.sum(jnp.where(hits, jnp.arange(perm.shape[0], dtype=jnp.int32)[None, :], 0), axis=1)
 
 
 def _pair_sum_kernel(part_ref, out_ref, own_buf, recv_buf, send_sem, recv_sem, local_sem):
@@ -173,15 +196,8 @@
     block = total // n_row
 
     pieces = stored.reshape(local_rows, n_row, stored.shape[1] // n_row).transpose(1, 0, 2)
-    regrouped = exchange_over_row(pieces).reshape(n_row * local_rows, pieces.shape[2])
-    gathered = lax.all_gather(regrouped, COL_AXES, axis=0, tiled=True)
-
-    s = jnp.arange(total, dtype=jnp.int32)
-    s_row = s // (local_rows * n_col)
-    s_col = (s // local_rows) % n_col
-    s_off = s % local_rows
-    pos_of_stored = s_col * (n_row * local_rows) + s_row * local_rows + s_off
-    inv = jnp.zeros((total,), jnp.int32).at[layout].set(s)
+    gathered = spread(pieces, n_row * n_col).reshape(total, pieces.shape[2])
+    inv = _inverse(layout)
 
     i = jnp.arange(total, dtype=jnp.int32)
     g = i // block
@@ -189,10 +205,10 @@
     core = (g // n_xh) % n_core
     z = g // (n_xh * n_core)
     p_of_i = ((z * n_xh + xh) * n_core + core) * block + (i % block)
-    q = partner[p_of_i]
+    q = _lookup(partner, p_of_i)
 
     ladder = jnp.dot(gathered, integrals, preferred_element_type=jnp.float32)
-    difference = antisymmetrize(ladder, pos_of_stored[inv[p_of_i]], pos_of_stored[inv[q]])
+    difference = antisymmetrize(ladder, _lookup(inv, p_of_i), _lookup(inv, q))
     part = lax.psum_scatter(difference, ("z", "core"), scatter_dimension=0, tiled=True)
     return sum_over_pair(part.reshape(n_xh, block, part.shape[1]))
 

time: 254 us -> 292 us (1.15)
  Pallas kernels: 58 us -> 158 us
  local copies, waits for them, and re-layouts: 37.3 us -> 1.79 us
  waiting for transfers between devices: 114 us -> 84.6 us
    pallas_call x1, Pallas kernels: 17.4 us -> 118 us  [spread(): pl.pallas_call(_spread_kernel, out_shape=jax.ShapeDtypeStruct((devices, r...]
    all_gather x1 -> x0, waiting for transfers between devices: 39.5 us -> none  [per_device(): gathered = lax.all_gather(regrouped, COL_AXES, axis=0, tiled=True)]
    gather x5 -> x0, local copies, waits for them, and re-layouts: 31.2 us -> none  [the longest x1 8.84 us: per_device(): pos_of_stored[inv[p_of_i]]]
    reduce_scatter x1, waiting for transfers between devices: 74 us -> 84.6 us  [per_device(): lax.psum_scatter(difference, ('z', 'core'), scatter_dimension=0, tiled=True)]
    scatter x1 -> x0, local copies, waits for them, and re-layouts: 4.31 us -> none  [per_device(): inv = jnp.zeros((total,), jnp.int32).at[layout].set(s)]
    reduce_sum x0 -> x2, other arithmetic: none -> 3.45 us  [_lookup(): return jnp.sum(jnp.where(hits, table[None, :], 0), axis=1)]
  transfers between devices with their start and end apart: 2 -> 1, of which waited for: 2 -> 1; matrix products, arithmetic and copies ran while one was open for 14% -> 0% of each run, Pallas kernels for 0% -> 0%
where the time goes in v11:
time: 292 us
  Pallas kernels  158 us (54%)
  waiting for transfers between devices  84.6 us (29%)
  matrix products  30.5 us (10%)
  between operations  13.4 us (5%)
  other arithmetic  3.46 us (1%)
    pallas_call x1, Pallas kernels, spread(): pl.pallas_call(_spread_kernel, out_shape=jax.ShapeDtypeStruct((devices, r...  118 us
    reduce_scatter x1, waiting for transfers between devices, per_device(): lax.psum_scatter(difference, ('z', 'core'), scatter_dimension=0, tiled=True)  84.6 us
    dot_general x1, matrix products, per_device(): ladder = jnp.dot(gathered, integrals, preferred_element_type=jnp.float32)  30.5 us
    pallas_call x1, Pallas kernels, sum_over_pair(): pl.pallas_call(_pair_sum_kernel, out_shape=jax.ShapeDtypeStruct((rows, wi...  21.9 us
    pallas_call x1, Pallas kernels, antisymmetrize(): pl.pallas_call(_antisym_kernel, grid_spec=pltpu.PrefetchScalarGridSpec(nu...  18.7 us
  transfers between devices with their start and end apart: 1, of which 1 were waited for; matrix products, arithmetic and copies ran while one was open for 0% of the time, Pallas kernels for 0%

profile of v11, /device:TPU:0, one launch (start us, length us, event | category | flops | bytes accessed | tf_op | source)
XLA Modules:
  0.0 292.0 jit_solution(9649593417276026307)
XLA Ops:
  6.5 0.0 copy-start
  6.5 0.0 copy-start.1
  6.5 0.0 reduce-scatter.2.cloned.1.call-start
  6.6 117.7 %shard_map.46 = bf16[128,8,3200]{2,1,0:T(8,128)(2,1)} custom-call(bf16[16,8,3200]{2,1,0:T(8,128)(2,1)} %bitcast.9), custom_call_target="tpu_custom_call" | custom-call | tf_op jit(solution)/shard_map/pallas_call | solution.py:113
  124.2 0.0 copy-done
  124.2 0.0 copy-done.1
  124.2 1.3 select_reduce_fusion.1
  125.6 2.1 select_reduce_fusion
  127.7 30.5 %fusion.all_ref = f32[1024,3200]{1,0:T(8,128)} fusion(bf16[3200,3200]{1,0:T(8,128)(2,1)} %param.5, bf16[128,8,3200]{2,1,0:T(8,128)(2,1)} %shard_map.46), kind=kOutput, calls=%fused_computation | convolution fusion | flops 20971520000 | bytes 40140800 | tf_op jit(solution)/shard_map/dot_general | solution.py:210
  158.2 18.7 %shard_map.47 = f32[1024,3200]{1,0:T(8,128)} custom-call(s32[1024]{0:T(1024)} %get-tuple-element.6.own_idx, s32[1024]{0:T(1024)} %get-tuple-element.5.partner_idx, f32[1024,3200]{1,0:T(8,128)} %fusion.all_ref), custom_call_target="tpu_custom_call" | custom-call | flops 3276800 | bytes 39321600 | tf_op jit(solution)/shard_map/pallas_call | solution.py:43
  176.9 0.0 reduce-scatter.2.cloned.1.call-update
  177.0 84.6 %reduce-scatter.2.cloned.1.call-done = f32[128,3200]{1,0:T(8,128)} async-done(((f32[1024,3200]{1,0:T(8,128)}), f32[128,3200]{1,0:T(8,128)}) %reduce-scatter.2.cloned.1.call-update) | async-done | bytes 1638416 | tf_op jit(solution)/shard_map/reduce_scatter | solution.py:212
  261.5 21.9 %shard_map.48 = bf16[64,3200]{1,0:T(8,128)(2,1)} custom-call(f32[2,64,3200]{2,1,0:T(8,128)} %bitcast.8), custom_call_target="tpu_custom_call" | custom-call | tf_op jit(solution)/shard_map/pallas_call | solution.py:172
  283.4 1.8 copy.6
  (1 shorter events, 0.0 us)
Async XLA Ops:
  6.5 117.7 %copy-start = (s32[1024]{0:T(1024)S(1)}, s32[1024]{0:T(1024)}, u32[]{:S(2)}) copy-start(s32[1024]{0:T(1024)} %param.7) | copy-start | bytes 12292
  6.5 117.7 %copy-start.1 = (s32[1024]{0:T(1024)S(1)}, s32[1024]{0:T(1024)}, u32[]{:S(2)}) copy-start(s32[1024]{0:T(1024)} %param.6) | copy-start | bytes 12292
  6.5 255.0 %reduce-scatter.2.cloned.1.call-start = ((), (), s32[]{:S(2)}) async-start(), calls=%async_computation.1 | async-start | bytes 14745600 | tf_op jit(solution)/shard_map/reduce_scatter | solution.py:212
Sparse Core Ops, SparseCore 0:
  177.1 84.3 reduce-scatter.1

commit v12 on v10

--- a/solution.py
+++ b/solution.py
@@ -109,6 +109,66 @@
         ],
         compiler_params=pltpu.CompilerParams(collective_id=0, has_side_effects=True),
     )(pieces)
+
+
+def _col_gather_kernel(src_ref, out_ref, send_sem, recv_sem, local_sem):
+    n_xl, n_y = (lax.axis_size(a) for a in COL_AXES)
+    n = n_xl * n_y
+    z, xh, core, xl, y = (lax.axis_index(a) for a in ROW_AXES + COL_AXES)
+    me = xl * n_y + y
+
+    def peer(k):
+        t = lax.rem(me + k, n)
+        return (z, xh, core, t // n_y, lax.rem(t, n_y))
+
+    barrier = pltpu.get_barrier_semaphore()
+    for k in range(1, n):
+        pl.semaphore_signal(barrier, inc=1, device_id=peer(k), device_id_type=pl.DeviceIdType.MESH)
+    pl.semaphore_wait(barrier, n - 1)
+
+    local = pltpu.make_async_copy(src_ref, out_ref.at[me], local_sem.at[0])
+    local.start()
+    sends = []
+    for k in range(1, n):
+        copy = pltpu.make_async_remote_copy(
+            src_ref=src_ref,
+            dst_ref=out_ref.at[me],
+            send_sem=send_sem.at[k - 1],
+            recv_sem=recv_sem.at[0],
+            device_id=peer(k),
+            device_id_type=pl.DeviceIdType.MESH,
+        )
+        copy.start()
+        sends.append(copy)
+    for copy in sends:
+        copy.wait_send()
+    pltpu.make_async_copy(out_ref.at[pl.ds(0, n - 1)], out_ref.at[pl.ds(0, n - 1)], recv_sem.at[0]).wait()
+    local.wait()
+
+
+def gather_over_col(block, n):
+    return pl.pallas_call(
+        _col_gather_kernel,
+        out_shape=jax.ShapeDtypeStruct((n,) + block.shape, block.dtype),
+        in_specs=[pl.BlockSpec(memory_space=pl.ANY)],
+        out_specs=pl.BlockSpec(memory_space=pl.ANY),
+        scratch_shapes=[
+            pltpu.SemaphoreType.DMA((n - 1,)),
+            pltpu.SemaphoreType.DMA((1,)),
+            pltpu.SemaphoreType.DMA((1,)),
+        ],
+        compiler_params=pltpu.CompilerParams(collective_id=2, has_side_effects=True),
+    )(block)
+
+
+def _lookup(table, index):
+    hits = index[:, None] == jnp.arange(table.shape[0], dtype=jnp.int32)[None, :]
+    return jnp.sum(jnp.where(hits, table[None, :], 0), axis=1)
+
+
+def _inverse(perm):
+    hits = perm[None, :] == jnp.arange(perm.shape[0], dtype=jnp.int32)[:, None]
+    return jnp.sum(jnp.where(hits, jnp.arange(perm.shape[0], dtype=jnp.int32)[None, :], 0), axis=1)
 
 
 def _pair_sum_kernel(part_ref, out_ref, own_buf, recv_buf, send_sem, recv_sem, local_sem):
@@ -174,14 +234,14 @@
 
     pieces = stored.reshape(local_rows, n_row, stored.shape[1] // n_row).transpose(1, 0, 2)
     regrouped = exchange_over_row(pieces).reshape(n_row * local_rows, pieces.shape[2])
-    gathered = lax.all_gather(regrouped, COL_AXES, axis=0, tiled=True)
+    gathered = gather_over_col(regrouped, n_col).reshape(total, regrouped.shape[1])
 
     s = jnp.arange(total, dtype=jnp.int32)
     s_row = s // (local_rows * n_col)
     s_col = (s // local_rows) % n_col
     s_off = s % local_rows
     pos_of_stored = s_col * (n_row * local_rows) + s_row * local_rows + s_off
-    inv = jnp.zeros((total,), jnp.int32).at[layout].set(s)
+    inv = _inverse(layout)
 
     i = jnp.arange(total, dtype=jnp.int32)
     g = i // block
@@ -189,10 +249,10 @@
     core = (g // n_xh) % n_core
     z = g // (n_xh * n_core)
     p_of_i = ((z * n_xh + xh) * n_core + core) * block + (i % block)
-    q = partner[p_of_i]
+    q = _lookup(partner, p_of_i)
 
     ladder = jnp.dot(gathered, integrals, preferred_element_type=jnp.float32)
-    difference = antisymmetrize(ladder, pos_of_stored[inv[p_of_i]], pos_of_stored[inv[q]])
+    difference = antisymmetrize(ladder, _lookup(pos_of_stored, _lookup(inv, p_of_i)), _lookup(pos_of_stored, _lookup(inv, q)))
     part = lax.psum_scatter(difference, ("z", "core"), scatter_dimension=0, tiled=True)
     return sum_over_pair(part.reshape(n_xh, block, part.shape[1]))
 

time: 254 us -> 291 us (1.15)
  Pallas kernels: 58 us -> 158 us
  local copies, waits for them, and re-layouts: 37.3 us -> 1.79 us
  waiting for transfers between devices: 114 us -> 81.8 us
  other arithmetic: 0.77 us -> 4.99 us
    pallas_call x0 -> x1, Pallas kernels: none -> 100 us  [gather_over_col(): pl.pallas_call(_col_gather_kernel, out_shape=jax.ShapeDtypeStruct((n,) +...]
    all_gather x1 -> x0, waiting for transfers between devices: 39.5 us -> none  [per_device(): gathered = lax.all_gather(regrouped, COL_AXES, axis=0, tiled=True)]
    gather x5 -> x0, local copies, waits for them, and re-layouts: 31.2 us -> none  [the longest x1 8.84 us: per_device(): pos_of_stored[inv[p_of_i]]]
    reduce_scatter x1, waiting for transfers between devices: 74 us -> 81.8 us  [per_device(): lax.psum_scatter(difference, ('z', 'core'), scatter_dimension=0, tiled=True)]
    reduce_sum x0 -> x3, other arithmetic: none -> 4.97 us  [_lookup(): return jnp.sum(jnp.where(hits, table[None, :], 0), axis=1)]
    scatter x1 -> x0, local copies, waits for them, and re-layouts: 4.31 us -> none  [per_device(): inv = jnp.zeros((total,), jnp.int32).at[layout].set(s)]
  transfers between devices with their start and end apart: 2 -> 1, of which waited for: 2 -> 1; matrix products, arithmetic and copies ran while one was open for 14% -> 0% of each run, Pallas kernels for 0% -> 0%
where the time goes in v12:
time: 291 us
  Pallas kernels  158 us (54%)
  waiting for transfers between devices  81.8 us (28%)
  matrix products  30.5 us (10%)
  between operations  13.5 us (5%)
  other arithmetic  4.99 us (2%)
    pallas_call x1, Pallas kernels, gather_over_col(): pl.pallas_call(_col_gather_kernel, out_shape=jax.ShapeDtypeStruct((n,) +...  100 us
    reduce_scatter x1, waiting for transfers between devices, per_device(): lax.psum_scatter(difference, ('z', 'core'), scatter_dimension=0, tiled=True)  81.8 us
    dot_general x1, matrix products, per_device(): ladder = jnp.dot(gathered, integrals, preferred_element_type=jnp.float32)  30.5 us
    pallas_call x1, Pallas kernels, sum_over_pair(): pl.pallas_call(_pair_sum_kernel, out_shape=jax.ShapeDtypeStruct((rows, wi...  21.9 us
    pallas_call x1, Pallas kernels, antisymmetrize(): pl.pallas_call(_antisym_kernel, grid_spec=pltpu.PrefetchScalarGridSpec(nu...  18.7 us
    pallas_call x1, Pallas kernels, exchange_over_row(): pl.pallas_call(_exchange_kernel, out_shape=jax.ShapeDtypeStruct(pieces.sh...  17.6 us
  transfers between devices with their start and end apart: 1, of which 1 were waited for; matrix products, arithmetic and copies ran while one was open for 0% of the time, Pallas kernels for 0%

profile of v12, /device:TPU:0, one launch (start us, length us, event | category | flops | bytes accessed | tf_op | source)
XLA Modules:
  0.0 291.0 jit_solution(18314291508182012316)
XLA Ops:
  6.5 0.0 reduce-scatter.2.cloned.1.call-start
  6.6 0.0 copy-start
  6.6 0.0 copy-start.1
  6.6 17.6 %shard_map.46 = bf16[16,8,3200]{2,1,0:T(8,128)(2,1)} custom-call(bf16[16,8,3200]{2,1,0:T(8,128)(2,1)} %bitcast.11), custom_call_target="tpu_custom_call" | custom-call | tf_op jit(solution)/shard_map/pallas_call | solution.py:100
  24.2 100.2 %shard_map.47 = bf16[8,128,3200]{2,1,0:T(8,128)(2,1)} custom-call(bf16[128,3200]{1,0:T(8,128)(2,1)} %bitcast.9), custom_call_target="tpu_custom_call" | custom-call | tf_op jit(solution)/shard_map/pallas_call | solution.py:150
  124.4 0.0 copy-done
  124.4 0.0 copy-done.1
  124.5 1.3 select_reduce_fusion.2
  125.8 1.5 select_reduce_fusion.1
  127.3 30.5 %fusion.28.all_ref = f32[1024,3200]{1,0:T(8,128)} fusion(bf16[1024,3200]{1,0:T(8,128)(2,1)} %bitcast.8, bf16[3200,3200]{1,0:T(8,128)(2,1)} %param.5), kind=kOutput, calls=%fused_computation.61 | convolution fusion | flops 20971520000 | bytes 40140800 | tf_op jit(solution)/shard_map/dot_general | solution.py:254
  157.8 2.1 select_reduce_fusion
  160.0 18.7 %shard_map.48 = f32[1024,3200]{1,0:T(8,128)} custom-call(s32[1024]{0:T(1024)} %get-tuple-element.6.own_idx, s32[1024]{0:T(1024)} %get-tuple-element.5.partner_idx, f32[1024,3200]{1,0:T(8,128)} %fusion.28.all_ref), custom_call_target="tpu_custom_call" | custom-call | flops 3276800 | bytes 39321600 | tf_op jit(solution)/shard_map/pallas_call | solution.py:43
  178.7 0.0 reduce-scatter.2.cloned.1.call-update
  178.7 81.8 %reduce-scatter.2.cloned.1.call-done = f32[128,3200]{1,0:T(8,128)} async-done(((f32[1024,3200]{1,0:T(8,128)}), f32[128,3200]{1,0:T(8,128)}) %reduce-scatter.2.cloned.1.call-update) | async-done | bytes 1638416 | tf_op jit(solution)/shard_map/reduce_scatter | solution.py:256
  260.5 21.9 %shard_map.49 = bf16[64,3200]{1,0:T(8,128)(2,1)} custom-call(f32[2,64,3200]{2,1,0:T(8,128)} %bitcast.10), custom_call_target="tpu_custom_call" | custom-call | tf_op jit(solution)/shard_map/pallas_call | solution.py:209
  282.4 1.8 copy.6
  (2 shorter events, 0.0 us)
Async XLA Ops:
  6.5 254.0 %reduce-scatter.2.cloned.1.call-start = ((), (), s32[]{:S(2)}) async-start(), calls=%async_computation.1 | async-start | bytes 14745600 | tf_op jit(solution)/shard_map/reduce_scatter | solution.py:256
  6.6 117.9 %copy-start = (s32[1024]{0:T(1024)S(1)}, s32[1024]{0:T(1024)}, u32[]{:S(2)}) copy-start(s32[1024]{0:T(1024)} %param.7) | copy-start | bytes 12292
  6.6 117.9 %copy-start.1 = (s32[1024]{0:T(1024)S(1)}, s32[1024]{0:T(1024)}, u32[]{:S(2)}) copy-start(s32[1024]{0:T(1024)} %param.6) | copy-start | bytes 12292
Sparse Core Ops, SparseCore 0:
  178.8 81.6 reduce-scatter.1

commit v13 on v10

--- a/solution.py
+++ b/solution.py
@@ -57,6 +57,85 @@
         compiler_params=pltpu.CompilerParams(dimension_semantics=("arbitrary",)),
         cost_estimate=pl.CostEstimate(flops=total * width, transcendentals=0, bytes_accessed=3 * total * width * 4),
     )(own_rows, partner_rows, ladder)
+
+
+def _pair_diff_kernel(a_idx, b_idx, ia_idx, ib_idx, all_ref, out_ref, a_buf, b_buf, o_buf, in_sem, out_sem):
+    rows = a_buf.shape[1]
+    step = pl.program_id(0)
+    steps = pl.num_programs(0)
+
+    def issue(at, slot):
+        base = at * rows
+
+        def body(r, carry):
+            pltpu.make_async_copy(all_ref.at[pl.ds(a_idx[base + r], 1)], a_buf.at[slot, pl.ds(r, 1)], in_sem.at[0, slot]).start()
+            pltpu.make_async_copy(all_ref.at[pl.ds(b_idx[base + r], 1)], b_buf.at[slot, pl.ds(r, 1)], in_sem.at[1, slot]).start()
+            return carry
+
+        lax.fori_loop(0, rows, body, 0)
+
+    def drain(slot):
+        pltpu.make_async_copy(o_buf.at[slot], out_ref.at[pl.ds(0, 2 * rows)], out_sem.at[slot]).wait()
+
+    @pl.when(step == 0)
+    def _():
+        issue(0, 0)
+
+    @pl.when(step + 1 < steps)
+    def _():
+        issue(step + 1, (step + 1) % 2)
+
+    slot = step % 2
+    pltpu.make_async_copy(all_ref.at[pl.ds(0, rows)], a_buf.at[slot], in_sem.at[0, slot]).wait()
+    pltpu.make_async_copy(all_ref.at[pl.ds(0, rows)], b_buf.at[slot], in_sem.at[1, slot]).wait()
+
+    @pl.when(step >= 2)
+    def _():
+        drain(slot)
+
+    d = a_buf[slot] - b_buf[slot]
+    o_buf[slot, pl.ds(0, rows)] = d
+    o_buf[slot, pl.ds(rows, rows)] = -d
+    base = step * rows
+
+    def put(r, carry):
+        pltpu.make_async_copy(o_buf.at[slot, pl.ds(r, 1)], out_ref.at[pl.ds(ia_idx[base + r], 1)], out_sem.at[slot]).start()
+        pltpu.make_async_copy(o_buf.at[slot, pl.ds(rows + r, 1)], out_ref.at[pl.ds(ib_idx[base + r], 1)], out_sem.at[slot]).start()
+        return carry
+
+    lax.fori_loop(0, rows, put, 0)
+
+    @pl.when(step == steps - 1)
+    def _():
+        drain(slot)
+
+        @pl.when(steps >= 2)
+        def _():
+            drain(1 - slot)
+
+
+def pair_differences(ladder, a_rows, b_rows, a_out, b_out, rows=64):
+    total, width = ladder.shape
+    pairs = a_rows.shape[0]
+    return pl.pallas_call(
+        _pair_diff_kernel,
+        grid_spec=pltpu.PrefetchScalarGridSpec(
+            num_scalar_prefetch=4,
+            grid=(pairs // rows,),
+            in_specs=[pl.BlockSpec(memory_space=pl.ANY)],
+            out_specs=pl.BlockSpec(memory_space=pl.ANY),
+            scratch_shapes=[
+                pltpu.VMEM((2, rows, width), ladder.dtype),
+                pltpu.VMEM((2, rows, width), ladder.dtype),
+                pltpu.VMEM((2, 2 * rows, width), ladder.dtype),
+                pltpu.SemaphoreType.DMA((2, 2)),
+                pltpu.SemaphoreType.DMA((2,)),
+            ],
+        ),
+        out_shape=jax.ShapeDtypeStruct(ladder.shape, ladder.dtype),
+        compiler_params=pltpu.CompilerParams(dimension_semantics=("arbitrary",)),
+        cost_estimate=pl.CostEstimate(flops=total * width, transcendentals=0, bytes_accessed=2 * total * width * 4),
+    )(a_rows, b_rows, a_out, b_out, ladder)
 
 
 def _exchange_kernel(src_ref, out_ref, send_sem, recv_sem, local_sem):
@@ -183,16 +262,25 @@
     pos_of_stored = s_col * (n_row * local_rows) + s_row * local_rows + s_off
     inv = jnp.zeros((total,), jnp.int32).at[layout].set(s)
 
-    i = jnp.arange(total, dtype=jnp.int32)
-    g = i // block
-    xh = g % n_xh
-    core = (g // n_xh) % n_core
-    z = g // (n_xh * n_core)
-    p_of_i = ((z * n_xh + xh) * n_core + core) * block + (i % block)
-    q = partner[p_of_i]
+    def row_of(p):
+        g = p // block
+        core = g % n_core
+        xh = (g // n_core) % n_xh
+        z = g // (n_core * n_xh)
+        return ((z * n_core + core) * n_xh + xh) * block + (p % block)
+
+    p_all = jnp.arange(total, dtype=jnp.int32)
+    first = partner > p_all
+    rank = jnp.cumsum(first.astype(jnp.int32)) - 1
+    k = jnp.arange(total // 2, dtype=jnp.int32)
+    hits = first[None, :] & (rank[None, :] == k[:, None])
+    rep = jnp.sum(jnp.where(hits, p_all[None, :], 0), axis=1)
+    other = partner[rep]
 
     ladder = jnp.dot(gathered, integrals, preferred_element_type=jnp.float32)
-    difference = antisymmetrize(ladder, pos_of_stored[inv[p_of_i]], pos_of_stored[inv[q]])
+    difference = pair_differences(
+        ladder, pos_of_stored[inv[rep]], pos_of_stored[inv[other]], row_of(rep), row_of(other)
+    )
     part = lax.psum_scatter(difference, ("z", "core"), scatter_dimension=0, tiled=True)
     return sum_over_pair(part.reshape(n_xh, block, part.shape[1]))
 

time: 254 us -> 253 us (level)
  local copies, waits for them, and re-layouts: 37.3 us -> 21.1 us
  waiting for transfers between devices: 114 us -> 128 us
    gather x5, local copies, waits for them, and re-layouts: 31.2 us -> 14.8 us  [the longest x1 3.44 us: per_device(): pos_of_stored[inv[other]]]
    all_gather x1, waiting for transfers between devices: 39.5 us -> 53.7 us  [per_device(): gathered = lax.all_gather(regrouped, COL_AXES, axis=0, tiled=True)]
  transfers between devices with their start and end apart: 2 -> 2, of which waited for: 2 -> 2; matrix products, arithmetic and copies ran while one was open for 14% -> 9% of each run, Pallas kernels for 0% -> 0%
where the time goes in v13:
time: 253 us
  waiting for transfers between devices  128 us (51%)
  Pallas kernels  56.8 us (22%)
  matrix products  30.5 us (12%)
  local copies, waits for them, and re-layouts  21.1 us (8%)
  between operations  13.5 us (5%)
  other arithmetic  2.94 us (1%)
    reduce_scatter x1, waiting for transfers between devices, per_device(): lax.psum_scatter(difference, ('z', 'core'), scatter_dimension=0, tiled=True)  74 us
    all_gather x1, waiting for transfers between devices, per_device(): gathered = lax.all_gather(regrouped, COL_AXES, axis=0, tiled=True)  53.7 us
    dot_general x1, matrix products, per_device(): ladder = jnp.dot(gathered, integrals, preferred_element_type=jnp.float32)  30.5 us
    pallas_call x1, Pallas kernels, sum_over_pair(): pl.pallas_call(_pair_sum_kernel, out_shape=jax.ShapeDtypeStruct((rows, wi...  21.8 us
    pallas_call x1, Pallas kernels, pair_differences(): pl.pallas_call(_pair_diff_kernel, grid_spec=pltpu.PrefetchScalarGridSpec(...  17.7 us
    pallas_call x1, Pallas kernels, exchange_over_row(): pl.pallas_call(_exchange_kernel, out_shape=jax.ShapeDtypeStruct(pieces.sh...  17.2 us
  transfers between devices with their start and end apart: 2, of which 2 were waited for; matrix products, arithmetic and copies ran while one was open for 9% of the time, Pallas kernels for 0%

profile of v13, /device:TPU:0, one launch (start us, length us, event | category | flops | bytes accessed | tf_op | source)
XLA Modules:
  0.0 252.7 jit_solution(14840295232849537443)
XLA Ops:
  6.5 0.0 all-gather.2.cloned.1.call-start
  6.5 17.2 %shard_map.46 = bf16[16,8,3200]{2,1,0:T(8,128)(2,1)} custom-call(bf16[16,8,3200]{2,1,0:T(8,128)(2,1)} %bitcast.22), custom_call_target="tpu_custom_call" | custom-call | tf_op jit(solution)/shard_map/pallas_call | solution.py:179
  23.8 0.0 all-gather.2.cloned.1.call-update
  23.8 0.0 reduce-scatter.2.cloned.1.call-start
  23.9 0.7 convert_bitcast_fusion
  24.6 0.3 reduce-window.9
  24.8 0.1 slice.7
  24.9 0.1 slice_reduce_fusion
  25.1 0.1 add_bitcast_fusion
  25.1 0.5 select_reduce_fusion
  25.7 3.4 %gather_fusion.2 = s32[512]{0:T(512)S(1)} fusion(s32[1024]{0:T(1024)} %param.7, s32[1024]{0:T(1024)S(1)} %pad_clamp_fusion.3), kind=kCustom, calls=%fused_computation.2 | custom fusion | bytes 6144 | tf_op jit(solution)/shard_map/gather | solution.py:278
  29.0 0.7 compare_select_fusion.4
  29.7 4.3 %scatter_custom_fusion = s32[1024]{0:T(1024)S(1)} fusion(s32[1024]{0:T(1024)S(1)} %compare_select_fusion.4, s32[1024]{0:T(1024)S(1)} %iota.18, s32[]{:T(128)} %constant.144.clone.1), kind=kCustom, calls=%fused_computation.98 | custom fusion | bytes 4100 | tf_op jit(solution)/shard_map/scatter | solution.py:263
  34.0 2.3 gather_fusion
  36.4 2.3 gather_fusion.3
  38.7 3.4 %gather_fusion.4 = s32[512]{0:T(512)} fusion(s32[1024]{0:T(1024)S(1)} %get-tuple-element.7, s32[1024]{0:T(1024)S(1)} %pad_clamp_fusion), kind=kCustom, calls=%fused_computation.4 | custom fusion | bytes 6144 | tf_op jit(solution)/shard_map/gather | solution.py:282
  42.2 3.4 %gather_fusion.1 = s32[512]{0:T(512)} fusion(s32[1024]{0:T(1024)S(1)} %get-tuple-element.7, s32[1024]{0:T(1024)S(1)} %get-tuple-element.8), kind=kCustom, calls=%fused_computation.1 | custom fusion | bytes 6144 | tf_op jit(solution)/shard_map/gather | solution.py:282
  45.6 0.6 fusion.21
  46.2 53.7 %all-gather.2.cloned.1.call-done = bf16[1024,3200]{1,0:T(8,128)(2,1)} async-done(((bf16[128,3200]{1,0:T(8,128)(2,1)}), bf16[1024,3200]{1,0:T(8,128)(2,1)}) %all-gather.2.cloned.1.call-update) | async-done | bytes 6553616 | tf_op jit(solution)/shard_map/all_gather | solution.py:256
  99.9 30.5 %fusion.37.all_ref = f32[1024,3200]{1,0:T(8,128)} fusion(bf16[1024,3200]{1,0:T(8,128)(2,1)} %all-gather.2.cloned.1.call-done, bf16[3200,3200]{1,0:T(8,128)(2,1)} %param.5), kind=kOutput, calls=%fused_computation.104 | convolution fusion | flops 20971520000 | bytes 40140800 | tf_op jit(solution)/shard_map/dot_general | solution.py:280
  130.4 17.7 %shard_map.47 = f32[1024,3200]{1,0:T(8,128)} custom-call(s32[512]{0:T(512)} %gather_fusion.1, s32[512]{0:T(512)} %gather_fusion.4, s32[512]{0:T(512)} %get-tuple-element.9.ia_idx, s32[512]{0:T(512)} %get-tuple-element.10.ib_idx, f32[1024,3200]{1,0:T(8,128)} %fusion.37.all_ref), custom_call_target="tpu_custom_call" | custom-call | flops 3276800 | bytes 26214400 | tf_op jit(solution)/shard_map/pallas_call | solution.py:120
  148.1 0.0 reduce-scatter.2.cloned.1.call-update
  148.2 74.0 %reduce-scatter.2.cloned.1.call-done = f32[128,3200]{1,0:T(8,128)} async-done(((f32[1024,3200]{1,0:T(8,128)}), f32[128,3200]{1,0:T(8,128)}) %reduce-scatter.2.cloned.1.call-update) | async-done | bytes 1638416 | tf_op jit(solution)/shard_map/reduce_scatter | solution.py:284
  222.2 21.8 %shard_map.48 = bf16[64,3200]{1,0:T(8,128)(2,1)} custom-call(f32[2,64,3200]{2,1,0:T(8,128)} %bitcast.21), custom_call_target="tpu_custom_call" | custom-call | tf_op jit(solution)/shard_map/pallas_call | solution.py:228
  244.0 1.8 copy.6
  (10 shorter events, 0.1 us)
Async XLA Ops:
  6.5 93.4 %all-gather.2.cloned.1.call-start = ((), (), s32[]{:S(2)}) async-start(), calls=%async_computation.1 | async-start | bytes 7372800 | tf_op jit(solution)/shard_map/all_gather | solution.py:256
  23.8 198.4 %reduce-scatter.2.cloned.1.call-start = ((), (), s32[]{:S(2)}) async-start(), calls=%async_computation.2 | async-start | bytes 14745600 | tf_op jit(solution)/shard_map/reduce_scatter | solution.py:284
Sparse Core Ops, SparseCore 0:
  23.9 75.9 all-gather.1
  148.3 73.8 reduce-scatter.1

commit v14 on v13

--- a/solution.py
+++ b/solution.py
@@ -282,7 +282,12 @@
         ladder, pos_of_stored[inv[rep]], pos_of_stored[inv[other]], row_of(rep), row_of(other)
     )
     part = lax.psum_scatter(difference, ("z", "core"), scatter_dimension=0, tiled=True)
-    return sum_over_pair(part.reshape(n_xh, block, part.shape[1]))
+    halves = part.reshape(n_xh, block, part.shape[1])
+    xh_me = lax.axis_index("xh")
+    mine = lax.dynamic_index_in_dim(halves, xh_me, keepdims=False)
+    theirs = lax.dynamic_index_in_dim(halves, lax.rem(xh_me + 1, n_xh), keepdims=False)
+    received = lax.ppermute(theirs, "xh", perm=[(j, (j + 1) % n_xh) for j in range(n_xh)])
+    return (mine + received).astype(jnp.bfloat16)
 
 
 def solution(mesh):

time: 253 us -> 253 us (level)
  Pallas kernels: 56.8 us -> 35 us
  waiting for transfers between devices: 128 us -> 146 us
  starting transfers between devices: 0.04 us -> 3.09 us
    pallas_call x1 -> x0, Pallas kernels: 21.8 us -> none  [sum_over_pair(): pl.pallas_call(_pair_sum_kernel, out_shape=jax.ShapeDtypeStruct((rows, wi...]
    ppermute x0 -> x1, waiting for transfers between devices: none -> 17.8 us  [per_device(): lax.ppermute(theirs, 'xh', perm=[(j, (j + 1) % n_xh) for j in range(n_xh)])]
    ppermute x0 -> x1, starting transfers between devices: none -> 3.05 us  [per_device(): lax.ppermute(theirs, 'xh', perm=[(j, (j + 1) % n_xh) for j in range(n_xh)])]
  transfers between devices with their start and end apart: 2 -> 3, of which waited for: 2 -> 3; matrix products, arithmetic and copies ran while one was open for 9% -> 9% of each run, Pallas kernels for 0% -> 0%
where the time goes in v14:
time: 253 us
  waiting for transfers between devices  146 us (58%)
  Pallas kernels  35 us (14%)
  matrix products  30.5 us (12%)
  local copies, waits for them, and re-layouts  20.5 us (8%)
  between operations  13.5 us (5%)
  other arithmetic  4.98 us (2%)
  starting transfers between devices  3.09 us (1%)
    reduce_scatter x1, waiting for transfers between devices, per_device(): lax.psum_scatter(difference, ('z', 'core'), scatter_dimension=0, tiled=True)  74 us
    all_gather x1, waiting for transfers between devices, per_device(): gathered = lax.all_gather(regrouped, COL_AXES, axis=0, tiled=True)  53.7 us
    dot_general x1, matrix products, per_device(): ladder = jnp.dot(gathered, integrals, preferred_element_type=jnp.float32)  30.5 us
    ppermute x1, waiting for transfers between devices, per_device(): lax.ppermute(theirs, 'xh', perm=[(j, (j + 1) % n_xh) for j in range(n_xh)])  17.8 us
    pallas_call x1, Pallas kernels, pair_differences(): pl.pallas_call(_pair_diff_kernel, grid_spec=pltpu.PrefetchScalarGridSpec(...  17.7 us
    pallas_call x1, Pallas kernels, exchange_over_row(): pl.pallas_call(_exchange_kernel, out_shape=jax.ShapeDtypeStruct(pieces.sh...  17.2 us
  transfers between devices with their start and end apart: 3, of which 3 were waited for; matrix products, arithmetic and copies ran while one was open for 9% of the time, Pallas kernels for 0%

profile of v14, /device:TPU:0, one launch (start us, length us, event | category | flops | bytes accessed | tf_op | source)
XLA Modules:
  0.0 253.1 jit_solution(8125778629739222397)
XLA Ops:
  6.5 0.0 all-gather.2.cloned.1.call-start
  6.5 17.2 %shard_map.46 = bf16[16,8,3200]{2,1,0:T(8,128)(2,1)} custom-call(bf16[16,8,3200]{2,1,0:T(8,128)(2,1)} %bitcast.28), custom_call_target="tpu_custom_call" | custom-call | tf_op jit(solution)/shard_map/pallas_call | solution.py:179
  23.8 0.0 all-gather.2.cloned.1.call-update
  23.8 0.0 reduce-scatter.2.cloned.1.call-start
  23.9 0.7 convert_bitcast_fusion
  24.6 0.3 reduce-window.9
  24.8 0.1 slice.7
  24.9 0.1 slice_reduce_fusion
  25.1 0.1 add_bitcast_fusion
  25.1 0.5 select_reduce_fusion
  25.7 3.4 %gather_fusion.2 = s32[512]{0:T(512)S(1)} fusion(s32[1024]{0:T(1024)} %param.7, s32[1024]{0:T(1024)S(1)} %pad_clamp_fusion.3), kind=kCustom, calls=%fused_computation.2 | custom fusion | bytes 6144 | tf_op jit(solution)/shard_map/gather | solution.py:278
  29.0 0.7 compare_select_fusion.4
  29.7 4.3 %scatter_custom_fusion = s32[1024]{0:T(1024)S(1)} fusion(s32[1024]{0:T(1024)S(1)} %compare_select_fusion.4, s32[1024]{0:T(1024)S(1)} %iota.18, s32[]{:T(128)} %constant.157.clone.1), kind=kCustom, calls=%fused_computation.101 | custom fusion | bytes 4100 | tf_op jit(solution)/shard_map/scatter | solution.py:263
  34.0 2.3 gather_fusion
  36.4 2.3 gather_fusion.3
  38.7 3.4 %gather_fusion.1 = s32[512]{0:T(512)} fusion(s32[1024]{0:T(1024)S(1)} %get-tuple-element.7, s32[1024]{0:T(1024)S(1)} %get-tuple-element.8), kind=kCustom, calls=%fused_computation.1 | custom fusion | bytes 6144 | tf_op jit(solution)/shard_map/gather | solution.py:282
  42.1 3.4 %gather_fusion.4 = s32[512]{0:T(512)} fusion(s32[1024]{0:T(1024)S(1)} %get-tuple-element.7, s32[1024]{0:T(1024)S(1)} %pad_clamp_fusion), kind=kCustom, calls=%fused_computation.4 | custom fusion | bytes 6144 | tf_op jit(solution)/shard_map/gather | solution.py:282
  45.6 0.6 fusion.22
  46.2 53.7 %all-gather.2.cloned.1.call-done = bf16[1024,3200]{1,0:T(8,128)(2,1)} async-done(((bf16[128,3200]{1,0:T(8,128)(2,1)}), bf16[1024,3200]{1,0:T(8,128)(2,1)}) %all-gather.2.cloned.1.call-update) | async-done | bytes 6553616 | tf_op jit(solution)/shard_map/all_gather | solution.py:256
  99.9 30.5 %fusion.38.all_ref = f32[1024,3200]{1,0:T(8,128)} fusion(bf16[1024,3200]{1,0:T(8,128)(2,1)} %all-gather.2.cloned.1.call-done, bf16[3200,3200]{1,0:T(8,128)(2,1)} %param.5), kind=kOutput, calls=%fused_computation.107 | convolution fusion | flops 20971520000 | bytes 40140800 | tf_op jit(solution)/shard_map/dot_general | solution.py:280
  130.4 17.7 %shard_map.47 = f32[1024,3200]{1,0:T(8,128)} custom-call(s32[512]{0:T(512)} %gather_fusion.1, s32[512]{0:T(512)} %gather_fusion.4, s32[512]{0:T(512)} %get-tuple-element.9.ia_idx, s32[512]{0:T(512)} %get-tuple-element.10.ib_idx, f32[1024,3200]{1,0:T(8,128)} %fusion.38.all_ref), custom_call_target="tpu_custom_call" | custom-call | flops 3276800 | bytes 26214400 | tf_op jit(solution)/shard_map/pallas_call | solution.py:120
  148.1 0.0 reduce-scatter.2.cloned.1.call-update
  148.2 74.0 %reduce-scatter.2.cloned.1.call-done = f32[128,3200]{1,0:T(8,128)} async-done(((f32[1024,3200]{1,0:T(8,128)}), f32[128,3200]{1,0:T(8,128)}) %reduce-scatter.2.cloned.1.call-update) | async-done | bytes 1638416 | tf_op jit(solution)/shard_map/reduce_scatter | solution.py:284
  222.2 1.2 dynamic-slice_bitcast_fusion
  223.4 3.1 %collective-permute-start = (f32[64,3200]{1,0:T(8,128)S(1)}, f32[64,3200]{1,0:T(8,128)S(1)}, u32[]{:S(2)}, u32[]{:S(2)}) collective-permute-start(f32[64,3200]{1,0:T(8,128)S(1)} %dynamic-slice_bitcast_fusion), channel_id=1, source_target_pairs={{0,16},{16,0},{1,17},{17,1},{2,18},{18,2},{3,19},{19,3},{4,20},{20... | collective-permute-start | bytes 2457608 | tf_op jit(solution)/shard_map/ppermute | solution.py:289
  226.4 17.8 %collective-permute-done = f32[64,3200]{1,0:T(8,128)S(1)} collective-permute-done((f32[64,3200]{1,0:T(8,128)S(1)}, f32[64,3200]{1,0:T(8,128)S(1)}, u32[]{:S(2)}, u32[]{:S(2)}) %collective-permute-start) | collective-permute-done | bytes 819232 | tf_op jit(solution)/shard_map/ppermute | solution.py:289
  244.2 2.0 fusion.1
  (10 shorter events, 0.1 us)
Async XLA Ops:
  6.5 93.4 %all-gather.2.cloned.1.call-start = ((), (), s32[]{:S(2)}) async-start(), calls=%async_computation.1 | async-start | bytes 7372800 | tf_op jit(solution)/shard_map/all_gather | solution.py:256
  23.8 198.4 %reduce-scatter.2.cloned.1.call-start = ((), (), s32[]{:S(2)}) async-start(), calls=%async_computation.2 | async-start | bytes 14745600 | tf_op jit(solution)/shard_map/reduce_scatter | solution.py:284
  223.4 20.8 %collective-permute-start = (f32[64,3200]{1,0:T(8,128)S(1)}, f32[64,3200]{1,0:T(8,128)S(1)}, u32[]{:S(2)}, u32[]{:S(2)}) collective-permute-start(f32[64,3200]{1,0:T(8,128)S(1)} %dynamic-slice_bitcast_fusion), channel_id=1, source_target_pairs={{0,16},{16,0},{1,17},{17,1},{2,18},{18,2},{3,19},{19,3},{4,20},{20... | collective-permute-start | bytes 2457608 | tf_op jit(solution)/shard_map/ppermute | solution.py:289
Sparse Core Ops, SparseCore 0:
  23.9 75.9 all-gather.1
  148.3 73.8 reduce-scatter.1

commit v15 on v13

--- a/solution.py
+++ b/solution.py
@@ -114,7 +114,7 @@
             drain(1 - slot)
 
 
-def pair_differences(ladder, a_rows, b_rows, a_out, b_out, rows=64):
+def pair_differences(ladder, a_rows, b_rows, a_out, b_out, rows=128):
     total, width = ladder.shape
     pairs = a_rows.shape[0]
     return pl.pallas_call(

time: 253 us -> 253 us (level)
  no operation moved by 1% of the time
where the time goes in v15:
time: 253 us
  waiting for transfers between devices  128 us (51%)
  Pallas kernels  56.9 us (22%)
  matrix products  30.5 us (12%)
  local copies, waits for them, and re-layouts  21.1 us (8%)
  between operations  13.5 us (5%)
  other arithmetic  2.94 us (1%)
    reduce_scatter x1, waiting for transfers between devices, per_device(): lax.psum_scatter(difference, ('z', 'core'), scatter_dimension=0, tiled=True)  74 us
    all_gather x1, waiting for transfers between devices, per_device(): gathered = lax.all_gather(regrouped, COL_AXES, axis=0, tiled=True)  53.7 us
    dot_general x1, matrix products, per_device(): ladder = jnp.dot(gathered, integrals, preferred_element_type=jnp.float32)  30.5 us
    pallas_call x1, Pallas kernels, sum_over_pair(): pl.pallas_call(_pair_sum_kernel, out_shape=jax.ShapeDtypeStruct((rows, wi...  21.8 us
    pallas_call x1, Pallas kernels, pair_differences(): pl.pallas_call(_pair_diff_kernel, grid_spec=pltpu.PrefetchScalarGridSpec(...  17.8 us
    pallas_call x1, Pallas kernels, exchange_over_row(): pl.pallas_call(_exchange_kernel, out_shape=jax.ShapeDtypeStruct(pieces.sh...  17.2 us
  transfers between devices with their start and end apart: 2, of which 2 were waited for; matrix products, arithmetic and copies ran while one was open for 9% of the time, Pallas kernels for 0%

profile of v15, /device:TPU:0, one launch (start us, length us, event | category | flops | bytes accessed | tf_op | source)
XLA Modules:
  0.0 252.7 jit_solution(95805198566150229)
XLA Ops:
  6.5 0.0 all-gather.2.cloned.1.call-start
  6.5 17.2 %shard_map.46 = bf16[16,8,3200]{2,1,0:T(8,128)(2,1)} custom-call(bf16[16,8,3200]{2,1,0:T(8,128)(2,1)} %bitcast.22), custom_call_target="tpu_custom_call" | custom-call | tf_op jit(solution)/shard_map/pallas_call | solution.py:179
  23.8 0.0 all-gather.2.cloned.1.call-update
  23.8 0.0 reduce-scatter.2.cloned.1.call-start
  23.9 0.7 convert_bitcast_fusion
  24.6 0.3 reduce-window.9
  24.8 0.1 slice.7
  24.9 0.1 slice_reduce_fusion
  25.1 0.1 add_bitcast_fusion
  25.1 0.5 select_reduce_fusion
  25.7 3.4 %gather_fusion.2 = s32[512]{0:T(512)S(1)} fusion(s32[1024]{0:T(1024)} %param.7, s32[1024]{0:T(1024)S(1)} %pad_clamp_fusion.3), kind=kCustom, calls=%fused_computation.2 | custom fusion | bytes 6144 | tf_op jit(solution)/shard_map/gather | solution.py:278
  29.0 0.7 compare_select_fusion.4
  29.7 4.3 %scatter_custom_fusion = s32[1024]{0:T(1024)S(1)} fusion(s32[1024]{0:T(1024)S(1)} %compare_select_fusion.4, s32[1024]{0:T(1024)S(1)} %iota.18, s32[]{:T(128)} %constant.144.clone.1), kind=kCustom, calls=%fused_computation.98 | custom fusion | bytes 4100 | tf_op jit(solution)/shard_map/scatter | solution.py:263
  34.0 2.3 gather_fusion
  36.4 2.3 gather_fusion.3
  38.7 3.4 %gather_fusion.4 = s32[512]{0:T(512)} fusion(s32[1024]{0:T(1024)S(1)} %get-tuple-element.7, s32[1024]{0:T(1024)S(1)} %pad_clamp_fusion), kind=kCustom, calls=%fused_computation.4 | custom fusion | bytes 6144 | tf_op jit(solution)/shard_map/gather | solution.py:282
  42.2 3.4 %gather_fusion.1 = s32[512]{0:T(512)} fusion(s32[1024]{0:T(1024)S(1)} %get-tuple-element.7, s32[1024]{0:T(1024)S(1)} %get-tuple-element.8), kind=kCustom, calls=%fused_computation.1 | custom fusion | bytes 6144 | tf_op jit(solution)/shard_map/gather | solution.py:282
  45.6 0.6 fusion.21
  46.2 53.7 %all-gather.2.cloned.1.call-done = bf16[1024,3200]{1,0:T(8,128)(2,1)} async-done(((bf16[128,3200]{1,0:T(8,128)(2,1)}), bf16[1024,3200]{1,0:T(8,128)(2,1)}) %all-gather.2.cloned.1.call-update) | async-done | bytes 6553616 | tf_op jit(solution)/shard_map/all_gather | solution.py:256
  99.9 30.5 %fusion.37.all_ref = f32[1024,3200]{1,0:T(8,128)} fusion(bf16[1024,3200]{1,0:T(8,128)(2,1)} %all-gather.2.cloned.1.call-done, bf16[3200,3200]{1,0:T(8,128)(2,1)} %param.5), kind=kOutput, calls=%fused_computation.104 | convolution fusion | flops 20971520000 | bytes 40140800 | tf_op jit(solution)/shard_map/dot_general | solution.py:280
  130.4 17.8 %shard_map.47 = f32[1024,3200]{1,0:T(8,128)} custom-call(s32[512]{0:T(512)} %gather_fusion.1, s32[512]{0:T(512)} %gather_fusion.4, s32[512]{0:T(512)} %get-tuple-element.9.ia_idx, s32[512]{0:T(512)} %get-tuple-element.10.ib_idx, f32[1024,3200]{1,0:T(8,128)} %fusion.37.all_ref), custom_call_target="tpu_custom_call" | custom-call | flops 3276800 | bytes 26214400 | tf_op jit(solution)/shard_map/pallas_call | solution.py:120
  148.2 0.0 reduce-scatter.2.cloned.1.call-update
  148.2 74.0 %reduce-scatter.2.cloned.1.call-done = f32[128,3200]{1,0:T(8,128)} async-done(((f32[1024,3200]{1,0:T(8,128)}), f32[128,3200]{1,0:T(8,128)}) %reduce-scatter.2.cloned.1.call-update) | async-done | bytes 1638416 | tf_op jit(solution)/shard_map/reduce_scatter | solution.py:284
  222.2 21.8 %shard_map.48 = bf16[64,3200]{1,0:T(8,128)(2,1)} custom-call(f32[2,64,3200]{2,1,0:T(8,128)} %bitcast.21), custom_call_target="tpu_custom_call" | custom-call | tf_op jit(solution)/shard_map/pallas_call | solution.py:228
  244.1 1.8 copy.6
  (10 shorter events, 0.1 us)
Async XLA Ops:
  6.5 93.4 %all-gather.2.cloned.1.call-start = ((), (), s32[]{:S(2)}) async-start(), calls=%async_computation.1 | async-start | bytes 7372800 | tf_op jit(solution)/shard_map/all_gather | solution.py:256
  23.8 198.4 %reduce-scatter.2.cloned.1.call-start = ((), (), s32[]{:S(2)}) async-start(), calls=%async_computation.2 | async-start | bytes 14745600 | tf_op jit(solution)/shard_map/reduce_scatter | solution.py:284
Sparse Core Ops, SparseCore 0:
  23.9 75.9 all-gather.1
  148.3 73.8 reduce-scatter.1

commit v16 on v13

--- a/solution.py
+++ b/solution.py
@@ -190,7 +190,7 @@
     )(pieces)
 
 
-def _pair_sum_kernel(part_ref, out_ref, own_buf, recv_buf, send_sem, recv_sem, local_sem):
+def _pair_sum_kernel(part_ref, out_ref, own_buf, recv_buf, res_buf, send_sem, recv_sem, local_sem):
     n_xh = lax.axis_size("xh")
     z, xh, core, xl, y = (lax.axis_index(a) for a in ROW_AXES + COL_AXES)
     other = lax.rem(xh + 1, n_xh)
@@ -220,7 +220,10 @@
     for copy in sends:
         copy.wait_send()
     pltpu.make_async_copy(part_ref.at[xh], recv_buf, recv_sem.at[0]).wait()
-    out_ref[...] = (own_buf[...] + recv_buf[...]).astype(out_ref.dtype)
+    res_buf[...] = (own_buf[...] + recv_buf[...]).astype(res_buf.dtype)
+    result = pltpu.make_async_copy(res_buf, out_ref, local_sem.at[0])
+    result.start()
+    result.wait()
 
 
 def sum_over_pair(part, pieces=4):
@@ -229,10 +232,11 @@
         _pair_sum_kernel,
         out_shape=jax.ShapeDtypeStruct((rows, width), jnp.bfloat16),
         in_specs=[pl.BlockSpec(memory_space=pl.ANY)],
-        out_specs=pl.BlockSpec(memory_space=pltpu.VMEM),
+        out_specs=pl.BlockSpec(memory_space=pl.ANY),
         scratch_shapes=[
             pltpu.VMEM((rows, width), part.dtype),
             pltpu.VMEM((rows, width), part.dtype),
+            pltpu.VMEM((rows, width), jnp.bfloat16),
             pltpu.SemaphoreType.DMA((pieces,)),
             pltpu.SemaphoreType.DMA((1,)),
             pltpu.SemaphoreType.DMA((1,)),

time: 253 us -> 253 us (level)
  no operation moved by 1% of the time
where the time goes in v16:
time: 253 us
  waiting for transfers between devices  128 us (51%)
  Pallas kernels  56.8 us (22%)
  matrix products  30.5 us (12%)
  local copies, waits for them, and re-layouts  21.1 us (8%)
  between operations  13.5 us (5%)
  other arithmetic  2.94 us (1%)
    reduce_scatter x1, waiting for transfers between devices, per_device(): lax.psum_scatter(difference, ('z', 'core'), scatter_dimension=0, tiled=True)  74 us
    all_gather x1, waiting for transfers between devices, per_device(): gathered = lax.all_gather(regrouped, COL_AXES, axis=0, tiled=True)  53.7 us
    dot_general x1, matrix products, per_device(): ladder = jnp.dot(gathered, integrals, preferred_element_type=jnp.float32)  30.5 us
    pallas_call x1, Pallas kernels, sum_over_pair(): pl.pallas_call(_pair_sum_kernel, out_shape=jax.ShapeDtypeStruct((rows, wi...  21.8 us
    pallas_call x1, Pallas kernels, pair_differences(): pl.pallas_call(_pair_diff_kernel, grid_spec=pltpu.PrefetchScalarGridSpec(...  17.7 us
    pallas_call x1, Pallas kernels, exchange_over_row(): pl.pallas_call(_exchange_kernel, out_shape=jax.ShapeDtypeStruct(pieces.sh...  17.2 us
  transfers between devices with their start and end apart: 2, of which 2 were waited for; matrix products, arithmetic and copies ran while one was open for 9% of the time, Pallas kernels for 0%

profile of v16, /device:TPU:0, one launch (start us, length us, event | category | flops | bytes accessed | tf_op | source)
XLA Modules:
  0.0 252.7 jit_solution(16089188484391322458)
XLA Ops:
  6.5 0.0 all-gather.2.cloned.1.call-start
  6.5 17.2 %shard_map.46 = bf16[16,8,3200]{2,1,0:T(8,128)(2,1)} custom-call(bf16[16,8,3200]{2,1,0:T(8,128)(2,1)} %bitcast.22), custom_call_target="tpu_custom_call" | custom-call | tf_op jit(solution)/shard_map/pallas_call | solution.py:179
  23.8 0.0 all-gather.2.cloned.1.call-update
  23.8 0.0 reduce-scatter.2.cloned.1.call-start
  23.9 0.7 convert_bitcast_fusion
  24.6 0.3 reduce-window.9
  24.8 0.1 slice.7
  24.9 0.1 slice_reduce_fusion
  25.1 0.1 add_bitcast_fusion
  25.1 0.5 select_reduce_fusion
  25.7 3.4 %gather_fusion.2 = s32[512]{0:T(512)S(1)} fusion(s32[1024]{0:T(1024)} %param.7, s32[1024]{0:T(1024)S(1)} %pad_clamp_fusion.3), kind=kCustom, calls=%fused_computation.2 | custom fusion | bytes 6144 | tf_op jit(solution)/shard_map/gather | solution.py:282
  29.0 0.7 compare_select_fusion.4
  29.7 4.3 %scatter_custom_fusion = s32[1024]{0:T(1024)S(1)} fusion(s32[1024]{0:T(1024)S(1)} %compare_select_fusion.4, s32[1024]{0:T(1024)S(1)} %iota.18, s32[]{:T(128)} %constant.144.clone.1), kind=kCustom, calls=%fused_computation.98 | custom fusion | bytes 4100 | tf_op jit(solution)/shard_map/scatter | solution.py:267
  34.0 2.3 gather_fusion
  36.4 2.3 gather_fusion.3
  38.7 3.4 %gather_fusion.4 = s32[512]{0:T(512)} fusion(s32[1024]{0:T(1024)S(1)} %get-tuple-element.7, s32[1024]{0:T(1024)S(1)} %pad_clamp_fusion), kind=kCustom, calls=%fused_computation.4 | custom fusion | bytes 6144 | tf_op jit(solution)/shard_map/gather | solution.py:286
  42.2 3.4 %gather_fusion.1 = s32[512]{0:T(512)} fusion(s32[1024]{0:T(1024)S(1)} %get-tuple-element.7, s32[1024]{0:T(1024)S(1)} %get-tuple-element.8), kind=kCustom, calls=%fused_computation.1 | custom fusion | bytes 6144 | tf_op jit(solution)/shard_map/gather | solution.py:286
  45.6 0.6 fusion.21
  46.2 53.7 %all-gather.2.cloned.1.call-done = bf16[1024,3200]{1,0:T(8,128)(2,1)} async-done(((bf16[128,3200]{1,0:T(8,128)(2,1)}), bf16[1024,3200]{1,0:T(8,128)(2,1)}) %all-gather.2.cloned.1.call-update) | async-done | bytes 6553616 | tf_op jit(solution)/shard_map/all_gather | solution.py:260
  99.9 30.5 %fusion.37.all_ref = f32[1024,3200]{1,0:T(8,128)} fusion(bf16[1024,3200]{1,0:T(8,128)(2,1)} %all-gather.2.cloned.1.call-done, bf16[3200,3200]{1,0:T(8,128)(2,1)} %param.5), kind=kOutput, calls=%fused_computation.104 | convolution fusion | flops 20971520000 | bytes 40140800 | tf_op jit(solution)/shard_map/dot_general | solution.py:284
  130.4 17.7 %shard_map.47 = f32[1024,3200]{1,0:T(8,128)} custom-call(s32[512]{0:T(512)} %gather_fusion.1, s32[512]{0:T(512)} %gather_fusion.4, s32[512]{0:T(512)} %get-tuple-element.9.ia_idx, s32[512]{0:T(512)} %get-tuple-element.10.ib_idx, f32[1024,3200]{1,0:T(8,128)} %fusion.37.all_ref), custom_call_target="tpu_custom_call" | custom-call | flops 3276800 | bytes 26214400 | tf_op jit(solution)/shard_map/pallas_call | solution.py:120
  148.1 0.0 reduce-scatter.2.cloned.1.call-update
  148.1 74.0 %reduce-scatter.2.cloned.1.call-done = f32[128,3200]{1,0:T(8,128)} async-done(((f32[1024,3200]{1,0:T(8,128)}), f32[128,3200]{1,0:T(8,128)}) %reduce-scatter.2.cloned.1.call-update) | async-done | bytes 1638416 | tf_op jit(solution)/shard_map/reduce_scatter | solution.py:288
  222.2 21.8 %shard_map.48 = bf16[64,3200]{1,0:T(8,128)(2,1)} custom-call(f32[2,64,3200]{2,1,0:T(8,128)} %bitcast.21), custom_call_target="tpu_custom_call" | custom-call | tf_op jit(solution)/shard_map/pallas_call | solution.py:231
  244.0 1.8 copy.6
  (10 shorter events, 0.1 us)
Async XLA Ops:
  6.5 93.4 %all-gather.2.cloned.1.call-start = ((), (), s32[]{:S(2)}) async-start(), calls=%async_computation.1 | async-start | bytes 7372800 | tf_op jit(solution)/shard_map/all_gather | solution.py:260
  23.8 198.4 %reduce-scatter.2.cloned.1.call-start = ((), (), s32[]{:S(2)}) async-start(), calls=%async_computation.2 | async-start | bytes 14745600 | tf_op jit(solution)/shard_map/reduce_scatter | solution.py:288
Sparse Core Ops, SparseCore 0:
  23.9 75.9 all-gather.1
  148.3 73.8 reduce-scatter.1

commit v17 on v13

--- a/solution.py
+++ b/solution.py
@@ -147,11 +147,6 @@
     def peer(k):
         t = lax.rem(me + k, n)
         return t, (t // (n_xh * n_core), lax.rem(t // n_core, n_xh), lax.rem(t, n_core), xl, y)
-
-    barrier = pltpu.get_barrier_semaphore()
-    for k in range(1, n):
-        pl.semaphore_signal(barrier, inc=1, device_id=peer(k)[1], device_id_type=pl.DeviceIdType.MESH)
-    pl.semaphore_wait(barrier, n - 1)
 
     local = pltpu.make_async_copy(src_ref.at[me], out_ref.at[me], local_sem.at[0])
     local.start()
@@ -186,7 +181,7 @@
             pltpu.SemaphoreType.DMA((1,)),
             pltpu.SemaphoreType.DMA((1,)),
         ],
-        compiler_params=pltpu.CompilerParams(collective_id=0, has_side_effects=True),
+        compiler_params=pltpu.CompilerParams(has_side_effects=True),
     )(pieces)
 
 

time: 253 us -> 258 us (1.020)
  Pallas kernels: 56.8 us -> 62.4 us
    pallas_call x1, Pallas kernels: 17.2 us -> 22.8 us  [exchange_over_row(): pl.pallas_call(_exchange_kernel, out_shape=jax.ShapeDtypeStruct(pieces.sh...]
where the time goes in v17:
time: 258 us; the launch traced here: 257 us
  waiting for transfers between devices  127 us (49%)
  Pallas kernels  62.4 us (24%)
  matrix products  30.5 us (12%)
  local copies, waits for them, and re-layouts  21.1 us (8%)
  between operations  13.5 us (5%)
  other arithmetic  2.94 us (1%)
    reduce_scatter x1, waiting for transfers between devices, per_device(): lax.psum_scatter(difference, ('z', 'core'), scatter_dimension=0, tiled=True)  74 us
    all_gather x1, waiting for transfers between devices, per_device(): gathered = lax.all_gather(regrouped, COL_AXES, axis=0, tiled=True)  52.8 us
    dot_general x1, matrix products, per_device(): ladder = jnp.dot(gathered, integrals, preferred_element_type=jnp.float32)  30.5 us
    pallas_call x1, Pallas kernels, exchange_over_row(): pl.pallas_call(_exchange_kernel, out_shape=jax.ShapeDtypeStruct(pieces.sh...  22.8 us
    pallas_call x1, Pallas kernels, sum_over_pair(): pl.pallas_call(_pair_sum_kernel, out_shape=jax.ShapeDtypeStruct((rows, wi...  21.8 us
    pallas_call x1, Pallas kernels, pair_differences(): pl.pallas_call(_pair_diff_kernel, grid_spec=pltpu.PrefetchScalarGridSpec(...  17.8 us
  transfers between devices with their start and end apart: 2, of which 2 were waited for; matrix products, arithmetic and copies ran while one was open for 9% of the time, Pallas kernels for 0%

profile of v17, /device:TPU:0, one launch (start us, length us, event | category | flops | bytes accessed | tf_op | source)
XLA Modules:
  0.0 257.3 jit_solution(1861106127712114858)
XLA Ops:
  6.5 0.0 all-gather.2.cloned.1.call-start
  6.5 22.8 %shard_map.46 = bf16[16,8,3200]{2,1,0:T(8,128)(2,1)} custom-call(bf16[16,8,3200]{2,1,0:T(8,128)(2,1)} %bitcast.22), custom_call_target="tpu_custom_call" | custom-call | tf_op jit(solution)/shard_map/pallas_call | solution.py:174
  29.3 0.0 all-gather.2.cloned.1.call-update
  29.3 0.0 reduce-scatter.2.cloned.1.call-start
  29.4 0.7 convert_bitcast_fusion
  30.1 0.3 reduce-window.9
  30.3 0.1 slice.7
  30.4 0.1 slice_reduce_fusion
  30.6 0.1 add_bitcast_fusion
  30.6 0.5 select_reduce_fusion
  31.2 3.4 %gather_fusion.2 = s32[512]{0:T(512)S(1)} fusion(s32[1024]{0:T(1024)} %param.7, s32[1024]{0:T(1024)S(1)} %pad_clamp_fusion.3), kind=kCustom, calls=%fused_computation.2 | custom fusion | bytes 6144 | tf_op jit(solution)/shard_map/gather | solution.py:273
  34.5 0.7 compare_select_fusion.4
  35.2 4.3 %scatter_custom_fusion = s32[1024]{0:T(1024)S(1)} fusion(s32[1024]{0:T(1024)S(1)} %compare_select_fusion.4, s32[1024]{0:T(1024)S(1)} %iota.18, s32[]{:T(128)} %constant.144.clone.1), kind=kCustom, calls=%fused_computation.98 | custom fusion | bytes 4100 | tf_op jit(solution)/shard_map/scatter | solution.py:258
  39.5 2.3 gather_fusion
  41.9 2.3 gather_fusion.3
  44.2 3.4 %gather_fusion.4 = s32[512]{0:T(512)} fusion(s32[1024]{0:T(1024)S(1)} %get-tuple-element.7, s32[1024]{0:T(1024)S(1)} %pad_clamp_fusion), kind=kCustom, calls=%fused_computation.4 | custom fusion | bytes 6144 | tf_op jit(solution)/shard_map/gather | solution.py:277
  47.7 3.4 %gather_fusion.1 = s32[512]{0:T(512)} fusion(s32[1024]{0:T(1024)S(1)} %get-tuple-element.7, s32[1024]{0:T(1024)S(1)} %get-tuple-element.8), kind=kCustom, calls=%fused_computation.1 | custom fusion | bytes 6144 | tf_op jit(solution)/shard_map/gather | solution.py:277
  51.1 0.6 fusion.21
  51.7 52.8 %all-gather.2.cloned.1.call-done = bf16[1024,3200]{1,0:T(8,128)(2,1)} async-done(((bf16[128,3200]{1,0:T(8,128)(2,1)}), bf16[1024,3200]{1,0:T(8,128)(2,1)}) %all-gather.2.cloned.1.call-update) | async-done | bytes 6553616 | tf_op jit(solution)/shard_map/all_gather | solution.py:251
  104.5 30.5 %fusion.37.all_ref = f32[1024,3200]{1,0:T(8,128)} fusion(bf16[1024,3200]{1,0:T(8,128)(2,1)} %all-gather.2.cloned.1.call-done, bf16[3200,3200]{1,0:T(8,128)(2,1)} %param.5), kind=kOutput, calls=%fused_computation.104 | convolution fusion | flops 20971520000 | bytes 40140800 | tf_op jit(solution)/shard_map/dot_general | solution.py:275
  135.0 17.8 %shard_map.47 = f32[1024,3200]{1,0:T(8,128)} custom-call(s32[512]{0:T(512)} %gather_fusion.1, s32[512]{0:T(512)} %gather_fusion.4, s32[512]{0:T(512)} %get-tuple-element.9.ia_idx, s32[512]{0:T(512)} %get-tuple-element.10.ib_idx, f32[1024,3200]{1,0:T(8,128)} %fusion.37.all_ref), custom_call_target="tpu_custom_call" | custom-call | flops 3276800 | bytes 26214400 | tf_op jit(solution)/shard_map/pallas_call | solution.py:120
  152.8 0.0 reduce-scatter.2.cloned.1.call-update
  152.8 74.0 %reduce-scatter.2.cloned.1.call-done = f32[128,3200]{1,0:T(8,128)} async-done(((f32[1024,3200]{1,0:T(8,128)}), f32[128,3200]{1,0:T(8,128)}) %reduce-scatter.2.cloned.1.call-update) | async-done | bytes 1638416 | tf_op jit(solution)/shard_map/reduce_scatter | solution.py:279
  226.9 21.8 %shard_map.48 = bf16[64,3200]{1,0:T(8,128)(2,1)} custom-call(f32[2,64,3200]{2,1,0:T(8,128)} %bitcast.21), custom_call_target="tpu_custom_call" | custom-call | tf_op jit(solution)/shard_map/pallas_call | solution.py:223
  248.7 1.8 copy.6
  (10 shorter events, 0.1 us)
Async XLA Ops:
  6.5 98.0 %all-gather.2.cloned.1.call-start = ((), (), s32[]{:S(2)}) async-start(), calls=%async_computation.1 | async-start | bytes 7372800 | tf_op jit(solution)/shard_map/all_gather | solution.py:251
  29.3 197.5 %reduce-scatter.2.cloned.1.call-start = ((), (), s32[]{:S(2)}) async-start(), calls=%async_computation.2 | async-start | bytes 14745600 | tf_op jit(solution)/shard_map/reduce_scatter | solution.py:279
Sparse Core Ops, SparseCore 0:
  29.4 75.0 all-gather.1
  152.9 73.8 reduce-scatter.1
